TPU v7x, 32 devices: a whole 2x2x4 slice. The times are simulated.
32 devices in a mesh: fsdp: 4 (over x, core), ctx: 8 (over z, y).
Axes of the slice: x: 2, y: 2, z: 4, core: 2. Of those that a mesh axis runs over, the one named last changes fastest.
Arguments:
- hidden: bfloat16 [4, 1024, 768], P('fsdp', 'ctx'), may hold values from -6 to 6
- encoded: bfloat16 [4, 256, 768], P('fsdp', 'ctx'), may hold values from -6 to 6
- cotangent: bfloat16 [4, 1024, 768], P('fsdp', 'ctx'), may hold values from -6 to 6
- dec_seg: int32 [4, 1024], P('fsdp', 'ctx'), may hold values from 0 to 15, as said below
- enc_seg: int32 [4, 256], P('fsdp', 'ctx'), may hold values from 0 to 15, as said below
- self_qkv: float32 [768, 2304], P('fsdp'), may hold values from -0.21875 to 0.21875
- self_out: float32 [768, 768], P('fsdp'), may hold values from -1.75 to 1.75
- cross_q: float32 [768, 768], P('fsdp'), may hold values from -0.21875 to 0.21875
- cross_kv: float32 [768, 1536], P('fsdp'), may hold values from -0.21875 to 0.21875
- cross_out: float32 [768, 768], P('fsdp'), may hold values from -0.875 to 0.875
- ffn_in: float32 [768, 3072], P('fsdp'), may hold values from -0.21875 to 0.21875
- ffn_out: float32 [3072, 768], P('fsdp'), may hold values from -0.109375 to 0.109375
- biases: float32 [10, 768], P(None, 'fsdp'), may hold values from -3 to 3
- gains: float32 [3, 768], P(None, 'fsdp'), may hold values from 0.25 to 1.75
- ffn_bias: float32 [3072], P('fsdp'), may hold values from -3 to 3
Outputs:
- output: bfloat16 [4, 1024, 768], P('fsdp', 'ctx')
- d_hidden: float32 [4, 1024, 768], P('fsdp', 'ctx')
- d_encoded: float32 [4, 256, 768], P('fsdp', 'ctx')
- d_self_qkv: float32 [768, 2304], P('fsdp')
- d_self_out: float32 [768, 768], P('fsdp')
- d_cross_q: float32 [768, 768], P('fsdp')
- d_cross_kv: float32 [768, 1536], P('fsdp')
- d_cross_out: float32 [768, 768], P('fsdp')
- d_ffn_in: float32 [768, 3072], P('fsdp')
- d_ffn_out: float32 [3072, 768], P('fsdp')
- d_biases: float32 [10, 768], P(None, 'fsdp')
- d_gains: float32 [3, 768], P(None, 'fsdp')
- d_ffn_bias: float32 [3072], P('fsdp')
Inputs may be any that keep to these rules, and one draw needn't show every extreme that they name: `dec_seg`: within a sequence the numbers never fall and each of 0 to 15 appears. `enc_seg`: within a sequence the numbers never fall and each of 0 to 15 appears, so every document of dec_seg has encoder rows.
All inputs are finite; a program needn't handle non-finite values.
Results may differ from a plain program's by a relative error of at most 0.025.
Values may be sent and summed in bfloat16 or wider, within the bound.
No kernel may reach another device: no remote copies, remote signals or barrier semaphores. Data moves between devices by JAX's collectives and lax.ppermute only.
A program may use at most 320 MiB of HBM per device.

v0:
```python
import jax
import jax.numpy as jnp
from jax import lax
from jax.sharding import PartitionSpec as P

H = 12
HD = 64


EPSILON = 1e-05
FLOOR_SCORE = -1e30


def from_behind(block, axis, distance):
    devices = range(lax.axis_size(axis))
    route = [((i - distance) % len(devices), i) for i in devices]
    return lax.ppermute(block, axis, route)


def layer_norm(values, gain, shift):
    center = values - jnp.mean(values, axis=-1, keepdims=True)
    spread = jnp.mean(center * center, axis=-1, keepdims=True)
    return center * lax.rsqrt(spread + EPSILON) * gain + shift


def exact_gelu(values):
    return jax.nn.gelu(values, approximate=False)


def matmul(left, right):
    return jnp.dot(left, right, preferred_element_type=jnp.float32)


def matmul_tn(left, right):
    return lax.dot_general(
        left, right, (((0,), (0,)), ((), ())), preferred_element_type=jnp.float32
    )


def matmul_nt(left, right):
    return lax.dot_general(
        left, right, (((1,), (1,)), ((), ())), preferred_element_type=jnp.float32
    )


def split_heads(values):
    return values.reshape(values.shape[0], H, HD)


def column_sum(values):
    return jnp.sum(values.astype(jnp.float32), axis=0)


def head_inner(grad_low, values):
    product = grad_low.astype(jnp.float32) * values
    return jnp.sum(product.reshape(values.shape[0], H, HD), axis=2).T


def empty_state(count):
    return (
        jnp.full((H, count), FLOOR_SCORE, jnp.float32),
        jnp.zeros((H, count), jnp.float32),
        jnp.zeros((H, count, HD), jnp.float32),
    )


def online_update(carry, scores, allowed, value_heads):
    running_max, running_sum, weighted = carry
    masked = jnp.where(allowed[None], scores, FLOOR_SCORE)
    new_max = jnp.maximum(running_max, jnp.max(masked, axis=2))
    factor = jnp.exp(running_max - new_max)
    weights = jnp.where(allowed[None], jnp.exp(masked - new_max[:, :, None]), 0.0)
    running_sum = running_sum * factor + jnp.sum(weights, axis=2)
    update = jnp.einsum(
        "hqk,khd->hqd",
        weights.astype(jnp.bfloat16),
        value_heads,
        preferred_element_type=jnp.float32,
    )
    return (new_max, running_sum, weighted * factor[:, :, None] + update)


def finish_state(carry):
    running_max, running_sum, weighted = carry
    result = weighted / running_sum[:, :, None]
    joined = jnp.transpose(result, (1, 0, 2)).reshape(result.shape[1], H * HD)
    return (joined, running_max + jnp.log(running_sum))


def block_grads(query_heads, grad_heads, log_total, inner, key_heads, value_heads, allowed):
    scores = jnp.einsum("qhd,khd->hqk", query_heads, key_heads, preferred_element_type=jnp.float32)
    probs = jnp.where(allowed[None], jnp.exp(scores - log_total[:, :, None]), 0.0)
    prob_grad = jnp.einsum(
        "qhd,khd->hqk", grad_heads, value_heads, preferred_element_type=jnp.float32
    )
    score_grad = (probs * (prob_grad - inner[:, :, None])).astype(jnp.bfloat16)
    query_grad = jnp.einsum(
        "hqk,khd->qhd", score_grad, key_heads, preferred_element_type=jnp.float32
    )
    key_grad = jnp.einsum(
        "hqk,qhd->khd", score_grad, query_heads, preferred_element_type=jnp.float32
    )
    value_grad = jnp.einsum(
        "hqk,qhd->khd", probs.astype(jnp.bfloat16), grad_heads, preferred_element_type=jnp.float32
    )
    count = key_heads.shape[0]
    pair_grad = jnp.concatenate(
        [key_grad.reshape(count, H * HD), value_grad.reshape(count, H * HD)], axis=1
    )
    return (query_grad.reshape(query_heads.shape[0], H * HD), pair_grad)


def body(
    hidden,
    encoded,
    cotangent,
    dec_seg,
    enc_seg,
    self_qkv,
    self_out,
    cross_q,
    cross_kv,
    cross_out,
    ffn_in,
    ffn_out,
    biases,
    gains,
    ffn_bias,
):
    tokens = hidden.shape[1]
    width = hidden.shape[2]
    ctx_count = lax.axis_size("ctx")
    own_index = lax.axis_index("ctx")
    scale = float(HD) ** (-0.5)
    gathered = (
        lax.all_gather(self_qkv.astype(jnp.bfloat16), "fsdp", axis=0, tiled=True),
        lax.all_gather(self_out.astype(jnp.bfloat16), "fsdp", axis=0, tiled=True),
        lax.all_gather(cross_q.astype(jnp.bfloat16), "fsdp", axis=0, tiled=True),
        lax.all_gather(cross_kv.astype(jnp.bfloat16), "fsdp", axis=0, tiled=True),
        lax.all_gather(cross_out.astype(jnp.bfloat16), "fsdp", axis=0, tiled=True),
        lax.all_gather(ffn_in.astype(jnp.bfloat16), "fsdp", axis=0, tiled=True),
        lax.all_gather(ffn_out.astype(jnp.bfloat16), "fsdp", axis=0, tiled=True),
        lax.all_gather(biases.astype(jnp.bfloat16), "fsdp", axis=1, tiled=True),
        lax.all_gather(gains.astype(jnp.bfloat16), "fsdp", axis=1, tiled=True),
        lax.all_gather(ffn_bias.astype(jnp.bfloat16), "fsdp", axis=0, tiled=True),
    )
    w_qkv, w_so, w_cq, w_ckv, w_co, w_fi, w_fo, bias_low, gain_low, inner_low = gathered
    bias = bias_low.astype(jnp.float32)
    gain = gain_low.astype(jnp.float32)
    inner_bias = inner_low.astype(jnp.float32)
    all_segments, all_sources = (
        lax.all_gather(dec_seg, "ctx", axis=1, tiled=True),
        lax.all_gather(enc_seg, "ctx", axis=1, tiled=True),
    )
    all_segments = all_segments[0]
    all_sources = all_sources[0]
    own_segments = dec_seg[0]
    positions = own_index * tokens + jnp.arange(tokens, dtype=jnp.int32)
    inputs = hidden[0]
    input_wide = inputs.astype(jnp.float32)
    projected = matmul(inputs, w_qkv)
    queries = ((projected[:, :width] + bias[3]) * scale).astype(jnp.bfloat16)
    key_value = jnp.concatenate(
        [projected[:, width : 2 * width], projected[:, 2 * width :] + bias[4]], axis=1
    ).astype(jnp.bfloat16)
    query_heads = split_heads(queries)
    piece = lax.all_gather(key_value, "ctx", axis=0, tiled=True)
    count = piece.shape[0]
    key_segments = all_segments
    key_places = jnp.arange(count, dtype=jnp.int32)
    allowed = (own_segments[:, None] == key_segments[None, :]) & (
        key_places[None, :] <= positions[:, None]
    )
    scores = jnp.einsum(
        "qhd,khd->hqk",
        query_heads,
        split_heads(piece[:, :width]),
        preferred_element_type=jnp.float32,
    )
    attended, self_total = finish_state(
        online_update(empty_state(tokens), scores, allowed, split_heads(piece[:, width:]))
    )
    attended_low = attended.astype(jnp.bfloat16)
    first_sum = input_wide + matmul(attended_low, w_so) + bias[5]
    first, first_back = jax.vjp(layer_norm, first_sum, gain[0], bias[0])
    first_low = first.astype(jnp.bfloat16)
    cross_queries = ((matmul(first_low, w_cq) + bias[6]) * scale).astype(jnp.bfloat16)
    source_proj = matmul(encoded[0], w_ckv)
    source_pair = jnp.concatenate(
        [source_proj[:, :width], source_proj[:, width:] + bias[7]], axis=1
    ).astype(jnp.bfloat16)
    all_source_pair = lax.all_gather(source_pair, "ctx", axis=0, tiled=True)
    source_len = all_source_pair.shape[0]
    block = source_len if source_len <= 1024 else 1024
    block_ids = jnp.arange(source_len // block, dtype=jnp.int32)
    cross_heads = split_heads(cross_queries)

    def source_block(index):
        begin = index * block
        piece = lax.dynamic_slice_in_dim(all_source_pair, begin, block)
        allowed = (
            own_segments[:, None] == lax.dynamic_slice_in_dim(all_sources, begin, block)[None, :]
        )
        return (piece, allowed)

    def cross_step(carry, index):
        piece, allowed = source_block(index)
        scores = jnp.einsum(
            "qhd,khd->hqk",
            cross_heads,
            split_heads(piece[:, :width]),
            preferred_element_type=jnp.float32,
        )
        return (online_update(carry, scores, allowed, split_heads(piece[:, width:])), None)

    cross_state, _ = lax.scan(cross_step, empty_state(tokens), block_ids)
    cross_attended, cross_total = finish_state(cross_state)
    cross_low = cross_attended.astype(jnp.bfloat16)
    second_sum = first + matmul(cross_low, w_co) + bias[8]
    second, second_back = jax.vjp(layer_norm, second_sum, gain[1], bias[1])
    second_low = second.astype(jnp.bfloat16)
    inner_pre = matmul(second_low, w_fi) + inner_bias
    activated, gelu_back = jax.vjp(exact_gelu, inner_pre)
    activated_low = activated.astype(jnp.bfloat16)
    third_sum = second + matmul(activated_low, w_fo) + bias[9]
    result, third_back = jax.vjp(layer_norm, third_sum, gain[2], bias[2])
    output = result.astype(jnp.bfloat16)[None]
    again = (
        lax.all_gather(self_qkv.astype(jnp.bfloat16), "fsdp", axis=0, tiled=True),
        lax.all_gather(self_out.astype(jnp.bfloat16), "fsdp", axis=0, tiled=True),
        lax.all_gather(cross_q.astype(jnp.bfloat16), "fsdp", axis=0, tiled=True),
        lax.all_gather(cross_kv.astype(jnp.bfloat16), "fsdp", axis=0, tiled=True),
        lax.all_gather(cross_out.astype(jnp.bfloat16), "fsdp", axis=0, tiled=True),
        lax.all_gather(ffn_in.astype(jnp.bfloat16), "fsdp", axis=0, tiled=True),
        lax.all_gather(ffn_out.astype(jnp.bfloat16), "fsdp", axis=0, tiled=True),
    )
    w_qkv, w_so, w_cq, w_ckv, w_co, w_fi, w_fo = again
    third_grad, gain_three, shift_three = third_back(cotangent[0].astype(jnp.float32))
    ffn_grad = third_grad.astype(jnp.bfloat16)
    w_fo_grad = matmul_tn(activated_low, ffn_grad)
    inner_grad = gelu_back(matmul_nt(ffn_grad, w_fo))[0].astype(jnp.bfloat16)
    w_fi_grad = matmul_tn(second_low, inner_grad)
    second_grad = third_grad + matmul_nt(inner_grad, w_fi)
    sum_two_grad, gain_two, shift_two = second_back(second_grad)
    cross_branch = sum_two_grad.astype(jnp.bfloat16)
    w_co_grad = matmul_tn(cross_low, cross_branch)
    cross_out_grad = matmul_nt(cross_branch, w_co).astype(jnp.bfloat16)
    cross_grad_heads = split_heads(cross_out_grad)
    cross_inner = head_inner(cross_out_grad, cross_attended)

    def cross_back(query_acc, index):
        piece, allowed = source_block(index)
        query_part, source_part = block_grads(
            cross_heads,
            cross_grad_heads,
            cross_total,
            cross_inner,
            split_heads(piece[:, :width]),
            split_heads(piece[:, width:]),
            allowed,
        )
        return (query_acc + query_part, source_part)

    cross_query_grad, source_parts = lax.scan(
        cross_back, jnp.zeros((tokens, width), jnp.float32), block_ids
    )
    source_terms = source_parts.reshape(source_len, 2 * width)
    source_grad = lax.psum_scatter(source_terms, "ctx", scatter_dimension=0, tiled=True).astype(
        jnp.bfloat16
    )
    w_ckv_grad = matmul_tn(encoded[0], source_grad)
    encoded_grad = matmul_nt(source_grad, w_ckv)
    cross_query_pre = (cross_query_grad.astype(jnp.bfloat16).astype(jnp.float32) * scale).astype(
        jnp.bfloat16
    )
    w_cq_grad = matmul_tn(first_low, cross_query_pre)
    first_grad = sum_two_grad + matmul_nt(cross_query_pre, w_cq)
    sum_one_grad, gain_one, shift_one = first_back(first_grad)
    self_branch = sum_one_grad.astype(jnp.bfloat16)
    w_so_grad = matmul_tn(attended_low, self_branch)
    attended_grad = matmul_nt(self_branch, w_so).astype(jnp.bfloat16)
    self_inner = head_inner(attended_grad, attended)
    grad_heads = split_heads(attended_grad)

    def key_step(step, state):
        moving, moving_grad, query_acc = state
        owner = (own_index - step) % ctx_count
        begin = owner * tokens
        key_places = begin + jnp.arange(tokens, dtype=jnp.int32)
        key_segments = lax.dynamic_slice_in_dim(all_segments, begin, tokens)
        allowed = (own_segments[:, None] == key_segments[None, :]) & (
            key_places[None, :] <= positions[:, None]
        )
        query_part, pair_part = block_grads(
            query_heads,
            grad_heads,
            self_total,
            self_inner,
            split_heads(moving[:, :width]),
            split_heads(moving[:, width:]),
            allowed,
        )
        moving_wide, moving_grad = (
            from_behind(moving.astype(jnp.float32).astype(jnp.bfloat16), "ctx", 1).astype(
                jnp.float32
            ),
            from_behind((moving_grad + pair_part).astype(jnp.bfloat16), "ctx", 1).astype(
                jnp.float32
            ),
        )
        return (moving_wide.astype(jnp.bfloat16), moving_grad, query_acc + query_part)

    start_state = (
        key_value,
        jnp.zeros((tokens, 2 * width), jnp.float32),
        jnp.zeros((tokens, width), jnp.float32),
    )
    _, own_pair_grad, self_query_grad = lax.fori_loop(0, ctx_count, key_step, start_state)
    self_query_pre = (self_query_grad.astype(jnp.bfloat16).astype(jnp.float32) * scale).astype(
        jnp.bfloat16
    )
    own_pair_low = own_pair_grad.astype(jnp.bfloat16)
    projected_grad = jnp.concatenate([self_query_pre, own_pair_low], axis=1)
    w_qkv_grad = matmul_tn(inputs, projected_grad)
    input_grad = sum_one_grad + matmul_nt(projected_grad, w_qkv)
    bias_grad = jnp.stack(
        [
            shift_one,
            shift_two,
            shift_three,
            column_sum(self_query_pre),
            column_sum(own_pair_low[:, width:]),
            column_sum(self_branch),
            column_sum(cross_query_pre),
            column_sum(source_grad[:, width:]),
            column_sum(cross_branch),
            column_sum(ffn_grad),
        ]
    )
    gain_grad = jnp.stack([gain_one, gain_two, gain_three])
    inner_bias_grad = column_sum(inner_grad)
    g_qkv, g_so, g_cq, g_ckv, g_co, g_fi, g_fo, g_bias, g_gain, g_inner = (
        lax.psum_scatter(
            w_qkv_grad.astype(jnp.bfloat16), "fsdp", scatter_dimension=0, tiled=True
        ).astype(jnp.float32),
        lax.psum_scatter(
            w_so_grad.astype(jnp.bfloat16), "fsdp", scatter_dimension=0, tiled=True
        ).astype(jnp.float32),
        lax.psum_scatter(
            w_cq_grad.astype(jnp.bfloat16), "fsdp", scatter_dimension=0, tiled=True
        ).astype(jnp.float32),
        lax.psum_scatter(
            w_ckv_grad.astype(jnp.bfloat16), "fsdp", scatter_dimension=0, tiled=True
        ).astype(jnp.float32),
        lax.psum_scatter(
            w_co_grad.astype(jnp.bfloat16), "fsdp", scatter_dimension=0, tiled=True
        ).astype(jnp.float32),
        lax.psum_scatter(
            w_fi_grad.astype(jnp.bfloat16), "fsdp", scatter_dimension=0, tiled=True
        ).astype(jnp.float32),
        lax.psum_scatter(
            w_fo_grad.astype(jnp.bfloat16), "fsdp", scatter_dimension=0, tiled=True
        ).astype(jnp.float32),
        lax.psum_scatter(
            bias_grad.astype(jnp.bfloat16), "fsdp", scatter_dimension=1, tiled=True
        ).astype(jnp.float32),
        lax.psum_scatter(
            gain_grad.astype(jnp.bfloat16), "fsdp", scatter_dimension=1, tiled=True
        ).astype(jnp.float32),
        lax.psum_scatter(
            inner_bias_grad.astype(jnp.bfloat16), "fsdp", scatter_dimension=0, tiled=True
        ).astype(jnp.float32),
    )
    totals = lax.psum((g_qkv, g_so, g_cq, g_ckv, g_co, g_fi, g_fo, g_bias, g_gain, g_inner), "ctx")
    return (output, input_grad[None], encoded_grad[None]) + tuple(totals)


def solution(mesh):
    return jax.shard_map(
        body,
        mesh=mesh,
        in_specs=(
            P("fsdp", "ctx", None),
            P("fsdp", "ctx", None),
            P("fsdp", "ctx", None),
            P("fsdp", "ctx"),
            P("fsdp", "ctx"),
            P("fsdp", None),
            P("fsdp", None),
            P("fsdp", None),
            P("fsdp", None),
            P("fsdp", None),
            P("fsdp", None),
            P("fsdp", None),
            P(None, "fsdp"),
            P(None, "fsdp"),
            P("fsdp"),
        ),
        out_specs=(
            P("fsdp", "ctx", None),
            P("fsdp", "ctx", None),
            P("fsdp", "ctx", None),
            P("fsdp", None),
            P("fsdp", None),
            P("fsdp", None),
            P("fsdp", None),
            P("fsdp", None),
            P("fsdp", None),
            P("fsdp", None),
            P(None, "fsdp"),
            P(None, "fsdp"),
            P("fsdp"),
        ),
        check_vma=False,
    )
```

profile of v0, /device:TPU:0, one launch (start us, length us, event | category | flops | bytes accessed | tf_op | source)
XLA Modules:
  0.0 1119.0 jit_solution(12571187997611477748)
XLA Ops:
  7.2 2.6 convert_element_type.290
  10.9 6.2 all-gather
  17.2 26.4 %all-gather.12.cloned.1.call-done = bf16[768,2304]{1,0:T(8,128)(2,1)} async-done(((bf16[192,2304]{1,0:T(8,128)(2,1)}), bf16[768,2304]{1,0:T(8,128)(2,1)}) %all-gather.12.cloned.1.call-update) | async-done | bytes 3538960 | tf_op jit(solution)/shard_map/all_gather | solution.py:136
  43.7 2.6 fusion.67
  47.3 2.0 convert_element_type.296
  54.4 2.8 convert_element_type.311
  57.3 20.4 %all_gather.53 = s32[1,1024]{1,0:T(1,128)S(1)} all-gather(s32[1,128]{1,0:T(1,128)S(1)} %copy-done.44), channel_id=1, replica_groups=mesh['fsdp'=4,'ctx'=8] {'ctx'}, dimensions={1}, use_global_device_ids=true | all-gather | bytes 4608 | tf_op jit(solution)/shard_map/all_gather | solution.py:152
  77.7 5.1 all-gather.1
  84.4 7.0 all-reduce
  91.3 5.2 all-gather.2
  96.9 2.2 fusion.75
  99.1 35.6 %all_gather.64 = bf16[256,1536]{1,0:T(8,128)(2,1)S(1)} all-gather(bf16[32,1536]{1,0:T(8,128)(2,1)S(1)} %pad_maximum_fusion.5), channel_id=1, replica_groups=mesh['fsdp'=4,'ctx'=8] {'ctx'}, dimensions={0}, use_global_device_ids=true | all-gather | bytes 884736 | tf_op jit(solution)/shard_map/all_gather | solution.py:192
  136.0 11.1 all-gather.14.cloned.1.call-done
  147.1 3.7 fusion.103
  152.6 2.6 copy.89
  156.4 1.9 fusion.9
  158.3 1.9 fusion.42
  160.2 5.1 all-gather.16.cloned.1.call-done
  167.3 17.0 %all-gather.18.cloned.1.call-done = bf16[768,768]{1,0:T(8,128)(2,1)} async-done(((bf16[192,768]{1,0:T(8,128)(2,1)}), bf16[768,768]{1,0:T(8,128)(2,1)}) %all-gather.18.cloned.1.call-update) | async-done | bytes 1179664 | tf_op jit(solution)/shard_map/all_gather | solution.py:138
  188.8 14.3 %all-gather.22.cloned.1.call-done = bf16[768,768]{1,0:T(8,128)(2,1)} async-done(((bf16[192,768]{1,0:T(8,128)(2,1)}), bf16[768,768]{1,0:T(8,128)(2,1)}) %all-gather.22.cloned.1.call-update) | async-done | bytes 1179664 | tf_op jit(solution)/shard_map/all_gather | solution.py:140
  205.1 37.7 %all-gather.24.cloned.1.call-done = bf16[768,3072]{1,0:T(8,128)(2,1)} async-done(((bf16[192,3072]{1,0:T(8,128)(2,1)}), bf16[768,3072]{1,0:T(8,128)(2,1)}) %all-gather.24.cloned.1.call-update) | async-done | bytes 4718608 | tf_op jit(solution)/shard_map/all_gather | solution.py:141
  242.8 8.5 multiply_convert_fusion.1
  251.3 31.1 %all-gather.26.cloned.1.call-done = bf16[3072,768]{1,0:T(8,128)(2,1)} async-done(((bf16[768,768]{1,0:T(8,128)(2,1)}), bf16[3072,768]{1,0:T(8,128)(2,1)}) %all-gather.26.cloned.1.call-update) | async-done | bytes 4718608 | tf_op jit(solution)/shard_map/all_gather | solution.py:142
  282.4 3.4 fusion.107
  287.4 1.9 fusion.93
  309.2 1.9 copy.98
  318.6 177.4 %while.13 = (s32[]{:T(128)}, bf16[128,1536]{0,1:T(8,128)(2,1)S(1)}, f32[128,1536]{0,1:T(8,128)S(1)}, f32[128,768]{0,1:T(8,128)}, s32[1,128]{1,0:T(1,128)S(1)}, /...) while((s32[]{:T(128)}, bf16[128,1536]{0,1:T(8,128)(2,1)S(1)}, ...), condition=%wide.region_19.20_spmd.clone, body=%wide.region_18.19_spmd.clone.sunk | while | flops 128237840 | bytes 15188403 | solution.py:318
  325.5 20.0 %collective-permute-done.1 = bf16[128,1536]{0,1:T(8,128)(2,1)} collective-permute-done((bf16[128,1536]{0,1:T(8,128)(2,1)}, bf16[128,1536]{0,1:T(8,128)(2,1)}, u32[]{:S(2)}, u32[]{:S(2)}) %collective-permute-start.1) | collective-permute-done | bytes 393248 | tf_op jit(solution)/shard_map/while/body/eval_jaxpr/ppermute | solution.py:17
  352.8 16.2 %collective-permute-done.1 = bf16[128,1536]{0,1:T(8,128)(2,1)} collective-permute-done((bf16[128,1536]{0,1:T(8,128)(2,1)}, bf16[128,1536]{0,1:T(8,128)(2,1)}, u32[]{:S(2)}, u32[]{:S(2)}) %collective-permute-start.1) | collective-permute-done | bytes 393248 | tf_op jit(solution)/shard_map/while/body/eval_jaxpr/ppermute | solution.py:17
  374.8 18.9 %collective-permute-done.1 = bf16[128,1536]{0,1:T(8,128)(2,1)} collective-permute-done((bf16[128,1536]{0,1:T(8,128)(2,1)}, bf16[128,1536]{0,1:T(8,128)(2,1)}, u32[]{:S(2)}, u32[]{:S(2)}) %collective-permute-start.1) | collective-permute-done | bytes 393248 | tf_op jit(solution)/shard_map/while/body/eval_jaxpr/ppermute | solution.py:17
  399.5 16.3 %collective-permute-done.1 = bf16[128,1536]{0,1:T(8,128)(2,1)} collective-permute-done((bf16[128,1536]{0,1:T(8,128)(2,1)}, bf16[128,1536]{0,1:T(8,128)(2,1)}, u32[]{:S(2)}, u32[]{:S(2)}) %collective-permute-start.1) | collective-permute-done | bytes 393248 | tf_op jit(solution)/shard_map/while/body/eval_jaxpr/ppermute | solution.py:17
  421.6 15.4 %collective-permute-done.1 = bf16[128,1536]{0,1:T(8,128)(2,1)} collective-permute-done((bf16[128,1536]{0,1:T(8,128)(2,1)}, bf16[128,1536]{0,1:T(8,128)(2,1)}, u32[]{:S(2)}, u32[]{:S(2)}) %collective-permute-start.1) | collective-permute-done | bytes 393248 | tf_op jit(solution)/shard_map/while/body/eval_jaxpr/ppermute | solution.py:17
  442.8 14.5 %collective-permute-done.1 = bf16[128,1536]{0,1:T(8,128)(2,1)} collective-permute-done((bf16[128,1536]{0,1:T(8,128)(2,1)}, bf16[128,1536]{0,1:T(8,128)(2,1)}, u32[]{:S(2)}, u32[]{:S(2)}) %collective-permute-start.1) | collective-permute-done | bytes 393248 | tf_op jit(solution)/shard_map/while/body/eval_jaxpr/ppermute | solution.py:17
  463.1 13.5 %collective-permute-done.1 = bf16[128,1536]{0,1:T(8,128)(2,1)} collective-permute-done((bf16[128,1536]{0,1:T(8,128)(2,1)}, bf16[128,1536]{0,1:T(8,128)(2,1)}, u32[]{:S(2)}, u32[]{:S(2)}) %collective-permute-start.1) | collective-permute-done | bytes 393248 | tf_op jit(solution)/shard_map/while/body/eval_jaxpr/ppermute | solution.py:17
  482.5 12.5 %collective-permute-done.1 = bf16[128,1536]{0,1:T(8,128)(2,1)} collective-permute-done((bf16[128,1536]{0,1:T(8,128)(2,1)}, bf16[128,1536]{0,1:T(8,128)(2,1)}, u32[]{:S(2)}, u32[]{:S(2)}) %collective-permute-start.1) | collective-permute-done | bytes 393248 | tf_op jit(solution)/shard_map/while/body/eval_jaxpr/ppermute | solution.py:17
  500.1 2.8 fusion.11
  503.0 5.8 copy.107
  510.6 2.4 copy.109
  514.1 3.6 convolution_convert_fusion.1
  518.9 3.6 convolution_convert_fusion
  524.4 6.5 all-reduce.1
  531.0 5.0 fusion.28
  539.3 25.8 %reduce-scatter.33.cloned.1.call-done = bf16[192,2304]{1,0:T(8,128)(2,1)} async-done(((bf16[768,2304]{1,0:T(8,128)(2,1)}), bf16[192,2304]{1,0:T(8,128)(2,1)}) %reduce-scatter.33.cloned.1.call-update) | async-done | bytes 884752
  566.6 34.7 %reduce-scatter.35.cloned.1.call-done = bf16[192,1536]{1,0:T(8,128)(2,1)} async-done(((bf16[768,1536]{1,0:T(8,128)(2,1)}), bf16[192,1536]{1,0:T(8,128)(2,1)}) %reduce-scatter.35.cloned.1.call-update) | async-done | bytes 589840
  602.7 48.9 %reduce-scatter.27.cloned.1.call-done = bf16[192,3072]{1,0:T(8,128)(2,1)} async-done(((bf16[768,3072]{1,0:T(8,128)(2,1)}), bf16[192,3072]{1,0:T(8,128)(2,1)}) %reduce-scatter.27.cloned.1.call-update) | async-done | bytes 1179664 | tf_op jit(solution)/shard_map/reduce_scatter | solution.py:358
  651.6 50.5 %reduce-scatter.29.cloned.1.call-done = bf16[768,768]{1,0:T(8,128)(2,1)} async-done(((bf16[3072,768]{1,0:T(8,128)(2,1)}), bf16[768,768]{1,0:T(8,128)(2,1)}) %reduce-scatter.29.cloned.1.call-update) | async-done | bytes 1179664 | tf_op jit(solution)/shard_map/reduce_scatter | solution.py:361
  702.0 405.2 %all-reduce.4 = (f32[192,2304]{0,1:T(8,128)}, f32[192,768]{1,0:T(8,128)}, f32[192,768]{1,0:T(8,128)}, f32[192,1536]{0,1:T(8,128)}, f32[192,768]{1,0:T(8,128)}, /...) all-reduce(bf16[192,2304]{0,1:T(8,128)(2,1)S(1)} %copy.108, ...), channel_id=1, replica_groups=mesh['fsdp'=4,'ctx'=8] {'ctx'}, use_global_device_ids=true, to_apply=%region_22.23 | all-reduce | flops 2362560 | bytes 14176896 | tf_op jit(solution)/shard_map/psum | solution.py:374
  1107.2 3.0 copy.103
  (420 shorter events, 115.6 us)
Async XLA Ops:
  7.2 89.7 %copy-start = (bf16[1,32,768]{2,1,0:T(8,128)(2,1)S(1)}, bf16[1,32,768]{2,1,0:T(8,128)(2,1)}, u32[]{:S(2)}) copy-start(bf16[1,32,768]{2,1,0:T(8,128)(2,1)} %param.18) | copy-start | bytes 147460
  7.2 36.5 %all-gather.12.cloned.1.call-start = ((), (), s32[]{:S(2)}) async-start(), calls=%async_computation.10 | async-start | bytes 4423680 | tf_op jit(solution)/shard_map/all_gather | solution.py:136
  9.8 33.9 %copy-start.21 = (bf16[1,128,768]{2,1,0:T(8,128)(2,1)S(1)}, bf16[1,128,768]{2,1,0:T(8,128)(2,1)}, u32[]{:S(2)}) copy-start(bf16[1,128,768]{2,1,0:T(8,128)(2,1)} %param.17) | copy-start | bytes 589828
  9.8 87.0 %all-gather.20.cloned.1.call-start = ((), (), s32[]{:S(2)}) async-start(), calls=%async_computation.14 | async-start | bytes 2949120 | tf_op jit(solution)/shard_map/all_gather | solution.py:139
  10.8 136.3 %all-gather.14.cloned.1.call-start = ((), (), s32[]{:S(2)}) async-start(), calls=%async_computation.11 | async-start | bytes 3538944 | tf_op jit(solution)/shard_map/all_gather | solution.py:167
  47.2 118.1 %all-gather.16.cloned.1.call-start = ((), (), s32[]{:S(2)}) async-start(), calls=%async_computation.12 | async-start | bytes 1474560 | tf_op jit(solution)/shard_map/all_gather | solution.py:137
  49.3 135.0 %all-gather.18.cloned.1.call-start = ((), (), s32[]{:S(2)}) async-start(), calls=%async_computation.13 | async-start | bytes 1474560 | tf_op jit(solution)/shard_map/all_gather | solution.py:138
  51.1 152.0 %all-gather.22.cloned.1.call-start = ((), (), s32[]{:S(2)}) async-start(), calls=%async_computation.15 | async-start | bytes 1474560 | tf_op jit(solution)/shard_map/all_gather | solution.py:140
  53.0 189.7 %all-gather.24.cloned.1.call-start = ((), (), s32[]{:S(2)}) async-start(), calls=%async_computation.16 | async-start | bytes 5898240 | tf_op jit(solution)/shard_map/all_gather | solution.py:141
  54.3 23.4 %copy-start.46 = (f32[3,192]{1,0:T(4,128)S(1)}, f32[3,192]{1,0:T(4,128)}, u32[]{:S(2)}) copy-start(f32[3,192]{1,0:T(4,128)} %param.30) | copy-start | bytes 6916
  54.3 28.7 %copy-start.50 = (u32[32]{0:T(128)S(1)}, u32[32]{0:T(128)}, u32[]{:S(2)}) copy-start(u32[32]{0:T(128)} %constant.216) | copy-start | bytes 388
  54.3 29.9 %copy-start.48 = (s32[1,32]{1,0:T(1,128)S(1)}, s32[1,32]{1,0:T(1,128)}, u32[]{:S(2)}) copy-start(s32[1,32]{1,0:T(1,128)} %param.21) | copy-start | bytes 388
  54.3 37.0 %copy-start.47 = (f32[768]{0:T(1024)S(1)}, f32[768]{0:T(1024)}, u32[]{:S(2)}) copy-start(f32[768]{0:T(1024)} %param.31) | copy-start | bytes 9220
  54.4 228.1 %all-gather.26.cloned.1.call-start = ((), (), s32[]{:S(2)}) async-start(), calls=%async_computation.17 | async-start | bytes 5898240 | tf_op jit(solution)/shard_map/all_gather | solution.py:142
  57.2 440.6 %reduce-scatter.31.cloned.1.call-start = ((), (), s32[]{:S(2)}) async-start(), calls=%async_computation.23 | async-start | bytes 1769472
  134.9 51.2 %copy-start.14 = (bf16[256,768]{0,1:T(8,128)(2,1)}, bf16[256,768]{0,1:T(8,128)(2,1)S(1)}, u32[]{:S(2)}) copy-start(bf16[256,768]{0,1:T(8,128)(2,1)S(1)} %copy.92) | copy-start | bytes 1179652
  160.2 25.7 %copy-start.9 = (f32[128,12,64]{0,2,1:T(8,128)}, f32[128,12,64]{0,2,1:T(8,128)S(1)}, u32[]{:S(2)}) copy-start(f32[128,12,64]{0,2,1:T(8,128)S(1)} %fusion.42) | copy-start | bytes 1179652
  187.9 17.0 %copy-start.11 = (f32[128,12,64]{0,2,1:T(8,128)}, f32[128,12,64]{0,2,1:T(8,128)S(1)}, u32[]{:S(2)}) copy-start(f32[128,12,64]{0,2,1:T(8,128)S(1)} %fusion.26) | copy-start | bytes 1179652
  251.3 34.5 %copy-start.2 = (bf16[128,3072]{1,0:T(8,128)(2,1)}, bf16[128,3072]{1,0:T(8,128)(2,1)S(1)}, u32[]{:S(2)}) copy-start(bf16[128,3072]{1,0:T(8,128)(2,1)S(1)} %get-tuple-element.570) | copy-start | bytes 2359300
  300.1 235.9 %reduce-scatter.39.cloned.1.call-start = ((), (), s32[]{:S(2)}) async-start(), calls=%async_computation.27 | async-start | bytes 245760
  304.4 232.5 %reduce-scatter.25.cloned.1.call-start = ((), (), s32[]{:S(2)}) async-start(), calls=%async_computation.20 | async-start | bytes 1474560 | tf_op jit(solution)/shard_map/reduce_scatter | solution.py:355
  306.1 230.8 %reduce-scatter.23.cloned.1.call-start = ((), (), s32[]{:S(2)}) async-start(), calls=%async_computation.19 | async-start | bytes 1474560 | tf_op jit(solution)/shard_map/reduce_scatter | solution.py:349
  307.8 229.2 %reduce-scatter.21.cloned.1.call-start = ((), (), s32[]{:S(2)}) async-start(), calls=%async_computation.18 | async-start | bytes 1474560 | tf_op jit(solution)/shard_map/reduce_scatter | solution.py:346
  318.5 219.9 %reduce-scatter.37.cloned.1.call-start = ((), (), s32[]{:S(2)}) async-start(), calls=%async_computation.26 | async-start | bytes 245760
  318.9 27.6 %collective-permute-start = (bf16[128,1536]{0,1:T(8,128)(2,1)S(1)}, bf16[128,1536]{0,1:T(8,128)(2,1)S(1)}, u32[]{:S(2)}, u32[]{:S(2)}) collective-permute-start(bf16[128,1536]{0,1:T(8,128)(2,1)S(1)} %copy.122), channel_id=1, source_target_pairs={{7,0},{0,1},{1,2},{2,3},{3,4},{4,5},{5,6},{6,7},{15,8},{8,9},{9,10... | collective-permute-start | bytes 1179656 | tf_op jit(solution)/shard_map/while/body/eval_jaxpr/ppermute | solution.py:17
  322.8 22.7 %collective-permute-start.1 = (bf16[128,1536]{0,1:T(8,128)(2,1)}, bf16[128,1536]{0,1:T(8,128)(2,1)}, u32[]{:S(2)}, u32[]{:S(2)}) collective-permute-start(bf16[128,1536]{0,1:T(8,128)(2,1)} %fusion.193), channel_id=1, source_target_pairs={{7,0},{0,1},{1,2},{2,3},{3,4},{4,5},{5,6},{6,7},{15,8},{8,9},{9,10... | collective-permute-start | bytes 1179656 | tf_op jit(solution)/shard_map/while/body/eval_jaxpr/ppermute | solution.py:17
  346.6 23.4 %collective-permute-start = (bf16[128,1536]{0,1:T(8,128)(2,1)S(1)}, bf16[128,1536]{0,1:T(8,128)(2,1)S(1)}, u32[]{:S(2)}, u32[]{:S(2)}) collective-permute-start(bf16[128,1536]{0,1:T(8,128)(2,1)S(1)} %copy.122), channel_id=1, source_target_pairs={{7,0},{0,1},{1,2},{2,3},{3,4},{4,5},{5,6},{6,7},{15,8},{8,9},{9,10... | collective-permute-start | bytes 1179656 | tf_op jit(solution)/shard_map/while/body/eval_jaxpr/ppermute | solution.py:17
  349.1 19.8 %collective-permute-start.1 = (bf16[128,1536]{0,1:T(8,128)(2,1)}, bf16[128,1536]{0,1:T(8,128)(2,1)}, u32[]{:S(2)}, u32[]{:S(2)}) collective-permute-start(bf16[128,1536]{0,1:T(8,128)(2,1)} %fusion.193), channel_id=1, source_target_pairs={{7,0},{0,1},{1,2},{2,3},{3,4},{4,5},{5,6},{6,7},{15,8},{8,9},{9,10... | collective-permute-start | bytes 1179656 | tf_op jit(solution)/shard_map/while/body/eval_jaxpr/ppermute | solution.py:17
  370.0 24.7 %collective-permute-start = (bf16[128,1536]{0,1:T(8,128)(2,1)S(1)}, bf16[128,1536]{0,1:T(8,128)(2,1)S(1)}, u32[]{:S(2)}, u32[]{:S(2)}) collective-permute-start(bf16[128,1536]{0,1:T(8,128)(2,1)S(1)} %copy.122), channel_id=1, source_target_pairs={{7,0},{0,1},{1,2},{2,3},{3,4},{4,5},{5,6},{6,7},{15,8},{8,9},{9,10... | collective-permute-start | bytes 1179656 | tf_op jit(solution)/shard_map/while/body/eval_jaxpr/ppermute | solution.py:17
  372.6 21.1 %collective-permute-start.1 = (bf16[128,1536]{0,1:T(8,128)(2,1)}, bf16[128,1536]{0,1:T(8,128)(2,1)}, u32[]{:S(2)}, u32[]{:S(2)}) collective-permute-start(bf16[128,1536]{0,1:T(8,128)(2,1)} %fusion.193), channel_id=1, source_target_pairs={{7,0},{0,1},{1,2},{2,3},{3,4},{4,5},{5,6},{6,7},{15,8},{8,9},{9,10... | collective-permute-start | bytes 1179656 | tf_op jit(solution)/shard_map/while/body/eval_jaxpr/ppermute | solution.py:17
  394.8 22.1 %collective-permute-start = (bf16[128,1536]{0,1:T(8,128)(2,1)S(1)}, bf16[128,1536]{0,1:T(8,128)(2,1)S(1)}, u32[]{:S(2)}, u32[]{:S(2)}) collective-permute-start(bf16[128,1536]{0,1:T(8,128)(2,1)S(1)} %copy.122), channel_id=1, source_target_pairs={{7,0},{0,1},{1,2},{2,3},{3,4},{4,5},{5,6},{6,7},{15,8},{8,9},{9,10... | collective-permute-start | bytes 1179656 | tf_op jit(solution)/shard_map/while/body/eval_jaxpr/ppermute | solution.py:17
  397.3 18.5 %collective-permute-start.1 = (bf16[128,1536]{0,1:T(8,128)(2,1)}, bf16[128,1536]{0,1:T(8,128)(2,1)}, u32[]{:S(2)}, u32[]{:S(2)}) collective-permute-start(bf16[128,1536]{0,1:T(8,128)(2,1)} %fusion.193), channel_id=1, source_target_pairs={{7,0},{0,1},{1,2},{2,3},{3,4},{4,5},{5,6},{6,7},{15,8},{8,9},{9,10... | collective-permute-start | bytes 1179656 | tf_op jit(solution)/shard_map/while/body/eval_jaxpr/ppermute | solution.py:17
  416.9 21.1 %collective-permute-start = (bf16[128,1536]{0,1:T(8,128)(2,1)S(1)}, bf16[128,1536]{0,1:T(8,128)(2,1)S(1)}, u32[]{:S(2)}, u32[]{:S(2)}) collective-permute-start(bf16[128,1536]{0,1:T(8,128)(2,1)S(1)} %copy.122), channel_id=1, source_target_pairs={{7,0},{0,1},{1,2},{2,3},{3,4},{4,5},{5,6},{6,7},{15,8},{8,9},{9,10... | collective-permute-start | bytes 1179656 | tf_op jit(solution)/shard_map/while/body/eval_jaxpr/ppermute | solution.py:17
  419.4 17.6 %collective-permute-start.1 = (bf16[128,1536]{0,1:T(8,128)(2,1)}, bf16[128,1536]{0,1:T(8,128)(2,1)}, u32[]{:S(2)}, u32[]{:S(2)}) collective-permute-start(bf16[128,1536]{0,1:T(8,128)(2,1)} %fusion.193), channel_id=1, source_target_pairs={{7,0},{0,1},{1,2},{2,3},{3,4},{4,5},{5,6},{6,7},{15,8},{8,9},{9,10... | collective-permute-start | bytes 1179656 | tf_op jit(solution)/shard_map/while/body/eval_jaxpr/ppermute | solution.py:17
  438.1 20.2 %collective-permute-start = (bf16[128,1536]{0,1:T(8,128)(2,1)S(1)}, bf16[128,1536]{0,1:T(8,128)(2,1)S(1)}, u32[]{:S(2)}, u32[]{:S(2)}) collective-permute-start(bf16[128,1536]{0,1:T(8,128)(2,1)S(1)} %copy.122), channel_id=1, source_target_pairs={{7,0},{0,1},{1,2},{2,3},{3,4},{4,5},{5,6},{6,7},{15,8},{8,9},{9,10... | collective-permute-start | bytes 1179656 | tf_op jit(solution)/shard_map/while/body/eval_jaxpr/ppermute | solution.py:17
  440.6 16.6 %collective-permute-start.1 = (bf16[128,1536]{0,1:T(8,128)(2,1)}, bf16[128,1536]{0,1:T(8,128)(2,1)}, u32[]{:S(2)}, u32[]{:S(2)}) collective-permute-start(bf16[128,1536]{0,1:T(8,128)(2,1)} %fusion.193), channel_id=1, source_target_pairs={{7,0},{0,1},{1,2},{2,3},{3,4},{4,5},{5,6},{6,7},{15,8},{8,9},{9,10... | collective-permute-start | bytes 1179656 | tf_op jit(solution)/shard_map/while/body/eval_jaxpr/ppermute | solution.py:17
  458.4 19.3 %collective-permute-start = (bf16[128,1536]{0,1:T(8,128)(2,1)S(1)}, bf16[128,1536]{0,1:T(8,128)(2,1)S(1)}, u32[]{:S(2)}, u32[]{:S(2)}) collective-permute-start(bf16[128,1536]{0,1:T(8,128)(2,1)S(1)} %copy.122), channel_id=1, source_target_pairs={{7,0},{0,1},{1,2},{2,3},{3,4},{4,5},{5,6},{6,7},{15,8},{8,9},{9,10... | collective-permute-start | bytes 1179656 | tf_op jit(solution)/shard_map/while/body/eval_jaxpr/ppermute | solution.py:17
  460.9 15.7 %collective-permute-start.1 = (bf16[128,1536]{0,1:T(8,128)(2,1)}, bf16[128,1536]{0,1:T(8,128)(2,1)}, u32[]{:S(2)}, u32[]{:S(2)}) collective-permute-start(bf16[128,1536]{0,1:T(8,128)(2,1)} %fusion.193), channel_id=1, source_target_pairs={{7,0},{0,1},{1,2},{2,3},{3,4},{4,5},{5,6},{6,7},{15,8},{8,9},{9,10... | collective-permute-start | bytes 1179656 | tf_op jit(solution)/shard_map/while/body/eval_jaxpr/ppermute | solution.py:17
  477.7 18.3 %collective-permute-start = (bf16[128,1536]{0,1:T(8,128)(2,1)S(1)}, bf16[128,1536]{0,1:T(8,128)(2,1)S(1)}, u32[]{:S(2)}, u32[]{:S(2)}) collective-permute-start(bf16[128,1536]{0,1:T(8,128)(2,1)S(1)} %copy.122), channel_id=1, source_target_pairs={{7,0},{0,1},{1,2},{2,3},{3,4},{4,5},{5,6},{6,7},{15,8},{8,9},{9,10... | collective-permute-start | bytes 1179656 | tf_op jit(solution)/shard_map/while/body/eval_jaxpr/ppermute | solution.py:17
  480.3 14.7 %collective-permute-start.1 = (bf16[128,1536]{0,1:T(8,128)(2,1)}, bf16[128,1536]{0,1:T(8,128)(2,1)}, u32[]{:S(2)}, u32[]{:S(2)}) collective-permute-start(bf16[128,1536]{0,1:T(8,128)(2,1)} %fusion.193), channel_id=1, source_target_pairs={{7,0},{0,1},{1,2},{2,3},{3,4},{4,5},{5,6},{6,7},{15,8},{8,9},{9,10... | collective-permute-start | bytes 1179656 | tf_op jit(solution)/shard_map/while/body/eval_jaxpr/ppermute | solution.py:17
  500.1 65.0 %reduce-scatter.33.cloned.1.call-start = ((), (), s32[]{:S(2)}) async-start(), calls=%async_computation.24 | async-start | bytes 4423680
  508.8 92.5 %reduce-scatter.35.cloned.1.call-start = ((), (), s32[]{:S(2)}) async-start(), calls=%async_computation.25 | async-start | bytes 2949120
  513.0 138.5 %reduce-scatter.27.cloned.1.call-start = ((), (), s32[]{:S(2)}) async-start(), calls=%async_computation.21 | async-start | bytes 5898240 | tf_op jit(solution)/shard_map/reduce_scatter | solution.py:358
  517.8 184.2 %reduce-scatter.29.cloned.1.call-start = ((), (), s32[]{:S(2)}) async-start(), calls=%async_computation.22 | async-start | bytes 5898240 | tf_op jit(solution)/shard_map/reduce_scatter | solution.py:361
  531.0 5.9 copy-start.5
  539.3 162.7 %copy-start.41 = (bf16[192,768]{1,0:T(8,128)(2,1)S(1)}, bf16[192,768]{1,0:T(8,128)(2,1)}, u32[]{:S(2)}) copy-start(bf16[192,768]{1,0:T(8,128)(2,1)} %reduce-scatter.25.cloned.1.call-done) | copy-start | bytes 884740
  539.3 162.7 %copy-start.42 = (bf16[192,768]{1,0:T(8,128)(2,1)S(1)}, bf16[192,768]{1,0:T(8,128)(2,1)}, u32[]{:S(2)}) copy-start(bf16[192,768]{1,0:T(8,128)(2,1)} %reduce-scatter.23.cloned.1.call-done) | copy-start | bytes 884740
  539.3 162.7 %copy-start.43 = (bf16[192,768]{1,0:T(8,128)(2,1)S(1)}, bf16[192,768]{1,0:T(8,128)(2,1)}, u32[]{:S(2)}) copy-start(bf16[192,768]{1,0:T(8,128)(2,1)} %reduce-scatter.21.cloned.1.call-done) | copy-start | bytes 884740
  (43 other events, 99.9 us)
Sparse Core Ops, SparseCore 0:
  10.2 33.4 all-gather.11
  45.8 24.0 all-gather.19
  72.7 74.3 all-gather.13
  148.5 16.7 all-gather.15
  166.8 17.4 all-gather.17
  185.7 17.4 all-gather.21
  205.3 37.4 all-gather.23
  244.9 37.4 all-gather.25
  300.3 78.3 reduce-scatter.30
  381.0 32.1 reduce-scatter.38
  416.0 25.6 reduce-scatter.24
  444.7 25.7 reduce-scatter.22
  473.8 25.7 reduce-scatter.20
  502.4 19.7 reduce-scatter.36
  524.6 40.4 reduce-scatter.32
  568.2 33.0 reduce-scatter.34
  603.7 47.8 reduce-scatter.26
  654.1 47.8 reduce-scatter.28
where the time goes:
time: 1120 us
  blocking collectives  491 us (44%)
  waiting for transfers between devices  430 us (38%)
  matrix products  72.6 us (6%)
  other arithmetic  50.8 us (5%)
  local copies, waits for them, and re-layouts  50.3 us (4%)
  between operations  17.2 us (2%)
    psum x1, blocking collectives, body(): lax.psum((g_qkv, g_so, g_cq, g_ckv, g_co, g_fi, g_fo, g_bias, g_gain, g_i...  405 us
    ppermute x16, waiting for transfers between devices, from_behind(): return lax.ppermute(block, axis, route)  127 us
    unnamed x23, waiting for transfers between devices  60.8 us
    reduce_scatter x1, waiting for transfers between devices, body(): lax.psum_scatter(w_fo_grad.astype(jnp.bfloat16), 'fsdp', scatter_dimensio...  50.5 us
    reduce_scatter x1, waiting for transfers between devices, body(): lax.psum_scatter(w_fi_grad.astype(jnp.bfloat16), 'fsdp', scatter_dimensio...  48.9 us
    all_gather x1, waiting for transfers between devices, body(): lax.all_gather(ffn_in.astype(jnp.bfloat16), 'fsdp', axis=0, tiled=True)  37.7 us
    all_gather x1, blocking collectives, body(): all_source_pair = lax.all_gather(source_pair, 'ctx', axis=0, tiled=True)  35.6 us
    unnamed x132, local copies, waits for them, and re-layouts  31.5 us
  transfers between devices with their start and end apart: 34, of which 19 were waited for; matrix products, arithmetic and copies ran while one was open for 13% of the time, Pallas kernels for 0%

commit v1 on v0

v1 whole, which is shorter than its diff:
```python
import jax
import jax.numpy as jnp
from jax import lax
from jax.sharding import PartitionSpec as P

H = 12
HD = 64
EPSILON = 1e-05
FLOOR_SCORE = -1e30
LOW = jnp.bfloat16
WIDE = jnp.float32


def mm(left, right):
    return jnp.dot(left, right, preferred_element_type=WIDE)


def mm_tn(left, right):
    return lax.dot_general(left, right, (((0,), (0,)), ((), ())), preferred_element_type=WIDE)


def mm_nt(left, right):
    return lax.dot_general(left, right, (((1,), (1,)), ((), ())), preferred_element_type=WIDE)


def flip_model(value, bit):
    count = lax.axis_size("fsdp")
    return lax.ppermute(value, "fsdp", [(i, i ^ bit) for i in range(count)])


def flip_ctx(value, bit):
    count = lax.axis_size("ctx")
    return lax.ppermute(value, "ctx", [(i, i ^ bit) for i in range(count)])


def swap_places(value):
    model = lax.axis_size("fsdp")
    ctx = lax.axis_size("ctx")
    lines = ctx // model
    route = []
    for f in range(model):
        for z in range(model):
            for r in range(lines):
                route.append((f * ctx + z * lines + r, z * ctx + f * lines + r))
    return lax.ppermute(value, ("fsdp", "ctx"), route)


def line_bits():
    lines = lax.axis_size("ctx") // lax.axis_size("fsdp")
    bits = []
    bit = 1
    while bit < lines:
        bits.append(bit)
        bit *= 2
    return bits


def ctx_bits():
    bits = []
    bit = 1
    while bit < lax.axis_size("ctx"):
        bits.append(bit)
        bit *= 2
    return bits


def gather_plane(block):
    part = jnp.stack([block, flip_model(block, 2)])[None]
    for bit in line_bits():
        part = jnp.concatenate([part, flip_ctx(part, bit)], axis=0)
    return jnp.stack([part, flip_model(part, 1)], axis=1)


def normalize(values):
    center = values - jnp.mean(values, axis=-1, keepdims=True)
    spread = jnp.mean(center * center, axis=-1, keepdims=True)
    rate = lax.rsqrt(spread + EPSILON)
    return center * rate, rate


def normalize_back(grad, normal, rate, gain):
    up = grad * gain
    mean_up = jnp.mean(up, axis=-1, keepdims=True)
    mean_both = jnp.mean(up * normal, axis=-1, keepdims=True)
    return rate * (up - mean_up - normal * mean_both)


def tensor_sum(partial):
    rows = partial.shape[0] // 2
    half = rows // 2
    mine = partial[:rows] + flip_model(partial[rows:].astype(LOW), 1).astype(WIDE)
    other = flip_model(mine.astype(LOW), 2)
    other = jnp.concatenate([other[half:], other[:half]], axis=0)
    return mine + other.astype(WIDE)


def spread_rows(half):
    return jnp.concatenate([half, flip_model(half, 1)], axis=0)


def pick(stacked, index):
    return lax.dynamic_index_in_dim(stacked, index, 0, keepdims=False)


def to_columns(blocks, own):
    far = flip_model(jnp.stack([blocks[2], blocks[3]]), 2)
    near = flip_model(jnp.stack([blocks[1], far[1]]), 1)
    relative = jnp.stack([blocks[0], near[0], far[0], near[1]])
    return [pick(relative, own ^ j) for j in range(4)]


def sum_ctx(grad, ctx_index, to_rows, own):
    bits = ctx_bits()
    scatter = bits[:2]
    for bit in scatter:
        half = grad.shape[1] // 2
        side = (ctx_index // bit) % 2
        keep = lax.dynamic_slice_in_dim(grad, side * half, half, axis=1)
        send = lax.dynamic_slice_in_dim(grad, (1 - side) * half, half, axis=1)
        grad = keep + flip_ctx(send.astype(LOW), bit).astype(WIDE)
    for bit in bits[2:]:
        low = grad.astype(LOW)
        grad = low.astype(WIDE) + flip_ctx(low, bit).astype(WIDE)
    low = grad.astype(LOW)
    if to_rows:
        columns = to_columns([pick(low, own ^ k) for k in range(4)], own)
        low = jnp.stack(columns, axis=1)
        low = low.reshape(1, low.shape[0], -1)
    for bit in reversed(scatter):
        side = (ctx_index // bit) % 2
        other = flip_ctx(low, bit)
        first = jnp.where(side == 0, low, other)
        second = jnp.where(side == 0, other, low)
        low = jnp.concatenate([first, second], axis=1)
    return low[0].astype(WIDE)


def attend(queries, keys, values, allowed):
    heads = queries.shape[1] // HD
    outs = []
    probs = []
    for h in range(heads):
        cols = slice(h * HD, (h + 1) * HD)
        scores = mm_nt(queries[:, cols], keys[:, cols])
        scores = jnp.where(allowed, scores, FLOOR_SCORE)
        top = jnp.max(scores, axis=1, keepdims=True)
        weights = jnp.exp(scores - top)
        prob = weights / jnp.sum(weights, axis=1, keepdims=True)
        probs.append(prob)
        outs.append(mm(prob.astype(LOW), values[:, cols]))
    return jnp.concatenate(outs, axis=1).astype(LOW), probs


def attend_back(queries, keys, values, probs, grad):
    heads = queries.shape[1] // HD
    query_grads, key_grads, value_grads = [], [], []
    for h in range(heads):
        cols = slice(h * HD, (h + 1) * HD)
        prob = probs[h]
        prob_grad = mm_nt(grad[:, cols], values[:, cols])
        inner = jnp.sum(prob * prob_grad, axis=1, keepdims=True)
        score_grad = (prob * (prob_grad - inner)).astype(LOW)
        query_grads.append(mm(score_grad, keys[:, cols]))
        key_grads.append(mm_tn(score_grad, queries[:, cols]))
        value_grads.append(mm_tn(prob.astype(LOW), grad[:, cols]))
    return (
        jnp.concatenate(query_grads, axis=1),
        jnp.concatenate(key_grads + value_grads, axis=1),
    )


def sum_lines(value):
    for bit in reversed(line_bits()):
        mine = value[:bit]
        value = mine + flip_ctx(value[bit:].astype(LOW), bit).astype(WIDE)
    return value[0]


def body(
    hidden,
    encoded,
    cotangent,
    dec_seg,
    enc_seg,
    self_qkv,
    self_out,
    cross_q,
    cross_kv,
    cross_out,
    ffn_in,
    ffn_out,
    biases,
    gains,
    ffn_bias,
):
    tokens = hidden.shape[1]
    width = hidden.shape[2]
    sources = encoded.shape[1]
    model = lax.axis_size("fsdp")
    lines = lax.axis_size("ctx") // model
    own = lax.axis_index("fsdp")
    ctx_index = lax.axis_index("ctx")
    line = ctx_index % lines
    local = width // model
    scale = float(HD) ** (-0.5)
    rows = 4 * tokens
    half = 2 * tokens

    marks = jnp.concatenate([dec_seg[0], enc_seg[0]]).astype(LOW)
    marks = jnp.pad(marks, (0, width - tokens - sources))[None]
    block = jnp.concatenate([hidden[0], jnp.pad(marks, ((0, 15), (0, 0)))], axis=0)
    plane = gather_plane(swap_places(block))
    inputs = plane[..., :tokens, :].reshape(lines * rows, width)
    segments = plane[..., tokens, :tokens].reshape(lines * rows).astype(jnp.int32)
    source_segments = plane[..., tokens, tokens : tokens + sources].reshape(-1).astype(jnp.int32)
    source_rows = gather_plane(swap_places(encoded[0])).reshape(-1, width)
    out_grad = swap_places(cotangent[0])
    out_grad = jnp.concatenate([out_grad, flip_model(out_grad, 2)], axis=0).astype(WIDE)

    line_ids = line ^ jnp.arange(lines, dtype=jnp.int32)[:, None]
    model_ids = own ^ jnp.array([0, 2, 1, 3], jnp.int32)[None, :]
    starts = (model_ids * lines + line_ids) * tokens
    places = (starts[:, :, None] + jnp.arange(tokens, dtype=jnp.int32)).reshape(-1)

    qkv_low = self_qkv.astype(LOW).reshape(local, 3, model, local)
    cq_low = cross_q.astype(LOW).reshape(local, model, local)
    ckv_low = cross_kv.astype(LOW).reshape(local, 2, model, local)
    fi_low = ffn_in.astype(LOW).reshape(local, model, -1)

    def qkv_block(k):
        piece = lax.dynamic_index_in_dim(qkv_low, own ^ k, 2, keepdims=False)
        return piece.reshape(local, -1)

    def rest_block(k):
        piece_q = lax.dynamic_index_in_dim(cq_low, own ^ k, 1, keepdims=False)
        piece_kv = lax.dynamic_index_in_dim(ckv_low, own ^ k, 2, keepdims=False)
        piece_fi = lax.dynamic_index_in_dim(fi_low, own ^ k, 1, keepdims=False)
        return jnp.concatenate([piece_q, piece_kv.reshape(local, -1), piece_fi], axis=1)

    w_qkv = jnp.concatenate(to_columns([qkv_block(k) for k in range(4)], own), axis=0)
    w_rest = jnp.concatenate(to_columns([rest_block(k) for k in range(4)], own), axis=0)
    w_cq = w_rest[:, :local]
    w_ckv = w_rest[:, local : 3 * local]
    w_fi = w_rest[:, 3 * local :]
    w_so = self_out.astype(LOW)
    w_co = cross_out.astype(LOW)
    w_fo = ffn_out.astype(LOW)
    small = jnp.concatenate([biases, gains], axis=0).astype(LOW)
    small_all = lax.all_gather(small, "fsdp", axis=1, tiled=True).astype(WIDE)
    bias = small_all[:10]
    gain = small_all[10:]
    bias_own = biases.astype(LOW).astype(WIDE)
    inner_bias = ffn_bias.astype(LOW).astype(WIDE)

    queries = ((mm(inputs[:rows], w_qkv[:, :local]) + bias_own[3]) * scale).astype(LOW)
    pair = mm(inputs, w_qkv[:, local:])
    keys = pair[:, :local].astype(LOW)
    values = (pair[:, local:] + bias_own[4]).astype(LOW)
    allowed = (segments[:rows, None] == segments[None, :]) & (places[None, :] <= places[:rows, None])
    attended, self_probs = attend(queries, keys, values, allowed)
    residual = inputs[:half].astype(WIDE)
    first_sum = residual + tensor_sum(mm(attended, w_so)) + bias[5]
    first_normal, first_rate = normalize(first_sum)
    first = first_normal * gain[0] + bias[0]
    first_low = spread_rows(first.astype(LOW))

    cross_queries = ((mm(first_low, w_cq) + bias_own[6]) * scale).astype(LOW)
    source_pair = mm(source_rows, w_ckv)
    source_keys = source_pair[:, :local].astype(LOW)
    source_values = (source_pair[:, local:] + bias_own[7]).astype(LOW)
    cross_allowed = segments[:rows, None] == source_segments[None, :]
    crossed, cross_probs = attend(cross_queries, source_keys, source_values, cross_allowed)
    second_sum = first + tensor_sum(mm(crossed, w_co)) + bias[8]
    second_normal, second_rate = normalize(second_sum)
    second = second_normal * gain[1] + bias[1]
    second_low = spread_rows(second.astype(LOW))

    inner_pre = mm(second_low, w_fi) + inner_bias
    bell = 0.5 * (1.0 + lax.erf(inner_pre * (0.5**0.5)))
    activated = (inner_pre * bell).astype(LOW)
    third_sum = second + tensor_sum(mm(activated, w_fo)) + bias[9]
    third_normal, third_rate = normalize(third_sum)
    result = third_normal[:tokens] * gain[2] + bias[2]
    output = swap_places(result.astype(LOW))[None]

    third_grad = normalize_back(out_grad, third_normal, third_rate, gain[2])
    ffn_grad = spread_rows(third_grad.astype(LOW))
    slope = bell + inner_pre * jnp.exp(-0.5 * inner_pre * inner_pre) * 0.3989422804014327
    inner_grad = (mm_nt(ffn_grad, w_fo) * slope).astype(LOW)
    second_grad = third_grad + tensor_sum(mm_nt(inner_grad, w_fi))
    d_fo = mm_tn(activated, ffn_grad)
    d_fi = mm_tn(second_low, inner_grad)
    g_fo = sum_ctx(d_fo[None], ctx_index, False, own)
    g_fi = sum_ctx(d_fi.reshape(model, local, -1), ctx_index, True, own)

    sum_two_grad = normalize_back(second_grad, second_normal, second_rate, gain[1])
    cross_branch = spread_rows(sum_two_grad.astype(LOW))
    crossed_grad = mm_nt(cross_branch, w_co).astype(LOW)
    cross_query_grad, source_grad = attend_back(
        cross_queries, source_keys, source_values, cross_probs, crossed_grad
    )
    cross_query_pre = (cross_query_grad.astype(LOW).astype(WIDE) * scale).astype(LOW)
    first_grad = sum_two_grad + tensor_sum(mm_nt(cross_query_pre, w_cq))
    d_co = mm_tn(crossed, cross_branch)
    d_cq = mm_tn(first_low, cross_query_pre)
    source_low = source_grad.astype(LOW)
    d_ckv = mm_tn(source_rows, source_low)
    source_own = sum_lines(source_grad.reshape(lines, 4 * sources, 2 * local)).astype(LOW)
    encoded_part = mm_nt(source_own, w_ckv)
    encoded_part = encoded_part[: 2 * sources] + flip_model(
        encoded_part[2 * sources :].astype(LOW), 1
    ).astype(WIDE)
    encoded_part = encoded_part[:sources] + flip_model(
        encoded_part[sources:].astype(LOW), 2
    ).astype(WIDE)
    encoded_grad = swap_places(encoded_part.astype(LOW)).astype(WIDE)[None]

    sum_one_grad = normalize_back(first_grad, first_normal, first_rate, gain[0])
    self_branch = spread_rows(sum_one_grad.astype(LOW))
    attended_grad = mm_nt(self_branch, w_so).astype(LOW)
    self_query_grad, pair_grad = attend_back(queries, keys, values, self_probs, attended_grad)
    self_query_pre = (self_query_grad.astype(LOW).astype(WIDE) * scale).astype(LOW)
    d_so = mm_tn(attended, self_branch)
    pair_low = pair_grad.astype(LOW)
    d_q = mm_tn(inputs[:rows], self_query_pre)
    d_kv = mm_tn(inputs, pair_low)
    d_qkv = jnp.concatenate([d_q, d_kv], axis=1)
    pair_own = sum_lines(pair_grad.reshape(lines, rows, 2 * local)).astype(LOW)
    projected_grad = jnp.concatenate([self_query_pre, pair_own], axis=1)
    input_part = mm_nt(projected_grad, w_qkv)
    input_part = input_part[:half] + flip_model(input_part[half:].astype(LOW), 1).astype(WIDE)
    input_part = input_part[:tokens] + flip_model(input_part[tokens:].astype(LOW), 2).astype(WIDE)
    input_grad = sum_one_grad[:tokens] + input_part
    hidden_grad = swap_places(input_grad.astype(LOW)).astype(WIDE)[None]

    row_kinds = jnp.concatenate([d_so, d_co], axis=1)[None]
    g_row = sum_ctx(row_kinds, ctx_index, False, own)
    column_kinds = jnp.concatenate([d_cq, d_ckv], axis=1).reshape(model, local, -1)
    g_col = sum_ctx(column_kinds, ctx_index, True, own).reshape(local, model, 3, local)
    g_qkv = sum_ctx(d_qkv.reshape(model, local, -1), ctx_index, True, own)
    g_qkv = g_qkv.reshape(local, model, 3, local).transpose(0, 2, 1, 3).reshape(local, 3 * width)
    g_so = g_row[:, :width]
    g_co = g_row[:, width:]
    g_cq = g_col[:, :, 0].reshape(local, width)
    g_ckv = g_col[:, :, 1:].transpose(0, 2, 1, 3).reshape(local, 2 * width)

    def columns(value):
        return jnp.sum(value.astype(WIDE), axis=0)

    wide_rows = jnp.stack(
        [
            columns(first_grad[:tokens]),
            columns(second_grad[:tokens]),
            columns(out_grad[:tokens]),
            columns((first_grad * first_normal)[:tokens]),
            columns((second_grad * second_normal)[:tokens]),
            columns((out_grad * third_normal)[:tokens]),
            columns(self_branch[:tokens]),
            columns(cross_branch[:tokens]),
            columns(ffn_grad[:tokens]),
        ]
    )
    for bit in (1, 2):
        wide_rows = wide_rows + flip_model(wide_rows, bit)
    wide_rows = lax.dynamic_slice_in_dim(wide_rows, own * local, local, axis=1)
    own_rows = jnp.stack(
        [
            columns(self_query_pre),
            columns(pair_low[:, local:]),
            columns(cross_query_pre),
            columns(source_low[:, local:]),
        ]
    )
    vectors = jnp.concatenate([wide_rows, own_rows, columns(inner_grad).reshape(-1, local)], axis=0)
    for bit in ctx_bits():
        vectors = vectors + flip_ctx(vectors, bit)
    d_bias = jnp.stack([vectors[i] for i in (0, 1, 2, 9, 10, 6, 11, 12, 7, 8)])
    d_gain = vectors[3:6]
    d_inner = vectors[13:].reshape(-1)
    return (
        output,
        hidden_grad,
        encoded_grad,
        g_qkv,
        g_so,
        g_cq,
        g_ckv,
        g_co,
        g_fi.reshape(local, -1),
        g_fo,
        d_bias,
        d_gain,
        d_inner,
    )


def solution(mesh):
    whole = P("fsdp", "ctx", None)
    matrix = P("fsdp", None)
    ids = P("fsdp", "ctx")
    table = P(None, "fsdp")
    return jax.shard_map(
        body,
        mesh=mesh,
        in_specs=(whole, whole, whole, ids, ids) + (matrix,) * 7 + (table, table, P("fsdp")),
        out_specs=(whole,) * 3 + (matrix,) * 7 + (table, table, P("fsdp")),
        check_vma=False,
    )
```

time: 1120 us -> 500 us (0.45)
  blocking collectives: 491 us -> 16.2 us
  waiting for transfers between devices: 430 us -> 168 us
  starting transfers between devices: 5.66 us -> 102 us
  local copies, waits for them, and re-layouts: 50.3 us -> 103 us
  matrix products: 72.6 us -> 36.5 us
  other arithmetic: 50.8 us -> 64.7 us
  between operations: 17.2 us -> 4.4 us
    psum x1 -> x0, blocking collectives: 405 us -> none  [body(): lax.psum((g_qkv, g_so, g_cq, g_ckv, g_co, g_fi, g_fo, g_bias, g_gain, g_i...]
    all_gather x8 -> x0, waiting for transfers between devices: 143 us -> none  [the longest x1 37.7 us: body(): lax.all_gather(ffn_in.astype(jnp.bfloat16), 'fsdp', axis=0, tiled=True)]
    reduce_scatter x5 -> x0, waiting for transfers between devices: 99.4 us -> none  [the longest x1 50.5 us: body(): lax.psum_scatter(w_fo_grad.astype(jnp.bfloat16), 'fsdp', scatter_dimensio...]
    ppermute x16 -> x74, starting transfers between devices: 4.91 us -> 102 us  [the longest x36 50.3 us: flip_model(): return lax.ppermute(value, 'fsdp', [(i, i ^ bit) for i in range(count)])]
    unnamed x23 -> x0, waiting for transfers between devices: 60.8 us -> none
    all_gather x5 -> x1, blocking collectives: 72.5 us -> 16.2 us  [body(): small_all = lax.all_gather(small, 'fsdp', axis=1, tiled=True).astype(WIDE)]
    ppermute x16 -> x74, waiting for transfers between devices: 127 us -> 168 us  [the longest x32 120 us: flip_ctx(): return lax.ppermute(value, 'ctx', [(i, i ^ bit) for i in range(count)])]
    dot_general x69 -> x59, matrix products: 72.6 us -> 36.5 us  [the longest x20 13.3 us: mm_tn(): lax.dot_general(left, right, (((0,), (0,)), ((), ())), preferred_element_...]
  transfers between devices with their start and end apart: 34 -> 74, of which waited for: 19 -> 33; matrix products, arithmetic and copies ran while one was open for 13% -> 29% of each run, Pallas kernels for 0% -> 0%
where the time goes in v1:
time: 500 us; the launch traced here: 494 us
  waiting for transfers between devices  168 us (34%)
  local copies, waits for them, and re-layouts  103 us (21%)
  starting transfers between devices  102 us (20%)
  other arithmetic  64.7 us (13%)
  matrix products  36.5 us (7%)
  blocking collectives  16.2 us (3%)
    ppermute x32, waiting for transfers between devices, flip_ctx(): return lax.ppermute(value, 'ctx', [(i, i ^ bit) for i in range(count)])  120 us
    ppermute x36, starting transfers between devices, flip_model(): return lax.ppermute(value, 'fsdp', [(i, i ^ bit) for i in range(count)])  50.3 us
    ppermute x36, waiting for transfers between devices, flip_model(): return lax.ppermute(value, 'fsdp', [(i, i ^ bit) for i in range(count)])  48.4 us
    ppermute x32, starting transfers between devices, flip_ctx(): return lax.ppermute(value, 'ctx', [(i, i ^ bit) for i in range(count)])  41.1 us
    unnamed x402, local copies, waits for them, and re-layouts  21.5 us
    all_gather x1, blocking collectives, body(): small_all = lax.all_gather(small, 'fsdp', axis=1, tiled=True).astype(WIDE)  16.2 us
    dot_general x20, matrix products, mm_tn(): lax.dot_general(left, right, (((0,), (0,)), ((), ())), preferred_element_...  13.3 us
    dot_general x19, matrix products, mm_nt(): lax.dot_general(left, right, (((1,), (1,)), ((), ())), preferred_element_...  12.5 us
  transfers between devices with their start and end apart: 74, of which 33 were waited for; matrix products, arithmetic and copies ran while one was open for 29% of the time, Pallas kernels for 0%

profile of v1, /device:TPU:0, one launch (start us, length us, event | category | flops | bytes accessed | tf_op | source)
XLA Modules:
  0.0 493.9 jit_solution(4367275584509355000)
XLA Ops:
  3.3 2.4 constant_dynamic-slice_fusion.25
  8.7 2.9 collective-permute-start.4
  12.4 3.5 collective-permute-start
  19.1 3.4 constant_dynamic-slice_fusion.20
  23.4 6.5 %dynamic-slice_reduce_fusion.3 = (bf16[192,2,192]{2,1,0:T(2,128)(2,1)}, bf16[192,2,192]{2,1,0:T(2,128)(2,1)S(1)}, bf16[192,2,192]{2,1,0:T(2,128)(2,1)}, bf16[192,2,192]{2,1,0:T(2,128)(2,1)}) fusion(bf16[192,2,4,192]{3,2,1,0:T(4,128)(2,1)S(1)} %reshape.289, s32[]{:T(128)S(6)} %select_n.308, s32[]{:T(128)S(6)} %select_n.310, s32[]{:T(128)S(6)} %select_n.309, ...), kind=kLoop, calls=%fused_computation.267 | loop fusion | bytes 1179664 | tf_op jit(solution)/shard_map/jit(dynamic_index_in_dim)/dynamic_slice | solution.py:236
  40.4 2.5 collective-permute-start.9
  45.5 5.5 %collective-permute-start.12 = (bf16[32,768]{1,0:T(8,128)(2,1)}, bf16[32,768]{1,0:T(8,128)(2,1)}, u32[]{:S(2)}, u32[]{:S(2)}) collective-permute-start(bf16[32,768]{1,0:T(8,128)(2,1)} %collective-permute-done.11), channel_id=1, source_target_pairs={{0,16},{8,24},{16,0},{24,8},{1,17},{9,25},{17,1},{25,9},{2,18},{10... | collective-permute-start | bytes 147464 | tf_op jit(solution)/shard_map/ppermute | solution.py:28
  53.4 16.2 %all-gather = bf16[4,192,13]{1,2,0:T(8,128)(2,1)S(1)} all-gather(bf16[1,192,13]{1,2,0:T(8,128)(2,1)S(1)} %maximum_bitcast_fusion.5), channel_id=1, replica_groups=mesh['fsdp'=4,'ctx'=8] {'fsdp'}, dimensions={0}, use_global_device_ids=true | all-gather | bytes 24960 | tf_op jit(solution)/shard_map/all_gather | solution.py:249
  74.3 3.3 collective-permute-start.1
  87.6 8.8 %collective-permute-done.2 = bf16[1,2,144,768]{3,1,2,0:T(2,128)(2,1)S(1)} collective-permute-done((bf16[1,2,144,768]{3,1,2,0:T(2,128)(2,1)S(1)}, bf16[1,2,144,768]{3,1,2,0:T(2,128)(2,1)S(1)}, u32[]{:S(2)}, u32[]{:S(2)}) %collective-permute-start.2) | collective-permute-done | bytes 442400 | tf_op jit(solution)/shard_map/ppermute | solution.py:33
  99.4 2.5 fusion.209
  104.7 2.7 slice_maximum_fusion
  124.0 9.6 %collective-permute-done.7 = bf16[256,768]{1,0:T(8,128)(2,1)S(1)} collective-permute-done((bf16[256,768]{1,0:T(8,128)(2,1)S(1)}, bf16[256,768]{1,0:T(8,128)(2,1)S(1)}, u32[]{:S(2)}, u32[]{:S(2)}) %collective-permute-start.7) | collective-permute-done | bytes 393248 | tf_op jit(solution)/shard_map/ppermute | solution.py:28
  144.6 9.7 %collective-permute-done.16 = bf16[256,768]{1,0:T(8,128)(2,1)S(1)} collective-permute-done((bf16[256,768]{1,0:T(8,128)(2,1)S(1)}, bf16[256,768]{1,0:T(8,128)(2,1)S(1)}, u32[]{:S(2)}, u32[]{:S(2)}) %collective-permute-start.16) | collective-permute-done | bytes 393248 | tf_op jit(solution)/shard_map/ppermute | solution.py:28
  157.0 2.4 multiply_convert_fusion.3
  164.2 11.4 %collective-permute-start.22 = (bf16[128,768]{1,0:T(8,128)(2,1)S(1)}, bf16[128,768]{1,0:T(8,128)(2,1)S(1)}, u32[]{:S(2)}, u32[]{:S(2)}) collective-permute-start(bf16[128,768]{1,0:T(8,128)(2,1)S(1)} %collective-permute-done.21), channel_id=1, source_target_pairs={{0,16},{8,24},{16,0},{24,8},{1,17},{9,25},{17,1},{25,9},{2,18},{10... | collective-permute-start | bytes 589832 | tf_op jit(solution)/shard_map/ppermute | solution.py:28
  175.5 5.9 %collective-permute-done.22 = bf16[128,768]{1,0:T(8,128)(2,1)S(1)} collective-permute-done((bf16[128,768]{1,0:T(8,128)(2,1)S(1)}, bf16[128,768]{1,0:T(8,128)(2,1)S(1)}, u32[]{:S(2)}, u32[]{:S(2)}) %collective-permute-start.22) | collective-permute-done | bytes 196640 | tf_op jit(solution)/shard_map/ppermute | solution.py:28
  184.9 3.0 collective-permute-start.20
  191.4 3.6 convert_reduce_fusion
  200.0 2.3 fusion.61
  206.5 9.1 %collective-permute-start.25 = (bf16[256,768]{1,0:T(8,128)(2,1)S(1)}, bf16[256,768]{1,0:T(8,128)(2,1)S(1)}, u32[]{:S(2)}, u32[]{:S(2)}) collective-permute-start(bf16[256,768]{1,0:T(8,128)(2,1)S(1)} %fusion.67), channel_id=1, source_target_pairs={{0,16},{8,24},{16,0},{24,8},{1,17},{9,25},{17,1},{25,9},{2,18},{10... | collective-permute-start | bytes 1179656 | tf_op jit(solution)/shard_map/ppermute | solution.py:28
  215.6 3.0 collective-permute-done.64
  218.9 11.4 %collective-permute-done.57 = bf16[4,96,768]{2,1,0:T(8,128)(2,1)S(1)} collective-permute-done((bf16[4,96,768]{2,1,0:T(8,128)(2,1)S(1)}, bf16[4,96,768]{2,1,0:T(8,128)(2,1)S(1)}, u32[]{:S(2)}, u32[]{:S(2)}) %collective-permute-start.57) | collective-permute-done | bytes 589856 | tf_op jit(solution)/shard_map/ppermute | solution.py:33
  233.7 10.8 %collective-permute-start.66 = (bf16[1,192,768]{2,1,0:T(8,128)(2,1)S(1)}, bf16[1,192,768]{2,1,0:T(8,128)(2,1)S(1)}, u32[]{:S(2)}, u32[]{:S(2)}) collective-permute-start(bf16[1,192,768]{2,1,0:T(8,128)(2,1)S(1)} %add_convert_fusion.1), channel_id=1, source_target_pairs={{0,4},{1,5},{2,6},{3,7},{4,0},{5,1},{6,2},{7,3},{8,12},{9,13},{10,... | collective-permute-start | bytes 884744 | tf_op jit(solution)/shard_map/ppermute | solution.py:33
  244.6 5.5 %collective-permute-start.59 = (bf16[4,48,768]{2,1,0:T(8,128)(2,1)S(1)}, bf16[4,48,768]{2,1,0:T(8,128)(2,1)S(1)}, u32[]{:S(2)}, u32[]{:S(2)}) collective-permute-start(bf16[4,48,768]{2,1,0:T(8,128)(2,1)S(1)} %add_convert_fusion.3), channel_id=1, source_target_pairs={{0,4},{1,5},{2,6},{3,7},{4,0},{5,1},{6,2},{7,3},{8,12},{9,13},{10,... | collective-permute-start | bytes 884744 | tf_op jit(solution)/shard_map/ppermute | solution.py:33
  251.3 13.6 %collective-permute-done.66 = bf16[1,192,768]{2,1,0:T(8,128)(2,1)S(1)} collective-permute-done((bf16[1,192,768]{2,1,0:T(8,128)(2,1)S(1)}, bf16[1,192,768]{2,1,0:T(8,128)(2,1)S(1)}, u32[]{:S(2)}, u32[]{:S(2)}) %collective-permute-start.66) | collective-permute-done | bytes 294944 | tf_op jit(solution)/shard_map/ppermute | solution.py:33
  265.7 5.5 %collective-permute-done.59 = bf16[4,48,768]{2,1,0:T(8,128)(2,1)S(1)} collective-permute-done((bf16[4,48,768]{2,1,0:T(8,128)(2,1)S(1)}, bf16[4,48,768]{2,1,0:T(8,128)(2,1)S(1)}, u32[]{:S(2)}, u32[]{:S(2)}) %collective-permute-start.59) | collective-permute-done | bytes 294944 | tf_op jit(solution)/shard_map/ppermute | solution.py:33
  285.0 2.8 copy.182
  292.0 2.2 fusion.60
  295.0 11.0 %collective-permute-done.34 = bf16[1,128,384]{1,2,0:T(8,128)(2,1)S(1)} collective-permute-done((bf16[1,128,384]{1,2,0:T(8,128)(2,1)}, bf16[1,128,384]{1,2,0:T(8,128)(2,1)S(1)}, u32[]{:S(2)}, u32[]{:S(2)}) %collective-permute-start.34) | collective-permute-done | bytes 98336 | tf_op jit(solution)/shard_map/ppermute | solution.py:33
  308.8 3.1 collective-permute-done.36
  328.4 5.6 %collective-permute-done.28 = bf16[256,768]{1,0:T(8,128)(2,1)S(1)} collective-permute-done((bf16[256,768]{1,0:T(8,128)(2,1)S(1)}, bf16[256,768]{1,0:T(8,128)(2,1)S(1)}, u32[]{:S(2)}, u32[]{:S(2)}) %collective-permute-start.28) | collective-permute-done | bytes 393248 | tf_op jit(solution)/shard_map/ppermute | solution.py:28
  344.3 9.2 %collective-permute-done.52 = bf16[4,48,576]{2,1,0:T(8,128)(2,1)S(1)} collective-permute-done((bf16[4,48,576]{2,1,0:T(8,128)(2,1)S(1)}, bf16[4,48,576]{2,1,0:T(8,128)(2,1)S(1)}, u32[]{:S(2)}, u32[]{:S(2)}) %collective-permute-start.52) | collective-permute-done | bytes 221216 | tf_op jit(solution)/shard_map/ppermute | solution.py:33
  355.6 3.4 collective-permute-done.53
  386.0 2.4 collective-permute-done.72
  395.7 8.3 %collective-permute-done.45 = bf16[1,96,1536]{2,1,0:T(8,128)(2,1)} collective-permute-done((bf16[1,96,1536]{2,1,0:T(8,128)(2,1)}, bf16[1,96,1536]{2,1,0:T(8,128)(2,1)}, u32[]{:S(2)}, u32[]{:S(2)}) %collective-permute-start.45) | collective-permute-done | bytes 294944 | tf_op jit(solution)/shard_map/ppermute | solution.py:33
  405.2 6.6 %collective-permute-done.30 = bf16[1,512,384]{1,2,0:T(8,128)(2,1)} collective-permute-done((bf16[1,512,384]{1,2,0:T(8,128)(2,1)}, bf16[1,512,384]{1,2,0:T(8,128)(2,1)}, u32[]{:S(2)}, u32[]{:S(2)}) %collective-permute-start.30) | collective-permute-done | bytes 393248 | tf_op jit(solution)/shard_map/ppermute | solution.py:33
  417.9 5.9 %collective-permute-done.47 = bf16[1,48,1536]{2,1,0:T(8,128)(2,1)S(1)} collective-permute-done((bf16[1,48,1536]{2,1,0:T(8,128)(2,1)S(1)}, bf16[1,48,1536]{2,1,0:T(8,128)(2,1)S(1)}, u32[]{:S(2)}, u32[]{:S(2)}) %collective-permute-start.47) | collective-permute-done | bytes 147488 | tf_op jit(solution)/shard_map/ppermute | solution.py:33
  424.0 3.7 collective-permute-done.39
  427.9 2.6 collective-permute-done.48
  432.3 8.2 %collective-permute-done.40 = bf16[4,48,576]{2,1,0:T(8,128)(2,1)S(1)} collective-permute-done((bf16[4,48,576]{2,1,0:T(8,128)(2,1)S(1)}, bf16[4,48,576]{2,1,0:T(8,128)(2,1)S(1)}, u32[]{:S(2)}, u32[]{:S(2)}) %collective-permute-start.40) | collective-permute-done | bytes 221216 | tf_op jit(solution)/shard_map/ppermute | solution.py:33
  442.5 3.4 collective-permute-done.41
  451.2 6.7 %collective-permute-done.55 = bf16[1,48,2304]{2,1,0:T(8,128)(2,1)S(1)} collective-permute-done((bf16[1,48,2304]{2,1,0:T(8,128)(2,1)S(1)}, bf16[1,48,2304]{2,1,0:T(8,128)(2,1)S(1)}, u32[]{:S(2)}, u32[]{:S(2)}) %collective-permute-start.55) | collective-permute-done | bytes 221216 | tf_op jit(solution)/shard_map/ppermute | solution.py:33
  458.6 3.8 collective-permute-done.43
  464.5 6.7 %collective-permute-done.56 = bf16[1,96,2304]{2,1,0:T(8,128)(2,1)S(1)} collective-permute-done((bf16[1,96,2304]{2,1,0:T(8,128)(2,1)S(1)}, bf16[1,96,2304]{2,1,0:T(8,128)(2,1)S(1)}, u32[]{:S(2)}, u32[]{:S(2)}) %collective-permute-start.56) | collective-permute-done | bytes 442400 | tf_op jit(solution)/shard_map/ppermute | solution.py:33
  478.0 2.3 reshape.302
  485.8 2.6 copy.181
  488.4 3.7 reshape.311
  (823 shorter events, 218.1 us)
Async XLA Ops:
  8.7 68.8 %collective-permute-start.4 = (bf16[2,192,576]{2,1,0:T(8,128)(2,1)}, bf16[2,192,576]{2,1,0:T(8,128)(2,1)}, u32[]{:S(2)}, u32[]{:S(2)}) collective-permute-start(bf16[2,192,576]{2,1,0:T(8,128)(2,1)} %copy.166), channel_id=1, source_target_pairs={{0,16},{8,24},{16,0},{24,8},{1,17},{9,25},{17,1},{25,9},{2,18},{10... | collective-permute-start | bytes 1327112 | tf_op jit(solution)/shard_map/ppermute | solution.py:28
  12.4 61.9 %collective-permute-start = (bf16[144,768]{1,0:T(8,128)(2,1)}, bf16[144,768]{1,0:T(8,128)(2,1)}, u32[]{:S(2)}, u32[]{:S(2)}) collective-permute-start(bf16[144,768]{1,0:T(8,128)(2,1)} %fusion.90), channel_id=1, source_target_pairs={{0,0},{1,1},{2,8},{3,9},{4,16},{5,17},{6,24},{7,25},{8,2},{9,3},{1... | collective-permute-start | bytes 663560 | tf_op jit(solution)/shard_map/ppermute | solution.py:45
  40.4 59.1 %collective-permute-start.9 = (bf16[2,192,1344]{2,1,0:T(8,128)(2,1)}, bf16[2,192,1344]{2,1,0:T(8,128)(2,1)}, u32[]{:S(2)}, u32[]{:S(2)}) collective-permute-start(bf16[2,192,1344]{2,1,0:T(8,128)(2,1)} %pad_maximum_fusion.7), channel_id=1, source_target_pairs={{0,16},{8,24},{16,0},{24,8},{1,17},{9,25},{17,1},{25,9},{2,18},{10... | collective-permute-start | bytes 3096584 | tf_op jit(solution)/shard_map/ppermute | solution.py:28
  45.5 26.3 %collective-permute-start.12 = (bf16[32,768]{1,0:T(8,128)(2,1)}, bf16[32,768]{1,0:T(8,128)(2,1)}, u32[]{:S(2)}, u32[]{:S(2)}) collective-permute-start(bf16[32,768]{1,0:T(8,128)(2,1)} %collective-permute-done.11), channel_id=1, source_target_pairs={{0,16},{8,24},{16,0},{24,8},{1,17},{9,25},{17,1},{25,9},{2,18},{10... | collective-permute-start | bytes 147464 | tf_op jit(solution)/shard_map/ppermute | solution.py:28
  74.3 9.1 %collective-permute-start.1 = (bf16[144,768]{1,0:T(8,128)(2,1)}, bf16[144,768]{1,0:T(8,128)(2,1)S(1)}, u32[]{:S(2)}, u32[]{:S(2)}) collective-permute-start(bf16[144,768]{1,0:T(8,128)(2,1)} %collective-permute-done), channel_id=1, source_target_pairs={{0,16},{8,24},{16,0},{24,8},{1,17},{9,25},{17,1},{25,9},{2,18},{10... | collective-permute-start | bytes 663560 | tf_op jit(solution)/shard_map/ppermute | solution.py:28
  84.7 11.7 %collective-permute-start.2 = (bf16[1,2,144,768]{3,1,2,0:T(2,128)(2,1)S(1)}, bf16[1,2,144,768]{3,1,2,0:T(2,128)(2,1)S(1)}, u32[]{:S(2)}, u32[]{:S(2)}) collective-permute-start(bf16[1,2,144,768]{3,1,2,0:T(2,128)(2,1)S(1)} %maximum_bitcast_fusion.3), channel_id=1, source_target_pairs={{0,1},{1,0},{2,3},{3,2},{4,5},{5,4},{6,7},{7,6},{8,9},{9,8},{10,11... | collective-permute-start | bytes 1327112 | tf_op jit(solution)/shard_map/ppermute | solution.py:33
  103.0 16.0 %collective-permute-start.10 = (bf16[2,192,1344]{2,1,0:T(8,128)(2,1)}, bf16[2,192,1344]{2,1,0:T(8,128)(2,1)}, u32[]{:S(2)}, u32[]{:S(2)}) collective-permute-start(bf16[2,192,1344]{2,1,0:T(8,128)(2,1)} %pad_maximum_fusion.8), channel_id=1, source_target_pairs={{0,8},{8,0},{16,24},{24,16},{1,9},{9,1},{17,25},{25,17},{2,10},{10... | collective-permute-start | bytes 3096584 | tf_op jit(solution)/shard_map/ppermute | solution.py:28
  122.0 11.6 %collective-permute-start.7 = (bf16[256,768]{1,0:T(8,128)(2,1)S(1)}, bf16[256,768]{1,0:T(8,128)(2,1)S(1)}, u32[]{:S(2)}, u32[]{:S(2)}) collective-permute-start(bf16[256,768]{1,0:T(8,128)(2,1)S(1)} %fusion.64), channel_id=1, source_target_pairs={{0,16},{8,24},{16,0},{24,8},{1,17},{9,25},{17,1},{25,9},{2,18},{10... | collective-permute-start | bytes 1179656 | tf_op jit(solution)/shard_map/ppermute | solution.py:28
  143.1 11.2 %collective-permute-start.16 = (bf16[256,768]{1,0:T(8,128)(2,1)S(1)}, bf16[256,768]{1,0:T(8,128)(2,1)S(1)}, u32[]{:S(2)}, u32[]{:S(2)}) collective-permute-start(bf16[256,768]{1,0:T(8,128)(2,1)S(1)} %fusion.65), channel_id=1, source_target_pairs={{0,16},{8,24},{16,0},{24,8},{1,17},{9,25},{17,1},{25,9},{2,18},{10... | collective-permute-start | bytes 1179656 | tf_op jit(solution)/shard_map/ppermute | solution.py:28
  162.2 19.4 %collective-permute-start.19 = (bf16[256,768]{1,0:T(8,128)(2,1)S(1)}, bf16[256,768]{1,0:T(8,128)(2,1)S(1)}, u32[]{:S(2)}, u32[]{:S(2)}) collective-permute-start(bf16[256,768]{1,0:T(8,128)(2,1)S(1)} %fusion.66), channel_id=1, source_target_pairs={{0,16},{8,24},{16,0},{24,8},{1,17},{9,25},{17,1},{25,9},{2,18},{10... | collective-permute-start | bytes 1179656 | tf_op jit(solution)/shard_map/ppermute | solution.py:28
  164.2 17.3 %collective-permute-start.22 = (bf16[128,768]{1,0:T(8,128)(2,1)S(1)}, bf16[128,768]{1,0:T(8,128)(2,1)S(1)}, u32[]{:S(2)}, u32[]{:S(2)}) collective-permute-start(bf16[128,768]{1,0:T(8,128)(2,1)S(1)} %collective-permute-done.21), channel_id=1, source_target_pairs={{0,16},{8,24},{16,0},{24,8},{1,17},{9,25},{17,1},{25,9},{2,18},{10... | collective-permute-start | bytes 589832 | tf_op jit(solution)/shard_map/ppermute | solution.py:28
  183.6 7.8 %collective-permute-start.23 = (bf16[256,768]{1,0:T(8,128)(2,1)}, bf16[256,768]{1,0:T(8,128)(2,1)}, u32[]{:S(2)}, u32[]{:S(2)}) collective-permute-start(bf16[256,768]{1,0:T(8,128)(2,1)} %fusion.189), channel_id=1, source_target_pairs={{0,8},{8,0},{16,24},{24,16},{1,9},{9,1},{17,25},{25,17},{2,10},{10... | collective-permute-start | bytes 1179656 | tf_op jit(solution)/shard_map/ppermute | solution.py:28
  202.3 16.3 %collective-permute-start.64 = (bf16[1,384,768]{2,1,0:T(8,128)(2,1)S(1)}, bf16[1,384,768]{2,1,0:T(8,128)(2,1)S(1)}, u32[]{:S(2)}, u32[]{:S(2)}) collective-permute-start(bf16[1,384,768]{2,1,0:T(8,128)(2,1)S(1)} %fusion.32), channel_id=1, source_target_pairs={{0,1},{1,0},{2,3},{3,2},{4,5},{5,4},{6,7},{7,6},{8,9},{9,8},{10,11... | collective-permute-start | bytes 1769480 | tf_op jit(solution)/shard_map/ppermute | solution.py:33
  203.8 26.5 %collective-permute-start.57 = (bf16[4,96,768]{2,1,0:T(8,128)(2,1)S(1)}, bf16[4,96,768]{2,1,0:T(8,128)(2,1)S(1)}, u32[]{:S(2)}, u32[]{:S(2)}) collective-permute-start(bf16[4,96,768]{2,1,0:T(8,128)(2,1)S(1)} %dynamic-slice_convert_fusion.1), channel_id=1, source_target_pairs={{0,1},{1,0},{2,3},{3,2},{4,5},{5,4},{6,7},{7,6},{8,9},{9,8},{10,11... | collective-permute-start | bytes 1769480 | tf_op jit(solution)/shard_map/ppermute | solution.py:33
  206.5 24.5 %collective-permute-start.25 = (bf16[256,768]{1,0:T(8,128)(2,1)S(1)}, bf16[256,768]{1,0:T(8,128)(2,1)S(1)}, u32[]{:S(2)}, u32[]{:S(2)}) collective-permute-start(bf16[256,768]{1,0:T(8,128)(2,1)S(1)} %fusion.67), channel_id=1, source_target_pairs={{0,16},{8,24},{16,0},{24,8},{1,17},{9,25},{17,1},{25,9},{2,18},{10... | collective-permute-start | bytes 1179656 | tf_op jit(solution)/shard_map/ppermute | solution.py:28
  218.8 14.8 %collective-permute-start.65 = (bf16[1,192,768]{2,1,0:T(8,128)(2,1)S(1)}, bf16[1,192,768]{2,1,0:T(8,128)(2,1)S(1)}, u32[]{:S(2)}, u32[]{:S(2)}) collective-permute-start(bf16[1,192,768]{2,1,0:T(8,128)(2,1)S(1)} %dynamic-slice_convert_fusion.4), channel_id=1, source_target_pairs={{0,2},{1,3},{2,0},{3,1},{4,6},{5,7},{6,4},{7,5},{8,10},{9,11},{10,... | collective-permute-start | bytes 884744 | tf_op jit(solution)/shard_map/ppermute | solution.py:33
  230.5 14.0 %collective-permute-start.58 = (bf16[4,48,768]{2,1,0:T(8,128)(2,1)S(1)}, bf16[4,48,768]{2,1,0:T(8,128)(2,1)S(1)}, u32[]{:S(2)}, u32[]{:S(2)}) collective-permute-start(bf16[4,48,768]{2,1,0:T(8,128)(2,1)S(1)} %dynamic-slice_convert_fusion.5), channel_id=1, source_target_pairs={{0,2},{1,3},{2,0},{3,1},{4,6},{5,7},{6,4},{7,5},{8,10},{9,11},{10,... | collective-permute-start | bytes 884744 | tf_op jit(solution)/shard_map/ppermute | solution.py:33
  233.5 40.3 %collective-permute-start.26 = (bf16[256,768]{1,0:T(8,128)(2,1)S(1)}, bf16[256,768]{1,0:T(8,128)(2,1)S(1)}, u32[]{:S(2)}, u32[]{:S(2)}) collective-permute-start(bf16[256,768]{1,0:T(8,128)(2,1)S(1)} %fusion.190), channel_id=1, source_target_pairs={{0,8},{8,0},{16,24},{24,16},{1,9},{9,1},{17,25},{25,17},{2,10},{10... | collective-permute-start | bytes 1179656 | tf_op jit(solution)/shard_map/ppermute | solution.py:28
  233.7 31.2 %collective-permute-start.66 = (bf16[1,192,768]{2,1,0:T(8,128)(2,1)S(1)}, bf16[1,192,768]{2,1,0:T(8,128)(2,1)S(1)}, u32[]{:S(2)}, u32[]{:S(2)}) collective-permute-start(bf16[1,192,768]{2,1,0:T(8,128)(2,1)S(1)} %add_convert_fusion.1), channel_id=1, source_target_pairs={{0,4},{1,5},{2,6},{3,7},{4,0},{5,1},{6,2},{7,3},{8,12},{9,13},{10,... | collective-permute-start | bytes 884744 | tf_op jit(solution)/shard_map/ppermute | solution.py:33
  244.6 26.6 %collective-permute-start.59 = (bf16[4,48,768]{2,1,0:T(8,128)(2,1)S(1)}, bf16[4,48,768]{2,1,0:T(8,128)(2,1)S(1)}, u32[]{:S(2)}, u32[]{:S(2)}) collective-permute-start(bf16[4,48,768]{2,1,0:T(8,128)(2,1)S(1)} %add_convert_fusion.3), channel_id=1, source_target_pairs={{0,4},{1,5},{2,6},{3,7},{4,0},{5,1},{6,2},{7,3},{8,12},{9,13},{10,... | collective-permute-start | bytes 884744 | tf_op jit(solution)/shard_map/ppermute | solution.py:33
  265.7 47.3 %collective-permute-start.67 = (bf16[1,192,768]{2,1,0:T(8,128)(2,1)}, bf16[1,192,768]{2,1,0:T(8,128)(2,1)}, u32[]{:S(2)}, u32[]{:S(2)}) collective-permute-start(bf16[1,192,768]{2,1,0:T(8,128)(2,1)} %add_convert_fusion), channel_id=1, source_target_pairs={{0,2},{1,3},{2,0},{3,1},{4,6},{5,7},{6,4},{7,5},{8,10},{9,11},{10,... | collective-permute-start | bytes 884744 | tf_op jit(solution)/shard_map/ppermute | solution.py:33
  272.7 33.7 %collective-permute-start.60 = (bf16[2,48,768]{2,1,0:T(8,128)(2,1)}, bf16[2,48,768]{2,1,0:T(8,128)(2,1)}, u32[]{:S(2)}, u32[]{:S(2)}) collective-permute-start(bf16[2,48,768]{2,1,0:T(8,128)(2,1)} %pad_maximum_fusion.45), channel_id=1, source_target_pairs={{0,16},{8,24},{16,0},{24,8},{1,17},{9,25},{17,1},{25,9},{2,18},{10... | collective-permute-start | bytes 442376 | tf_op jit(solution)/shard_map/ppermute | solution.py:28
  283.3 37.6 %collective-permute-start.27 = (bf16[256,768]{1,0:T(8,128)(2,1)}, bf16[256,768]{1,0:T(8,128)(2,1)}, u32[]{:S(2)}, u32[]{:S(2)}) collective-permute-start(bf16[256,768]{1,0:T(8,128)(2,1)} %slice.939), channel_id=1, source_target_pairs={{0,8},{8,0},{16,24},{24,16},{1,9},{9,1},{17,25},{25,17},{2,10},{10... | collective-permute-start | bytes 1179656 | tf_op jit(solution)/shard_map/ppermute | solution.py:28
  290.0 32.7 %collective-permute-start.50 = (bf16[4,96,576]{2,1,0:T(8,128)(2,1)}, bf16[4,96,576]{2,1,0:T(8,128)(2,1)}, u32[]{:S(2)}, u32[]{:S(2)}) collective-permute-start(bf16[4,96,576]{2,1,0:T(8,128)(2,1)} %dynamic-slice_convert_fusion.2), channel_id=1, source_target_pairs={{0,1},{1,0},{2,3},{3,2},{4,5},{5,4},{6,7},{7,6},{8,9},{9,8},{10,11... | collective-permute-start | bytes 1327112 | tf_op jit(solution)/shard_map/ppermute | solution.py:33
  290.5 15.4 %collective-permute-start.34 = (bf16[1,128,384]{1,2,0:T(8,128)(2,1)}, bf16[1,128,384]{1,2,0:T(8,128)(2,1)S(1)}, u32[]{:S(2)}, u32[]{:S(2)}) collective-permute-start(bf16[1,128,384]{1,2,0:T(8,128)(2,1)} %slice_bitcast_fusion.4), channel_id=1, source_target_pairs={{0,1},{1,0},{2,3},{3,2},{4,5},{5,4},{6,7},{7,6},{8,9},{9,8},{10,11... | collective-permute-start | bytes 294920 | tf_op jit(solution)/shard_map/ppermute | solution.py:33
  311.9 8.4 %collective-permute-start.37 = (bf16[32,768]{1,0:T(8,128)(2,1)S(1)}, bf16[32,768]{1,0:T(8,128)(2,1)S(1)}, u32[]{:S(2)}, u32[]{:S(2)}) collective-permute-start(bf16[32,768]{1,0:T(8,128)(2,1)S(1)} %fusion.123), channel_id=1, source_target_pairs={{0,0},{1,1},{2,8},{3,9},{4,16},{5,17},{6,24},{7,25},{8,2},{9,3},{1... | collective-permute-start | bytes 147464 | tf_op jit(solution)/shard_map/ppermute | solution.py:45
  315.0 39.3 %collective-permute-start.68 = (bf16[1,384,768]{2,1,0:T(8,128)(2,1)}, bf16[1,384,768]{2,1,0:T(8,128)(2,1)}, u32[]{:S(2)}, u32[]{:S(2)}) collective-permute-start(bf16[1,384,768]{2,1,0:T(8,128)(2,1)} %pad_maximum_fusion.19), channel_id=1, source_target_pairs={{0,1},{1,0},{2,3},{3,2},{4,5},{5,4},{6,7},{7,6},{8,9},{9,8},{10,11... | collective-permute-start | bytes 1769480 | tf_op jit(solution)/shard_map/ppermute | solution.py:33
  318.4 9.1 %collective-permute-start.62 = (bf16[1,48,3072]{2,1,0:T(8,128)(2,1)}, bf16[1,48,3072]{2,1,0:T(8,128)(2,1)S(1)}, u32[]{:S(2)}, u32[]{:S(2)}) collective-permute-start(bf16[1,48,3072]{2,1,0:T(8,128)(2,1)} %reshape.304), channel_id=1, source_target_pairs={{0,2},{1,3},{2,0},{3,1},{4,6},{5,7},{6,4},{7,5},{8,10},{9,11},{10,... | collective-permute-start | bytes 884744 | tf_op jit(solution)/shard_map/ppermute | solution.py:33
  322.3 11.7 %collective-permute-start.28 = (bf16[256,768]{1,0:T(8,128)(2,1)S(1)}, bf16[256,768]{1,0:T(8,128)(2,1)S(1)}, u32[]{:S(2)}, u32[]{:S(2)}) collective-permute-start(bf16[256,768]{1,0:T(8,128)(2,1)S(1)} %fusion.68), channel_id=1, source_target_pairs={{0,16},{8,24},{16,0},{24,8},{1,17},{9,25},{17,1},{25,9},{2,18},{10... | collective-permute-start | bytes 1179656 | tf_op jit(solution)/shard_map/ppermute | solution.py:28
  324.9 12.9 %collective-permute-start.51 = (bf16[4,48,576]{2,1,0:T(8,128)(2,1)}, bf16[4,48,576]{2,1,0:T(8,128)(2,1)}, u32[]{:S(2)}, u32[]{:S(2)}) collective-permute-start(bf16[4,48,576]{2,1,0:T(8,128)(2,1)} %dynamic-slice_convert_fusion.6), channel_id=1, source_target_pairs={{0,2},{1,3},{2,0},{3,1},{4,6},{5,7},{6,4},{7,5},{8,10},{9,11},{10,... | collective-permute-start | bytes 663560 | tf_op jit(solution)/shard_map/ppermute | solution.py:33
  339.1 14.4 %collective-permute-start.52 = (bf16[4,48,576]{2,1,0:T(8,128)(2,1)S(1)}, bf16[4,48,576]{2,1,0:T(8,128)(2,1)S(1)}, u32[]{:S(2)}, u32[]{:S(2)}) collective-permute-start(bf16[4,48,576]{2,1,0:T(8,128)(2,1)S(1)} %add_convert_fusion.5), channel_id=1, source_target_pairs={{0,4},{1,5},{2,6},{3,7},{4,0},{5,1},{6,2},{7,3},{8,12},{9,13},{10,... | collective-permute-start | bytes 663560 | tf_op jit(solution)/shard_map/ppermute | solution.py:33
  341.9 18.9 %collective-permute-start.63 = (bf16[1,96,3072]{2,1,0:T(8,128)(2,1)S(1)}, bf16[1,96,3072]{2,1,0:T(8,128)(2,1)S(1)}, u32[]{:S(2)}, u32[]{:S(2)}) collective-permute-start(bf16[1,96,3072]{2,1,0:T(8,128)(2,1)S(1)} %pad_maximum_fusion.18), channel_id=1, source_target_pairs={{0,1},{1,0},{2,3},{3,2},{4,5},{5,4},{6,7},{7,6},{8,9},{9,8},{10,11... | collective-permute-start | bytes 1769480 | tf_op jit(solution)/shard_map/ppermute | solution.py:33
  343.5 19.2 %collective-permute-start.29 = (bf16[256,768]{1,0:T(8,128)(2,1)S(1)}, bf16[256,768]{1,0:T(8,128)(2,1)S(1)}, u32[]{:S(2)}, u32[]{:S(2)}) collective-permute-start(bf16[256,768]{1,0:T(8,128)(2,1)S(1)} %copy-done.81), channel_id=1, source_target_pairs={{0,8},{8,0},{16,24},{24,16},{1,9},{9,1},{17,25},{25,17},{2,10},{10... | collective-permute-start | bytes 1179656 | tf_op jit(solution)/shard_map/ppermute | solution.py:28
  383.4 30.8 %collective-permute-start.38 = (bf16[4,96,576]{2,1,0:T(8,128)(2,1)}, bf16[4,96,576]{2,1,0:T(8,128)(2,1)}, u32[]{:S(2)}, u32[]{:S(2)}) collective-permute-start(bf16[4,96,576]{2,1,0:T(8,128)(2,1)} %dynamic-slice_convert_fusion.3), channel_id=1, source_target_pairs={{0,1},{1,0},{2,3},{3,2},{4,5},{5,4},{6,7},{7,6},{8,9},{9,8},{10,11... | collective-permute-start | bytes 1327112 | tf_op jit(solution)/shard_map/ppermute | solution.py:33
  389.7 14.4 %collective-permute-start.45 = (bf16[1,96,1536]{2,1,0:T(8,128)(2,1)}, bf16[1,96,1536]{2,1,0:T(8,128)(2,1)}, u32[]{:S(2)}, u32[]{:S(2)}) collective-permute-start(bf16[1,96,1536]{2,1,0:T(8,128)(2,1)} %fusion.81), channel_id=1, source_target_pairs={{0,1},{1,0},{2,3},{3,2},{4,5},{5,4},{6,7},{7,6},{8,9},{9,8},{10,11... | collective-permute-start | bytes 884744 | tf_op jit(solution)/shard_map/ppermute | solution.py:33
  391.2 20.6 %collective-permute-start.30 = (bf16[1,512,384]{1,2,0:T(8,128)(2,1)}, bf16[1,512,384]{1,2,0:T(8,128)(2,1)}, u32[]{:S(2)}, u32[]{:S(2)}) collective-permute-start(bf16[1,512,384]{1,2,0:T(8,128)(2,1)} %slice_bitcast_fusion.2), channel_id=1, source_target_pairs={{0,1},{1,0},{2,3},{3,2},{4,5},{5,4},{6,7},{7,6},{8,9},{9,8},{10,11... | collective-permute-start | bytes 1179656 | tf_op jit(solution)/shard_map/ppermute | solution.py:33
  405.1 8.9 %collective-permute-start.46 = (bf16[1,48,1536]{2,1,0:T(8,128)(2,1)S(1)}, bf16[1,48,1536]{2,1,0:T(8,128)(2,1)S(1)}, u32[]{:S(2)}, u32[]{:S(2)}) collective-permute-start(bf16[1,48,1536]{2,1,0:T(8,128)(2,1)S(1)} %dynamic-slice_convert_fusion.8), channel_id=1, source_target_pairs={{0,2},{1,3},{2,0},{3,1},{4,6},{5,7},{6,4},{7,5},{8,10},{9,11},{10,... | collective-permute-start | bytes 442376 | tf_op jit(solution)/shard_map/ppermute | solution.py:33
  414.0 17.2 %collective-permute-start.31 = (bf16[256,768]{1,0:T(8,128)(2,1)S(1)}, bf16[256,768]{1,0:T(8,128)(2,1)S(1)}, u32[]{:S(2)}, u32[]{:S(2)}) collective-permute-start(bf16[256,768]{1,0:T(8,128)(2,1)S(1)} %slice.938), channel_id=1, source_target_pairs={{0,8},{8,0},{16,24},{24,16},{1,9},{9,1},{17,25},{25,17},{2,10},{10... | collective-permute-start | bytes 1179656 | tf_op jit(solution)/shard_map/ppermute | solution.py:28
  414.1 9.8 %collective-permute-start.47 = (bf16[1,48,1536]{2,1,0:T(8,128)(2,1)S(1)}, bf16[1,48,1536]{2,1,0:T(8,128)(2,1)S(1)}, u32[]{:S(2)}, u32[]{:S(2)}) collective-permute-start(bf16[1,48,1536]{2,1,0:T(8,128)(2,1)S(1)} %add_convert_fusion.10), channel_id=1, source_target_pairs={{0,4},{1,5},{2,6},{3,7},{4,0},{5,1},{6,2},{7,3},{8,12},{9,13},{10,... | collective-permute-start | bytes 442376 | tf_op jit(solution)/shard_map/ppermute | solution.py:33
  415.7 12.0 %collective-permute-start.39 = (bf16[4,48,576]{2,1,0:T(8,128)(2,1)S(1)}, bf16[4,48,576]{2,1,0:T(8,128)(2,1)S(1)}, u32[]{:S(2)}, u32[]{:S(2)}) collective-permute-start(bf16[4,48,576]{2,1,0:T(8,128)(2,1)S(1)} %dynamic-slice_convert_fusion.7), channel_id=1, source_target_pairs={{0,2},{1,3},{2,0},{3,1},{4,6},{5,7},{6,4},{7,5},{8,10},{9,11},{10,... | collective-permute-start | bytes 663560 | tf_op jit(solution)/shard_map/ppermute | solution.py:33
  427.8 12.7 %collective-permute-start.40 = (bf16[4,48,576]{2,1,0:T(8,128)(2,1)S(1)}, bf16[4,48,576]{2,1,0:T(8,128)(2,1)S(1)}, u32[]{:S(2)}, u32[]{:S(2)}) collective-permute-start(bf16[4,48,576]{2,1,0:T(8,128)(2,1)S(1)} %add_convert_fusion.7), channel_id=1, source_target_pairs={{0,4},{1,5},{2,6},{3,7},{4,0},{5,1},{6,2},{7,3},{8,12},{9,13},{10,... | collective-permute-start | bytes 663560 | tf_op jit(solution)/shard_map/ppermute | solution.py:33
  430.6 15.5 %collective-permute-start.49 = (bf16[1,96,1536]{2,1,0:T(8,128)(2,1)S(1)}, bf16[1,96,1536]{2,1,0:T(8,128)(2,1)S(1)}, u32[]{:S(2)}, u32[]{:S(2)}) collective-permute-start(bf16[1,96,1536]{2,1,0:T(8,128)(2,1)S(1)} %pad_maximum_fusion.35), channel_id=1, source_target_pairs={{0,1},{1,0},{2,3},{3,2},{4,5},{5,4},{6,7},{7,6},{8,9},{9,8},{10,11... | collective-permute-start | bytes 884744 | tf_op jit(solution)/shard_map/ppermute | solution.py:33
  431.2 10.6 %collective-permute-start.32 = (bf16[128,768]{1,0:T(8,128)(2,1)S(1)}, bf16[128,768]{1,0:T(8,128)(2,1)S(1)}, u32[]{:S(2)}, u32[]{:S(2)}) collective-permute-start(bf16[128,768]{1,0:T(8,128)(2,1)S(1)} %slice.944), channel_id=1, source_target_pairs={{0,16},{8,24},{16,0},{24,8},{1,17},{9,25},{17,1},{25,9},{2,18},{10... | collective-permute-start | bytes 589832 | tf_op jit(solution)/shard_map/ppermute | solution.py:28
  441.8 8.6 %collective-permute-start.33 = (bf16[128,768]{1,0:T(8,128)(2,1)S(1)}, bf16[128,768]{1,0:T(8,128)(2,1)S(1)}, u32[]{:S(2)}, u32[]{:S(2)}) collective-permute-start(bf16[128,768]{1,0:T(8,128)(2,1)S(1)} %fusion.80), channel_id=1, source_target_pairs={{0,0},{1,1},{2,8},{3,9},{4,16},{5,17},{6,24},{7,25},{8,2},{9,3},{1... | collective-permute-start | bytes 589832 | tf_op jit(solution)/shard_map/ppermute | solution.py:45
  447.9 10.1 %collective-permute-start.55 = (bf16[1,48,2304]{2,1,0:T(8,128)(2,1)S(1)}, bf16[1,48,2304]{2,1,0:T(8,128)(2,1)S(1)}, u32[]{:S(2)}, u32[]{:S(2)}) collective-permute-start(bf16[1,48,2304]{2,1,0:T(8,128)(2,1)S(1)} %reshape.301), channel_id=1, source_target_pairs={{0,2},{1,3},{2,0},{3,1},{4,6},{5,7},{6,4},{7,5},{8,10},{9,11},{10,... | collective-permute-start | bytes 663560 | tf_op jit(solution)/shard_map/ppermute | solution.py:33
  448.4 14.1 %collective-permute-start.43 = (bf16[1,48,2304]{2,1,0:T(8,128)(2,1)S(1)}, bf16[1,48,2304]{2,1,0:T(8,128)(2,1)S(1)}, u32[]{:S(2)}, u32[]{:S(2)}) collective-permute-start(bf16[1,48,2304]{2,1,0:T(8,128)(2,1)S(1)} %reshape.297), channel_id=1, source_target_pairs={{0,2},{1,3},{2,0},{3,1},{4,6},{5,7},{6,4},{7,5},{8,10},{9,11},{10,... | collective-permute-start | bytes 663560 | tf_op jit(solution)/shard_map/ppermute | solution.py:33
  458.1 13.1 %collective-permute-start.56 = (bf16[1,96,2304]{2,1,0:T(8,128)(2,1)S(1)}, bf16[1,96,2304]{2,1,0:T(8,128)(2,1)S(1)}, u32[]{:S(2)}, u32[]{:S(2)}) collective-permute-start(bf16[1,96,2304]{2,1,0:T(8,128)(2,1)S(1)} %pad_maximum_fusion.31), channel_id=1, source_target_pairs={{0,1},{1,0},{2,3},{3,2},{4,5},{5,4},{6,7},{7,6},{8,9},{9,8},{10,11... | collective-permute-start | bytes 1327112 | tf_op jit(solution)/shard_map/ppermute | solution.py:33
  464.0 17.3 %collective-permute-start.44 = (bf16[1,96,2304]{2,1,0:T(8,128)(2,1)}, bf16[1,96,2304]{2,1,0:T(8,128)(2,1)}, u32[]{:S(2)}, u32[]{:S(2)}) collective-permute-start(bf16[1,96,2304]{2,1,0:T(8,128)(2,1)} %pad_maximum_fusion.30), channel_id=1, source_target_pairs={{0,1},{1,0},{2,3},{3,2},{4,5},{5,4},{6,7},{7,6},{8,9},{9,8},{10,11... | collective-permute-start | bytes 1327112 | tf_op jit(solution)/shard_map/ppermute | solution.py:33
  (218 other events, 1205.2 us)

commit v2 on v1

v2 whole, which is shorter than its diff:
```python
import jax
import jax.numpy as jnp
from jax import lax
from jax.experimental import pallas as pl
from jax.experimental.pallas import tpu as pltpu
from jax.sharding import PartitionSpec as P

H = 12
HD = 64
EPSILON = 1e-05
FLOOR_SCORE = -1e30
SCALE = float(HD) ** (-0.5)
LOW = jnp.bfloat16
WIDE = jnp.float32


def mm(left, right):
    return jnp.dot(left, right, preferred_element_type=WIDE)


def mm_tn(left, right):
    return lax.dot_general(left, right, (((0,), (0,)), ((), ())), preferred_element_type=WIDE)


def mm_nt(left, right):
    return lax.dot_general(left, right, (((1,), (1,)), ((), ())), preferred_element_type=WIDE)


def flip_model(value, bit):
    count = lax.axis_size("fsdp")
    return lax.ppermute(value, "fsdp", [(i, i ^ bit) for i in range(count)])


def flip_ctx(value, bit):
    count = lax.axis_size("ctx")
    return lax.ppermute(value, "ctx", [(i, i ^ bit) for i in range(count)])


def swap_places(value):
    model = lax.axis_size("fsdp")
    ctx = lax.axis_size("ctx")
    lines = ctx // model
    route = []
    for f in range(model):
        for z in range(model):
            for r in range(lines):
                route.append((f * ctx + z * lines + r, z * ctx + f * lines + r))
    return lax.ppermute(value, ("fsdp", "ctx"), route)


def powers(limit):
    bits = []
    bit = 1
    while bit < limit:
        bits.append(bit)
        bit *= 2
    return bits


def line_bits():
    return powers(lax.axis_size("ctx") // lax.axis_size("fsdp"))


def after(value, *others):
    return lax.optimization_barrier((value,) + others)[0]


def shape(dims, kind):
    return jax.ShapeDtypeStruct(tuple(dims), kind)


def cost(flops, *arrays):
    count = 0
    for array in arrays:
        count += array.size * array.dtype.itemsize
    return pl.CostEstimate(flops=flops, transcendentals=0, bytes_accessed=count)


def call(kernel, outs, spot, operands, flops=0, scratch=(), limit=12, piped=False):
    many = isinstance(outs, tuple)
    listed = outs if many else (outs,)
    if piped:
        place = lambda value: pl.BlockSpec(value.shape, lambda i, spot: (0,) * len(value.shape))
        spec = dict(
            grid_spec=pltpu.PrefetchScalarGridSpec(
                num_scalar_prefetch=1,
                grid=(1,),
                in_specs=[place(value) for value in operands],
                out_specs=tuple(place(value) for value in listed) if many else place(outs),
                scratch_shapes=list(scratch),
            )
        )
        limit = limit + 12
    else:
        place = pl.BlockSpec(memory_space=pltpu.VMEM)
        spec = dict(
            in_specs=[pl.BlockSpec(memory_space=pltpu.SMEM)] + [place] * len(operands),
            out_specs=tuple(place for _ in listed) if many else place,
            scratch_shapes=list(scratch),
        )
    return pl.pallas_call(
        kernel,
        out_shape=outs,
        cost_estimate=cost(flops, *operands, *listed),
        compiler_params=pltpu.CompilerParams(vmem_limit_bytes=limit << 20),
        **spec,
    )(spot, *operands)


def prepare_qkv(spot, weight, small):
    rows = weight.shape[0]

    def kernel(spot_ref, w_ref, small_ref, own_ref, near_ref, far_ref, all_ref):
        me = spot_ref[0]
        side = spot_ref[2]
        small = small_ref[...].astype(LOW)
        tail = jnp.zeros((16, 2 * rows), LOW)
        for d in range(4):
            for p in range(3):
                piece = w_ref[:, p * 4 * rows + d * rows : p * 4 * rows + (d + 1) * rows]
                all_ref[me ^ d, :, p * rows : (p + 1) * rows] = piece.astype(LOW)
        own_ref[:rows] = all_ref[0]
        near_ref[:rows] = all_ref[1]
        far_ref[:rows] = all_ref[2 + side]
        for ref in (own_ref, near_ref, far_ref):
            ref[rows:, :rows] = small
            ref[rows:, rows:] = tail

    piece = (rows + 16, 3 * rows)
    return call(
        kernel,
        (shape(piece, LOW),) * 3,
        spot,
        (weight, small),
        scratch=[pltpu.VMEM((4, rows, 3 * rows), LOW)],
    )


def prepare_rest(spot, cross_q, cross_kv, ffn_in, self_out, cross_out, ffn_out):
    rows = cross_q.shape[0]
    wide = ffn_in.shape[1] // 4
    piece = (rows, 3 * rows + wide)

    def kernel(spot_ref, q_ref, kv_ref, fi_ref, so_ref, co_ref, fo_ref, *outs):
        own_ref, near_ref, far_ref, so_out, co_out, fo_out, all_ref = outs
        me = spot_ref[0]
        side = spot_ref[2]
        for d in range(4):
            all_ref[me ^ d, :, :rows] = q_ref[:, d * rows : (d + 1) * rows].astype(LOW)
            for p in range(2):
                part = kv_ref[:, (p * 4 + d) * rows : (p * 4 + d + 1) * rows]
                all_ref[me ^ d, :, (1 + p) * rows : (2 + p) * rows] = part.astype(LOW)
            all_ref[me ^ d, :, 3 * rows :] = fi_ref[:, d * wide : (d + 1) * wide].astype(LOW)
        own_ref[...] = all_ref[0]
        near_ref[...] = all_ref[1]
        far_ref[...] = all_ref[2 + side]
        so_out[...] = so_ref[...].astype(LOW)
        co_out[...] = co_ref[...].astype(LOW)
        fo_out[...] = fo_ref[...].astype(LOW)

    return call(
        kernel,
        (shape(piece, LOW),) * 3
        + (shape(self_out.shape, LOW), shape(cross_out.shape, LOW), shape(ffn_out.shape, LOW)),
        spot,
        (cross_q, cross_kv, ffn_in, self_out, cross_out, ffn_out),
        scratch=[pltpu.VMEM((4,) + piece, LOW)],
        limit=16,
        piped=True,
    )


def ordered_blocks(spot_ref, refs, pair_ref):
    side = spot_ref[2]
    pair_ref[0, side] = refs[2][...]
    pair_ref[0, 1 - side] = refs[3][...]
    pair_ref[1, side] = refs[4][...]
    pair_ref[1, 1 - side] = refs[5][...]
    return refs[0][...], refs[1][...], pair_ref[0, 0], pair_ref[1, 1]


def arrange_rest(spot, blocks, source_rows, table):
    rows = blocks[0].shape[0]
    wide = blocks[0].shape[1] - 3 * rows
    count, width = source_rows.shape

    def kernel(spot_ref, *refs):
        x_ref, table_ref, q_ref, kv_ref, fi_ref, keys_ref, values_ref, rel_ref, pair_ref = refs[6:]
        me = spot_ref[0]
        parts = ordered_blocks(spot_ref, refs[:6], pair_ref)
        for k in range(4):
            start = pl.multiple_of((me ^ k) * rows, 64)
            q_ref[pl.ds(start, rows), :] = parts[k][:, :rows]
            kv_ref[pl.ds(start, rows), :] = parts[k][:, rows : 3 * rows]
            fi_ref[pl.ds(start, rows), :] = parts[k][:, 3 * rows :]
        for j in range(4):
            rel_ref[j] = table_ref[:, j * rows : (j + 1) * rows]
        shift = rel_ref[me][7:8]
        out = mm(x_ref[...], kv_ref[...])
        keys_ref[...] = out[:, :rows].astype(LOW)
        values_ref[...] = (out[:, rows:] + shift).astype(LOW)

    return call(
        kernel,
        (
            shape((4 * rows, rows), LOW),
            shape((4 * rows, 2 * rows), LOW),
            shape((4 * rows, wide), LOW),
            shape((count, rows), LOW),
            shape((count, rows), LOW),
        ),
        spot,
        tuple(blocks) + (source_rows, table),
        flops=4 * count * width * rows,
        scratch=[pltpu.VMEM((4, 16, rows), WIDE), pltpu.VMEM((2, 2) + blocks[0].shape, LOW)],
        limit=16,
    )


def project(spot, near_rows, far_rows, blocks, tokens, sources):
    lines = near_rows.shape[0]
    width = near_rows.shape[-1]
    local = width // 4
    span = near_rows.shape[2]
    rows = 4 * tokens

    def kernel(spot_ref, a_ref, b_ref, *refs):
        x_ref, e_ref, q_ref, k_ref, v_ref, wq_ref, wkv_ref, table_ref, *outs = refs[6:]
        marks_ref, emarks_ref, rel_ref, w_ref, pair_ref = outs
        me = spot_ref[0]

        @pl.when(pl.program_id(0) == 0)
        def _():
            parts = ordered_blocks(spot_ref, refs[:6], pair_ref)
            for k in range(4):
                start = pl.multiple_of((me ^ k) * local, 64)
                w_ref[pl.ds(start, local), :] = parts[k][:local]
                rel_ref[k] = parts[k][local:, :local].astype(WIDE)
            for j in range(4):
                table_ref[:, j * local : (j + 1) * local] = rel_ref[me ^ j]
            wq_ref[...] = w_ref[:, :local]
            wkv_ref[...] = w_ref[:, local:]

        lane = lax.broadcasted_iota(jnp.int32, (1, 128), 1)
        emarks = jnp.zeros((1, 128), WIDE)
        for kc, ref in enumerate((a_ref, b_ref)):
            for kx in range(2):
                at = 2 * kc + kx
                start = at * tokens
                x_ref[start : start + tokens, :] = ref[0, kx, :tokens, :]
                e_ref[at * sources : (at + 1) * sources, :] = ref[0, kx, tokens : tokens + sources, :]
                marks = ref[0, kx, tokens + sources : tokens + sources + 16, :256].astype(WIDE)
                marks_ref[:, start : start + tokens] = marks[0:1, :tokens]
                moved = pltpu.roll(marks[:8, 128:], at * sources, 1)[0:1]
                emarks = emarks + jnp.where((lane // sources) == at, moved, 0.0)
        emarks_ref[...] = emarks
        own_small = rel_ref[0]
        out = mm(x_ref[...], w_ref[...])
        k_ref[...] = out[:, local : 2 * local].astype(LOW)
        v_ref[...] = (out[:, 2 * local :] + own_small[4:5]).astype(LOW)

        @pl.when(pl.program_id(0) == 0)
        def _():
            q_ref[...] = ((out[:, :local] + own_small[3:4]) * SCALE).astype(LOW)

    full = lambda *dims: pl.BlockSpec(dims, lambda i, spot: (0,) * len(dims))
    band = lambda w: pl.BlockSpec((rows, w), lambda i, spot: (i, 0))
    part = pl.BlockSpec((1, 2, span, width), lambda i, spot: (i, 0, 0, 0))
    piece = (local + 16, 3 * local)
    outs = (
        shape((lines * rows, width), LOW),
        shape((lines * 4 * sources, width), LOW),
        shape((rows, local), LOW),
        shape((lines * rows, local), LOW),
        shape((lines * rows, local), LOW),
        shape((width, local), LOW),
        shape((width, 2 * local), LOW),
        shape((16, width), WIDE),
        shape((1, lines * rows), WIDE),
        shape((1, lines * 4 * sources), WIDE),
    )
    operands = (near_rows, far_rows) + tuple(blocks)
    return pl.pallas_call(
        kernel,
        out_shape=outs,
        grid_spec=pltpu.PrefetchScalarGridSpec(
            num_scalar_prefetch=1,
            grid=(lines,),
            in_specs=[part, part] + [full(*piece)] * 6,
            out_specs=(
                band(width),
                pl.BlockSpec((4 * sources, width), lambda i, spot: (i, 0)),
                full(rows, local),
                band(local),
                band(local),
                full(width, local),
                full(width, 2 * local),
                full(16, width),
                pl.BlockSpec((1, rows), lambda i, spot: (0, i)),
                pl.BlockSpec((1, 4 * sources), lambda i, spot: (0, i)),
            ),
            scratch_shapes=[
                pltpu.VMEM((4, 16, local), WIDE),
                pltpu.VMEM((width, 3 * local), LOW),
                pltpu.VMEM((2, 2) + piece, LOW),
            ],
        ),
        cost_estimate=cost(6 * lines * rows * width * local, *operands, *outs),
        compiler_params=pltpu.CompilerParams(vmem_limit_bytes=20 << 20),
    )(spot, *operands)


def block_start(spot_ref, index, tokens, lines):
    me = spot_ref[0]
    line = spot_ref[3]
    kr, kc, kx = index // 4, (index // 2) % 2, index % 2
    return ((me ^ (kc + 2 * kx)) * lines + (line ^ kr)) * tokens


def upright(row):
    return jnp.transpose(jnp.broadcast_to(row, (128, row.shape[1])))


def self_floor(spot_ref, marks_ref, query_blocks, tokens, turned):
    blocks = marks_ref.shape[1] // tokens
    lines = blocks // 4
    down = lax.broadcasted_iota(jnp.int32, (tokens, tokens), 0)
    right = lax.broadcasted_iota(jnp.int32, (tokens, tokens), 1)
    outer, inner = (range(blocks), query_blocks) if turned else (query_blocks, range(blocks))
    table = []
    for i in outer:
        tall = upright(marks_ref[:, i * tokens : (i + 1) * tokens])
        line = []
        for j in inner:
            flat = marks_ref[:, j * tokens : (j + 1) * tokens]
            gap = block_start(spot_ref, j, tokens, lines) - block_start(spot_ref, i, tokens, lines)
            ahead = (right + gap) - down
            near = (ahead >= 0) if turned else (ahead <= 0)
            line.append(jnp.where((tall == flat) & near, 0.0, FLOOR_SCORE))
        table.append(jnp.concatenate(line, axis=1))
    return jnp.concatenate(table, axis=0)


def head_lanes(value, head):
    lane = lax.broadcasted_iota(jnp.int32, (1, value.shape[1]), 1) // HD
    return jnp.where(lane == head, value, jnp.zeros_like(value))


def attend_rows(queries, keys, values, floor):
    heads = queries.shape[1] // HD
    total = None
    for h in range(heads):
        scores = mm_nt(head_lanes(queries, h), keys) + floor
        top = jnp.max(scores, axis=1, keepdims=True)
        weights = jnp.exp(scores - top)
        prob = weights / jnp.sum(weights, axis=1, keepdims=True)
        part = head_lanes(mm(prob.astype(LOW), values), h)
        total = part if total is None else total + part
    return total.astype(LOW)


def attend_rows_back(queries, keys, values, grads, floor):
    heads = queries.shape[1] // HD
    query_grad = key_grad = value_grad = None
    for h in range(heads):
        own_queries = head_lanes(queries, h)
        own_grads = head_lanes(grads, h)
        scores = mm_nt(keys, own_queries) + floor
        top = jnp.max(scores, axis=0, keepdims=True)
        weights = jnp.exp(scores - top)
        prob = weights / jnp.sum(weights, axis=0, keepdims=True)
        prob_grad = mm_nt(values, own_grads)
        inner = jnp.sum(prob * prob_grad, axis=0, keepdims=True)
        score_grad = (prob * (prob_grad - inner)).astype(LOW)
        part_q = head_lanes(mm_tn(score_grad, keys), h)
        part_k = mm(score_grad, own_queries)
        part_v = mm(prob.astype(LOW), own_grads)
        query_grad = part_q if query_grad is None else query_grad + part_q
        key_grad = part_k if key_grad is None else key_grad + part_k
        value_grad = part_v if value_grad is None else value_grad + part_v
    return query_grad, key_grad, value_grad


def block_rows(keys):
    return 256 if keys <= 1024 else 128


def self_forward(spot, marks, queries, keys, values, weight, tokens):
    rows, local = queries.shape
    width = weight.shape[1]
    size = block_rows(keys.shape[0])

    def kernel(spot_ref, marks_ref, q_ref, k_ref, v_ref, w_ref, o_ref, keep_ref, send_ref):
        for begin in range(0, rows, size):
            blocks = range(begin // tokens, (begin + size) // tokens)
            floor = self_floor(spot_ref, marks_ref, blocks, tokens, False)
            low = attend_rows(q_ref[begin : begin + size], k_ref[...], v_ref[...], floor)
            o_ref[begin : begin + size] = low
            part = mm(low, w_ref[...])
            if begin < rows // 2:
                keep_ref[begin : begin + size] = part
            else:
                send_ref[begin - rows // 2 : begin - rows // 2 + size] = part.astype(LOW)

    return call(
        kernel,
        (shape((rows, local), LOW), shape((rows // 2, width), WIDE), shape((rows // 2, width), LOW)),
        spot,
        (marks, queries, keys, values, weight),
        flops=4 * rows * keys.size + 2 * rows * weight.size,
        limit=20,
    )


def plain_floor(marks, places, rows):
    same = marks.reshape(-1)[:rows, None] == marks
    return jnp.where(same & (places[None, :] <= places[:rows, None]), 0.0, FLOOR_SCORE)


def plain_forward(marks, places, queries, keys, values, weight):
    rows = queries.shape[0]
    low = attend_rows(queries, keys, values, plain_floor(marks, places, rows))
    part = mm(low, weight)
    return low, part[: rows // 2], part[rows // 2 :].astype(LOW)


def plain_back(marks, places, low, other, w_so, queries, keys, values):
    grads = mm_nt(jnp.concatenate([low, other], axis=0), w_so).astype(LOW)
    floor = plain_floor(marks, places, queries.shape[0])
    dq, dk, dv = attend_rows_back(queries, keys, values, grads, floor.T)
    pre = (dq.astype(LOW).astype(WIDE) * SCALE).astype(LOW)
    sums = jnp.concatenate(column_rows(pre, dv), axis=0)
    return pre, jnp.concatenate([dk, dv], axis=1).astype(LOW), sums


def norm_rows(values):
    center = values - jnp.mean(values, axis=-1, keepdims=True)
    spread = jnp.mean(center * center, axis=-1, keepdims=True)
    rate = lax.rsqrt(spread + EPSILON)
    return center * rate, rate


def turned_halves(ref):
    half = ref.shape[0] // 2
    return jnp.concatenate([ref[half:], ref[:half]], axis=0).astype(WIDE)


def residual_norm(residual, mine, other, table, bias_row, norm_row):
    rows, width = mine.shape

    def kernel(spot_ref, r_ref, mine_ref, other_ref, table_ref, h_ref, low_ref, n_ref, rate_ref):
        total = r_ref[:rows].astype(WIDE) + mine_ref[...] + turned_halves(other_ref)
        normal, rate = norm_rows(total + table_ref[bias_row : bias_row + 1])
        gain = table_ref[10 + norm_row : 11 + norm_row]
        result = normal * gain + table_ref[norm_row : norm_row + 1]
        h_ref[...] = result
        low_ref[...] = result.astype(LOW)
        n_ref[...] = normal
        rate_ref[...] = rate

    return call(
        kernel,
        (
            shape((rows, width), WIDE),
            shape((rows, width), LOW),
            shape((rows, width), WIDE),
            shape((rows, 1), WIDE),
        ),
        jnp.zeros((1,), jnp.int32),
        (residual, mine, other, table),
    )


def cross_forward(spot, marks, emarks, low, other, w_cq, keys, values, w_co, small, tokens):
    half, width = low.shape
    local = w_cq.shape[1]

    def kernel(spot_ref, marks_ref, emarks_ref, a_ref, b_ref, w_ref, k_ref, v_ref, o_ref, small_ref, *outs):
        q_out, c_out, keep_ref, send_ref = outs
        for place, ref in enumerate((a_ref, b_ref)):
            at = slice(place * half, (place + 1) * half)
            low = ((mm(ref[...], w_ref[...]) + small_ref[6:7]) * SCALE).astype(LOW)
            q_out[at] = low
            tall = []
            for i in range(place * half // tokens, (place + 1) * half // tokens):
                tall.append(upright(marks_ref[:, i * tokens : (i + 1) * tokens])[:, :1])
            tall = jnp.concatenate(tall, axis=0)
            floor = jnp.where(tall == emarks_ref[...], 0.0, FLOOR_SCORE)
            crossed = attend_rows(low, k_ref[...], v_ref[...], floor)
            c_out[at] = crossed
            part = mm(crossed, o_ref[...])
            if place == 0:
                keep_ref[...] = part
            else:
                send_ref[...] = part.astype(LOW)

    return call(
        kernel,
        (
            shape((2 * half, local), LOW),
            shape((2 * half, local), LOW),
            shape((half, width), WIDE),
            shape((half, width), LOW),
        ),
        spot,
        (marks, emarks, low, other, w_cq, keys, values, w_co, small),
        flops=8 * half * width * local,
        limit=16,
    )


def ffn_forward(low, other, w_fi, w_fo, shift):
    half, width = low.shape
    wide = w_fi.shape[1]

    def kernel(spot_ref, a_ref, b_ref, w_ref, o_ref, shift_ref, g_ref, slope_ref, keep_ref, send_ref):
        for place, ref in enumerate((a_ref, b_ref)):
            at = slice(place * half, (place + 1) * half)
            pre = mm(ref[...], w_ref[...]) + shift_ref[...]
            bell = 0.5 * (1.0 + lax.erf(pre * (0.5**0.5)))
            act = (pre * bell).astype(LOW)
            g_ref[at] = act
            slope_ref[at] = bell + pre * jnp.exp(-0.5 * pre * pre) * 0.3989422804014327
            part = mm(act, o_ref[...])
            if place == 0:
                keep_ref[...] = part
            else:
                send_ref[...] = part.astype(LOW)

    return call(
        kernel,
        (
            shape((2 * half, wide), LOW),
            shape((2 * half, wide), WIDE),
            shape((half, width), WIDE),
            shape((half, width), LOW),
        ),
        jnp.zeros((1,), jnp.int32),
        (low, other, w_fi, w_fo, shift),
        flops=8 * half * width * wide,
    )


def norm_back(grad, normal, rate, gain):
    up = grad * gain
    mean_up = jnp.mean(up, axis=-1, keepdims=True)
    mean_both = jnp.mean(up * normal, axis=-1, keepdims=True)
    return rate * (up - mean_up - normal * mean_both)


def column_rows(*values):
    rows = [jnp.sum(value.astype(WIDE), axis=0, keepdims=True) for value in values]
    return rows


def turn_around(residual, mine, other, table, own_grad, other_grad, tokens):
    rows, width = mine.shape

    def kernel(spot_ref, r_ref, mine_ref, other_ref, table_ref, a_ref, b_ref, out_ref, d_ref, low_ref, sum_ref):
        total = r_ref[...] + mine_ref[...] + turned_halves(other_ref) + table_ref[9:10]
        normal, rate = norm_rows(total)
        gain = table_ref[12:13]
        out_ref[...] = (normal[:tokens] * gain + table_ref[2:3]).astype(LOW)
        grad = jnp.concatenate([a_ref[:tokens], b_ref[:tokens]], axis=0).astype(WIDE)
        back = norm_back(grad, normal, rate, gain)
        low = back.astype(LOW)
        d_ref[...] = back
        low_ref[...] = low
        rows = column_rows(grad[:tokens], (grad * normal)[:tokens], low[:tokens])
        for i in range(3):
            sum_ref[i : i + 1] = rows[i]

    return call(
        kernel,
        (
            shape((tokens, width), LOW),
            shape((rows, width), WIDE),
            shape((rows, width), LOW),
            shape((3, width), WIDE),
        ),
        jnp.zeros((1,), jnp.int32),
        (residual, mine, other, table, own_grad, other_grad),
        piped=True,
    )


def residual_back(previous, mine, other, normal, rate, table, norm_row, tokens):
    rows, width = mine.shape

    def kernel(spot_ref, p_ref, mine_ref, other_ref, n_ref, rate_ref, table_ref, d_ref, low_ref, sum_ref):
        grad = p_ref[...] + mine_ref[...] + turned_halves(other_ref)
        normal = n_ref[...]
        back = norm_back(grad, normal, rate_ref[...], table_ref[10 + norm_row : 11 + norm_row])
        low = back.astype(LOW)
        d_ref[...] = back
        low_ref[...] = low
        rows = column_rows(grad[:tokens], (grad * normal)[:tokens], low[:tokens])
        for i in range(3):
            sum_ref[i : i + 1] = rows[i]

    return call(
        kernel,
        (shape((rows, width), WIDE), shape((rows, width), LOW), shape((3, width), WIDE)),
        jnp.zeros((1,), jnp.int32),
        (previous, mine, other, normal, rate, table),
        piped=True,
    )


def ffn_back(low, other, w_fo, w_fi, slope):
    half, width = low.shape
    wide = w_fi.shape[1]

    def kernel(spot_ref, a_ref, b_ref, o_ref, w_ref, slope_ref, u_ref, keep_ref, send_ref, sum_ref):
        total = None
        for place, ref in enumerate((a_ref, b_ref)):
            at = slice(place * half, (place + 1) * half)
            inner = (mm_nt(ref[...], o_ref[...]) * slope_ref[at]).astype(LOW)
            u_ref[at] = inner
            row = column_rows(inner)[0]
            total = row if total is None else total + row
            part = mm_nt(inner, w_ref[...])
            if place == 0:
                keep_ref[...] = part
            else:
                send_ref[...] = part.astype(LOW)
        sum_ref[...] = total

    return call(
        kernel,
        (
            shape((2 * half, wide), LOW),
            shape((half, width), WIDE),
            shape((half, width), LOW),
            shape((1, wide), WIDE),
        ),
        jnp.zeros((1,), jnp.int32),
        (low, other, w_fo, w_fi, slope),
        flops=8 * half * width * wide,
        piped=True,
    )


def cross_back(spot, marks, emarks, low, other, w_co, queries, keys, values, w_cq, tokens):
    half, width = low.shape
    count, local = keys.shape

    def kernel(spot_ref, marks_ref, emarks_ref, a_ref, b_ref, co_ref, q_ref, k_ref, v_ref, cq_ref, *outs):
        dq_ref, dkv_ref, keep_ref, send_ref, sum_ref = outs
        key_grad = value_grad = None
        tall = []
        for i in range(count // 128):
            tall.append(upright(emarks_ref[:, i * 128 : (i + 1) * 128])[:, :1])
        tall = jnp.concatenate(tall, axis=0)
        totals = None
        for place, ref in enumerate((a_ref, b_ref)):
            at = slice(place * half, (place + 1) * half)
            grads = mm_nt(ref[...], co_ref[...]).astype(LOW)
            floor = jnp.where(tall == marks_ref[:, at], 0.0, FLOOR_SCORE)
            dq, dk, dv = attend_rows_back(q_ref[at], k_ref[...], v_ref[...], grads, floor)
            pre = (dq.astype(LOW).astype(WIDE) * SCALE).astype(LOW)
            dq_ref[at] = pre
            key_grad = dk if key_grad is None else key_grad + dk
            value_grad = dv if value_grad is None else value_grad + dv
            row = column_rows(pre)[0]
            totals = row if totals is None else totals + row
            part = mm_nt(pre, cq_ref[...])
            if place == 0:
                keep_ref[...] = part
            else:
                send_ref[...] = part.astype(LOW)
        dkv_ref[:, :local] = key_grad.astype(LOW)
        dkv_ref[:, local:] = value_grad.astype(LOW)
        sum_ref[0:1] = totals
        sum_ref[1:2] = column_rows(value_grad)[0]

    return call(
        kernel,
        (
            shape((2 * half, local), LOW),
            shape((count, 2 * local), LOW),
            shape((half, width), WIDE),
            shape((half, width), LOW),
            shape((2, local), WIDE),
        ),
        spot,
        (marks, emarks, low, other, w_co, queries, keys, values, w_cq),
        flops=8 * half * width * local,
        limit=16,
        piped=True,
    )


def self_back(spot, marks, low, other, w_so, queries, keys, values, tokens):
    half, width = low.shape
    count, local = keys.shape
    rows = 2 * half
    size = block_rows(count)

    def kernel(spot_ref, marks_ref, a_ref, b_ref, so_ref, q_ref, k_ref, v_ref, dq_ref, dkv_ref, sum_ref, dk_ref, dv_ref):
        totals = None
        for begin in range(0, rows, size):
            source = a_ref if begin < half else b_ref
            local_at = begin % half
            grads = mm_nt(source[local_at : local_at + size], so_ref[...]).astype(LOW)
            blocks = range(begin // tokens, (begin + size) // tokens)
            floor = self_floor(spot_ref, marks_ref, blocks, tokens, True)
            at = slice(begin, begin + size)
            dq, dk, dv = attend_rows_back(q_ref[at], k_ref[...], v_ref[...], grads, floor)
            pre = (dq.astype(LOW).astype(WIDE) * SCALE).astype(LOW)
            dq_ref[at] = pre
            row = column_rows(pre)[0]
            totals = row if totals is None else totals + row
            if begin == 0:
                dk_ref[...] = dk
                dv_ref[...] = dv
            else:
                dk_ref[...] += dk
                dv_ref[...] += dv
        dkv_ref[:, :local] = dk_ref[...].astype(LOW)
        dkv_ref[:, local:] = dv_ref[...].astype(LOW)
        sum_ref[0:1] = totals
        sum_ref[1:2] = column_rows(dv_ref[...])[0]

    return call(
        kernel,
        (shape((rows, local), LOW), shape((count, 2 * local), LOW), shape((2, local), WIDE)),
        spot,
        (marks, low, other, w_so, queries, keys, values),
        flops=10 * rows * keys.size,
        scratch=[pltpu.VMEM((count, local), WIDE), pltpu.VMEM((count, local), WIDE)],
        limit=24,
        piped=True,
    )


def input_back(query_grad, pair_grad, w_q, w_kv):
    rows = query_grad.shape[0]
    width = w_q.shape[0]

    def kernel(spot_ref, q_ref, kv_ref, wq_ref, wkv_ref, keep_ref, send_ref):
        part = mm_nt(q_ref[...], wq_ref[...]) + mm_nt(kv_ref[...], wkv_ref[...])
        keep_ref[...] = part[: rows // 2]
        send_ref[...] = part[rows // 2 :].astype(LOW)

    return call(
        kernel,
        (shape((rows // 2, width), WIDE), shape((rows // 2, width), LOW)),
        jnp.zeros((1,), jnp.int32),
        (query_grad, pair_grad, w_q, w_kv),
        flops=2 * rows * (w_q.size + w_kv.size),
        piped=True,
    )


def produce_ffn(spot, activated, grad_low, grad_other, low, other, inner_grad):
    wide = activated.shape[1]
    half, width = grad_low.shape
    part = width // 16

    def kernel(spot_ref, a_ref, g0_ref, g1_ref, x0_ref, x1_ref, u_ref, *refs):
        outs, all_ref = refs[:4], refs[4]
        me = spot_ref[0]
        high = spot_ref[1]
        low = spot_ref[2]
        for place in range(2):
            if place == 0:
                result = mm_tn(a_ref[:half], g0_ref[...]) + mm_tn(a_ref[half:], g1_ref[...])
            else:
                result = mm_tn(x0_ref[...], u_ref[:half]) + mm_tn(x1_ref[...], u_ref[half:])
            for d in range(4):
                for z in range(2):
                    for y in range(2):
                        at = (4 * d + 2 * z + y) * part
                        piece = result[at : at + part]
                        if place == 0:
                            all_ref[low ^ y, high ^ z, d] = piece
                        else:
                            all_ref[high ^ z, low ^ y, me ^ d] = piece
            outs[2 * place][...] = all_ref[0]
            outs[2 * place + 1][...] = all_ref[1].astype(LOW)

    piece = (2, 4, part, width)
    return call(
        kernel,
        (shape(piece, WIDE), shape(piece, LOW)) * 2,
        spot,
        (activated, grad_low, grad_other, low, other, inner_grad),
        flops=8 * half * width * wide,
        scratch=[pltpu.VMEM((2,) + piece, WIDE)],
        limit=16,
        piped=True,
    )


def finish_ffn(spot, out_pieces, in_pieces):
    part, width = out_pieces[0].shape[1:]
    rows = 4 * part

    def kernel(spot_ref, oa_ref, ob_ref, oc_ref, ia_ref, ib_ref, ic_ref, fo_ref, fi_ref):
        me = spot_ref[0]
        high = spot_ref[1]
        low = spot_ref[2]
        for kz in range(2):
            for ky in range(2):
                quarter = ((kz ^ high) * 2 + (ky ^ low)) * part
                source = oc_ref.at[kz] if ky else (ob_ref if kz else oa_ref)
                for d in range(4):
                    row = pl.multiple_of(d * rows + quarter, 16)
                    fo_ref[pl.ds(row, part), :] = source[d].astype(WIDE)
                source = ic_ref.at[ky] if kz else (ib_ref if ky else ia_ref)
                row = pl.multiple_of(quarter, 16)
                for j in range(4):
                    fi_ref[pl.ds(row, part), j * width : (j + 1) * width] = source[me ^ j].astype(WIDE)

    return call(
        kernel,
        (shape((4 * rows, width), WIDE), shape((rows, 4 * width), WIDE)),
        spot,
        tuple(out_pieces) + tuple(in_pieces),
        limit=16,
        piped=True,
    )


def produce_mixed(spot, one_ins, one_grad, two_in, two_grad, heads, grad_low, grad_other):
    local = one_grad.shape[1]
    half, width = grad_low.shape
    part = local // 4
    count = len(one_ins)

    def kernel(spot_ref, *refs):
        a_refs, refs = refs[:count], refs[count:]
        ag_ref, b_ref, bg_ref, o_ref, g0_ref, g1_ref, keep_ref, send_ref, all_ref = refs
        me = spot_ref[0]
        high = spot_ref[1]
        low = spot_ref[2]
        if count == 2:
            one = mm_tn(a_refs[0][...], ag_ref[:half]) + mm_tn(a_refs[1][...], ag_ref[half:])
        else:
            one = mm_tn(a_refs[0][: 2 * half], ag_ref[...])
        two = mm_tn(b_ref[...], bg_ref[...])
        three = mm_tn(o_ref[:half], g0_ref[...]) + mm_tn(o_ref[half:], g1_ref[...])
        for z in range(2):
            for y in range(2):
                quarter = (2 * z + y) * part
                for d in range(4):
                    at = d * local + quarter
                    all_ref[low ^ y, high ^ z, me ^ d, :, :local] = one[at : at + part]
                    all_ref[low ^ y, high ^ z, me ^ d, :, local : 3 * local] = two[at : at + part]
                    piece = three[quarter : quarter + part, d * local : (d + 1) * local]
                    all_ref[low ^ y, high ^ z, d, :, 3 * local :] = piece
        keep_ref[...] = all_ref[0]
        send_ref[...] = all_ref[1].astype(LOW)

    operands = tuple(one_ins) + (one_grad, two_in, two_grad, heads, grad_low, grad_other)
    return call(
        kernel,
        (shape((2, 4, part, width), WIDE), shape((2, 4, part, width), LOW)),
        spot,
        operands,
        flops=2 * width * (one_grad.size + two_grad.size + heads.size),
        scratch=[pltpu.VMEM((2, 2, 4, part, width), WIDE)],
        piped=True,
    )


def finish_mixed(spot, own_piece, first_piece, last_pieces, fused):
    part, width = own_piece.shape[1:]
    local = 4 * part

    def kernel(spot_ref, a_ref, b_ref, c_ref, *outs):
        me = spot_ref[0]
        high = spot_ref[1]
        low = spot_ref[2]
        for kz in range(2):
            for ky in range(2):
                row = pl.multiple_of(((kz ^ high) * 2 + (ky ^ low)) * part, 16)
                early, late = (kz, ky) if fused else (ky, kz)
                ref = c_ref.at[early] if late else (b_ref if early else a_ref)
                for j in range(4):
                    block = ref[me ^ j].astype(WIDE)
                    for p in range(3):
                        piece = block[:, p * local : (p + 1) * local]
                        if fused:
                            out, at = outs[0], p * width + j * local
                        elif p == 0:
                            out, at = outs[0], j * local
                        else:
                            out, at = outs[1], (p - 1) * width + j * local
                        out[pl.ds(row, part), at : at + local] = piece
                    flat = ref[j, :, 3 * local :].astype(WIDE)
                    outs[-1][pl.ds(row, part), j * local : (j + 1) * local] = flat

    widths = (3 * width, width) if fused else (width, 2 * width, width)
    return call(
        kernel,
        tuple(shape((local, w), WIDE) for w in widths),
        spot,
        (own_piece, first_piece, last_pieces),
        piped=True,
    )


def exchange_sum(keep, send, bit, *holds):
    got = flip_ctx(send, bit)
    if holds:
        got = after(got, *holds)
    return keep + got.astype(WIDE)


def sum_rest(total):
    lines = lax.axis_size("ctx") // lax.axis_size("fsdp")
    for bit in powers(lax.axis_size("ctx")):
        if bit not in (1, lines):
            low = total.astype(LOW)
            total = low.astype(WIDE) + flip_ctx(low, bit).astype(WIDE)
    return total.astype(LOW)


def trade_columns(low):
    part = low.shape[1]
    local = 4 * part
    far = flip_model(low[2:], 2)
    near = flip_model(jnp.stack([low[1], far[1]]), 1)
    columns = jnp.stack([low[0], near[0], far[0], near[1]])
    return jnp.concatenate([columns[..., : 3 * local], low[..., 3 * local :]], axis=-1)


def gather_pieces(piece, bits):
    first = flip_ctx(piece, bits[0])
    return piece, first, flip_ctx(jnp.stack([piece, first]), bits[1])


def move_columns(mate, cross, *holds):
    line = flip_ctx(after(cross, *holds), 1)
    return flip_model(mate, 1), cross, line, flip_model(cross, 1), flip_model(line, 1)


def core_sum(keep, send):
    mine = keep + flip_model(send, 1).astype(WIDE)
    return mine, flip_model(mine.astype(LOW), 2)


def sum_lines(low, lines):
    value = low.reshape(lines, -1, low.shape[1])
    for bit in reversed(line_bits()):
        value = value[:bit].astype(WIDE) + flip_ctx(value[bit:], bit).astype(WIDE)
        value = value.astype(LOW)
    return value[0]


def body(
    hidden,
    encoded,
    cotangent,
    dec_seg,
    enc_seg,
    self_qkv,
    self_out,
    cross_q,
    cross_kv,
    cross_out,
    ffn_in,
    ffn_out,
    biases,
    gains,
    ffn_bias,
):
    tokens = hidden.shape[1]
    width = hidden.shape[2]
    sources = encoded.shape[1]
    model = lax.axis_size("fsdp")
    lines = lax.axis_size("ctx") // model
    own = lax.axis_index("fsdp")
    ctx_index = lax.axis_index("ctx")
    local = width // model
    spot = jnp.stack([own, (ctx_index // lines) % 2, ctx_index % 2, ctx_index % lines])
    spot = spot.astype(jnp.int32)

    marks = jnp.concatenate([dec_seg[0], enc_seg[0]]).astype(LOW)
    marks = jnp.pad(marks, (0, width - tokens - sources))[None]
    block = jnp.concatenate([hidden[0], encoded[0], jnp.pad(marks, ((0, 15), (0, 0)))], axis=0)
    self_qkv = after(self_qkv, block)
    block = swap_places(block)
    small = jnp.concatenate([biases, gains, jnp.zeros((3, local), WIDE)], axis=0)
    qkv_own, qkv_mate, qkv_away = prepare_qkv(spot, self_qkv, small)
    qkv_cross = flip_model(qkv_away, 2)
    block = after(block, qkv_cross)
    block_far = flip_model(block, 2)
    qkv_blocks = (qkv_own,) + move_columns(qkv_mate, qkv_cross, block)
    near_rows = jnp.stack([block, block_far])[None]
    rest_own, rest_mate, rest_away, w_so, w_co, w_fo = prepare_rest(
        spot, cross_q, cross_kv, ffn_in, self_out, cross_out, ffn_out
    )
    near_rows = after(near_rows, rest_away, qkv_blocks[3])
    rest_cross = flip_model(after(rest_away, block_far), 2)
    other = swap_places(after(cotangent[0], block_far))
    for bit in line_bits():
        near_rows = jnp.concatenate([near_rows, flip_ctx(near_rows, bit)], axis=0)
    near_rows = after(near_rows, rest_cross)
    far_rows = flip_model(near_rows, 1)
    rest_blocks = (rest_own,) + move_columns(rest_mate, rest_cross, near_rows)

    inputs, source_rows, queries, keys, values, w_q, w_kv, table, marks, emarks = project(
        spot, near_rows, far_rows, qkv_blocks, tokens, sources
    )
    queries = after(queries, other)
    other_far = flip_model(other, 2)
    plain = keys.shape[0] > 2048
    line_ids = (ctx_index % lines) ^ jnp.arange(lines, dtype=jnp.int32)[:, None]
    model_ids = own ^ jnp.array([0, 2, 1, 3], jnp.int32)[None, :]
    starts = (model_ids * lines + line_ids) * tokens
    places = (starts[:, :, None] + jnp.arange(tokens, dtype=jnp.int32)).reshape(-1)
    if plain:
        attended, keep, send = plain_forward(marks, places, queries, keys, values, w_so)
    else:
        attended, keep, send = self_forward(spot, marks, queries, keys, values, w_so, tokens)
    keep, send = after(keep, other_far), after(send, other_far)
    mine, away = core_sum(keep, send)
    w_cq, w_ckv, w_fi, source_keys, source_values = arrange_rest(
        spot, rest_blocks, source_rows, table
    )
    away = after(away, w_cq)
    first, first_low, first_normal, first_rate = residual_norm(inputs, mine, away, table, 5, 0)
    first_other = flip_model(first_low, 1)
    small_low = small.astype(LOW).astype(WIDE)
    cross_queries, crossed, keep, send = cross_forward(
        spot, marks, emarks, first_low, first_other, w_cq, source_keys, source_values, w_co, small_low, tokens
    )
    mine, away = core_sum(keep, send)
    second, second_low, second_normal, second_rate = residual_norm(first, mine, away, table, 8, 1)
    second_other = flip_model(second_low, 1)
    inner_bias = ffn_bias.astype(LOW).astype(WIDE)[None]
    activated, slope, keep, send = ffn_forward(second_low, second_other, w_fi, w_fo, inner_bias)
    mine, away = core_sum(keep, send)
    result, third_grad, ffn_low, third_sums = turn_around(
        second, mine, away, table, other, other_far, tokens
    )
    result = swap_places(result)
    output = result[None]

    ffn_other = flip_model(ffn_low, 1)
    inner_grad, keep, send, inner_sum = ffn_back(ffn_low, ffn_other, w_fo, w_fi, slope)
    mine, away = core_sum(keep, send)
    out_keep, out_send, in_keep, in_send = produce_ffn(
        spot, activated, ffn_low, ffn_other, second_low, second_other, inner_grad
    )
    away = after(away, in_keep, result)
    out_got = flip_ctx(out_send, 1)
    in_got = flip_ctx(in_send, lines)
    second_grad, cross_low, second_sums = residual_back(
        third_grad, mine, away, second_normal, second_rate, table, 1, tokens
    )
    cross_other = flip_model(cross_low, 1)
    cross_query_pre, source_grad, keep, send, cross_sums = cross_back(
        spot, marks, emarks, cross_low, cross_other, w_co, cross_queries, source_keys, source_values, w_cq, tokens
    )
    mine, away = core_sum(keep, send)
    cross_keep, cross_send = produce_mixed(
        spot, (first_low, first_other), cross_query_pre, source_rows, source_grad, crossed, cross_low, cross_other
    )
    away = after(away, cross_keep)
    cross_got = flip_ctx(cross_send, 1)
    first_grad, self_low, first_sums = residual_back(
        second_grad, mine, away, first_normal, first_rate, table, 0, tokens
    )
    self_other = flip_model(self_low, 1)
    out_half = out_keep + after(out_got, self_low).astype(WIDE)
    in_half = in_keep + after(in_got, self_low).astype(WIDE)
    out_got = flip_ctx(out_half[1].astype(LOW), lines)
    in_got = flip_ctx(in_half[1].astype(LOW), 1)
    if plain:
        self_query_pre, pair_grad, self_sums = plain_back(
            marks, places, self_low, self_other, w_so, queries, keys, values
        )
    else:
        self_query_pre, pair_grad, self_sums = self_back(
            spot, marks, self_low, self_other, w_so, queries, keys, values, tokens
        )
    self_keep, self_send = produce_mixed(
        spot, (inputs,), self_query_pre, inputs, pair_grad, attended, self_low, self_other
    )
    self_total = exchange_sum(self_keep, self_send, 1)
    ffn_total = jnp.stack(
        [
            out_half[0] + after(out_got, self_keep).astype(WIDE),
            in_half[0] + after(in_got, self_keep).astype(WIDE),
        ]
    )
    ffn_total = sum_rest(ffn_total)
    cross_total = cross_keep + after(cross_got, self_keep).astype(WIDE)
    cross_total = exchange_sum(cross_total[0], cross_total[1].astype(LOW), lines, self_total)
    cross_piece = sum_rest(after(cross_total, ffn_total))
    pair_own = sum_lines(after(pair_grad, self_total), lines)
    source_own = sum_lines(after(source_grad, self_total), lines)
    encoded_part = mm_nt(source_own, w_ckv)
    encoded_part = encoded_part[: 2 * sources] + flip_model(
        encoded_part[2 * sources :].astype(LOW), 1
    ).astype(WIDE)
    encoded_part = encoded_part[:sources] + flip_model(
        encoded_part[sources:].astype(LOW), 2
    ).astype(WIDE)

    keep, send = input_back(self_query_pre, pair_own, w_q, w_kv)
    input_part = keep + flip_model(send, 1).astype(WIDE)
    input_part = input_part[:tokens] + flip_model(input_part[tokens:].astype(LOW), 2).astype(WIDE)
    input_grad = first_grad[:tokens] + input_part
    both = jnp.concatenate([input_grad, encoded_part], axis=0).astype(LOW)
    both = swap_places(both).astype(WIDE)[None]
    hidden_grad = both[:, :tokens]
    encoded_grad = both[:, tokens:]

    self_total = exchange_sum(self_total[0], self_total[1].astype(LOW), lines)
    self_piece = sum_rest(self_total)
    cross_pieces = gather_pieces(trade_columns(cross_piece), (1, lines))
    self_pieces = gather_pieces(trade_columns(self_piece), (lines, 1))
    ffn_far = flip_model(ffn_total[1, 2:], 2)
    ffn_near = flip_model(jnp.stack([ffn_total[1, 1], ffn_far[1]]), 1)
    ffn_piece = jnp.stack([ffn_total[1, 0], ffn_near[0], ffn_far[0], ffn_near[1]])
    out_pieces = gather_pieces(ffn_total[0], (lines, 1))
    in_pieces = gather_pieces(ffn_piece, (1, lines))
    g_cq, g_ckv, g_co = finish_mixed(spot, *cross_pieces, False)
    g_fo, g_fi = finish_ffn(spot, out_pieces, in_pieces)
    g_qkv, g_so = finish_mixed(spot, *self_pieces, True)

    wide_rows = jnp.concatenate([first_sums, second_sums, third_sums], axis=0)
    wide_rows = after(wide_rows, self_keep)
    for bit in (1, 2):
        wide_rows = wide_rows + flip_model(wide_rows, bit)
    wide_rows = lax.dynamic_slice_in_dim(wide_rows, own * local, local, axis=1)
    vectors = jnp.concatenate(
        [wide_rows, self_sums, cross_sums, inner_sum.reshape(-1, local)], axis=0
    )
    vectors = after(vectors, pair_own)
    holds = {1: input_grad, lines: self_piece}
    for bit in powers(lax.axis_size("ctx")):
        vectors = vectors + after(flip_ctx(vectors, bit), holds.get(bit, self_piece))
    d_bias = jnp.stack([vectors[i] for i in (0, 3, 6, 9, 10, 2, 11, 12, 5, 8)])
    d_gain = jnp.stack([vectors[i] for i in (1, 4, 7)])
    d_inner = vectors[13:].reshape(-1)
    return (
        output,
        hidden_grad,
        encoded_grad,
        g_qkv,
        g_so,
        g_cq,
        g_ckv,
        g_co,
        g_fi,
        g_fo,
        d_bias,
        d_gain,
        d_inner,
    )


def solution(mesh):
    whole = P("fsdp", "ctx", None)
    matrix = P("fsdp", None)
    ids = P("fsdp", "ctx")
    table = P(None, "fsdp")
    return jax.shard_map(
        body,
        mesh=mesh,
        in_specs=(whole, whole, whole, ids, ids) + (matrix,) * 7 + (table, table, P("fsdp")),
        out_specs=(whole,) * 3 + (matrix,) * 7 + (table, table, P("fsdp")),
        check_vma=False,
    )
```

time: 500 us -> 332 us (0.66)
  local copies, waits for them, and re-layouts: 103 us -> 22.5 us
  Pallas kernels: 0 us -> 53.6 us
  other arithmetic: 64.7 us -> 15.9 us
  matrix products: 36.5 us -> 0.32 us
  starting transfers between devices: 102 us -> 72.5 us
  blocking collectives: 16.2 us -> 0 us
  waiting for transfers between devices: 168 us -> 161 us
    pallas_call x0 -> x22, Pallas kernels: none -> 53.6 us  [the longest x21 50.7 us: call(): pl.pallas_call(kernel, out_shape=outs, cost_estimate=cost(flops, *operand...]
    ppermute x32 -> x27, waiting for transfers between devices: 120 us -> 81.6 us  [flip_ctx(): return lax.ppermute(value, 'ctx', [(i, i ^ bit) for i in range(count)])]
    ppermute x36 -> x38, waiting for transfers between devices: 48.4 us -> 78.9 us  [flip_model(): return lax.ppermute(value, 'fsdp', [(i, i ^ bit) for i in range(count)])]
    dot_general x40 -> x0, matrix products: 23.9 us -> none  [the longest x20 13.3 us: mm_tn(): lax.dot_general(left, right, (((0,), (0,)), ((), ())), preferred_element_...]
    convert_element_type x45 -> x10, other arithmetic: 23.1 us -> 1.64 us  [the longest x1 0.81 us: body(): small_low = small.astype(LOW).astype(WIDE)]
    reshape x16 -> x1, local copies, waits for them, and re-layouts: 20 us -> 0.76 us  [body(): inner_sum.reshape(-1, local)]
    all_gather x1 -> x0, blocking collectives: 16.2 us -> none  [body(): small_all = lax.all_gather(small, 'fsdp', axis=1, tiled=True).astype(WIDE)]
    dynamic_slice x7 -> x0, local copies, waits for them, and re-layouts: 14.7 us -> none  [the longest x1 6.46 us: rest_block(): piece_kv = lax.dynamic_index_in_dim(ckv_low, own ^ k, 2, keepdims=False)]
  transfers between devices with their start and end apart: 74 -> 69, of which waited for: 33 -> 34; matrix products, arithmetic and copies ran while one was open for 29% -> 7% of each run, Pallas kernels for 0% -> 11%
where the time goes in v2:
time: 332 us; the launch traced here: 327 us
  waiting for transfers between devices  161 us (48%)
  starting transfers between devices  72.5 us (22%)
  Pallas kernels  53.6 us (16%)
  local copies, waits for them, and re-layouts  22.5 us (7%)
  other arithmetic  15.9 us (5%)
    ppermute x27, waiting for transfers between devices, flip_ctx(): return lax.ppermute(value, 'ctx', [(i, i ^ bit) for i in range(count)])  81.6 us
    ppermute x38, waiting for transfers between devices, flip_model(): return lax.ppermute(value, 'fsdp', [(i, i ^ bit) for i in range(count)])  78.9 us
    pallas_call x21, Pallas kernels, call(): pl.pallas_call(kernel, out_shape=outs, cost_estimate=cost(flops, *operand...  50.7 us
    ppermute x38, starting transfers between devices, flip_model(): return lax.ppermute(value, 'fsdp', [(i, i ^ bit) for i in range(count)])  39.6 us
    ppermute x27, starting transfers between devices, flip_ctx(): return lax.ppermute(value, 'ctx', [(i, i ^ bit) for i in range(count)])  26.7 us
    unnamed x73, local copies, waits for them, and re-layouts  13.5 us
  transfers between devices with their start and end apart: 69, of which 34 were waited for; matrix products, arithmetic and copies ran while one was open for 7% of the time, Pallas kernels for 11%

profile of v2, /device:TPU:0, one launch (start us, length us, event | category | flops | bytes accessed | tf_op | source)
XLA Modules:
  0.0 327.3 jit_solution(15866500590444373458)
XLA Ops:
  7.8 6.2 %collective-permute-start.1 = (bf16[208,576]{1,0:T(8,128)(2,1)S(1)}, bf16[208,576]{1,0:T(8,128)(2,1)S(1)}, u32[]{:S(2)}, u32[]{:S(2)}) collective-permute-start(bf16[208,576]{1,0:T(8,128)(2,1)S(1)} %get-tuple-element.124), channel_id=1, source_target_pairs={{0,16},{8,24},{16,0},{24,8},{1,17},{9,25},{17,1},{25,9},{2,18},{10... | collective-permute-start | bytes 718856 | tf_op jit(solution)/shard_map/ppermute | solution.py:31
  13.9 10.6 %collective-permute-done.1.refs_2_ = bf16[208,576]{1,0:T(8,128)(2,1)S(1)} collective-permute-done((bf16[208,576]{1,0:T(8,128)(2,1)S(1)}, bf16[208,576]{1,0:T(8,128)(2,1)S(1)}, u32[]{:S(2)}, u32[]{:S(2)}) %collective-permute-start.1) | collective-permute-done | bytes 239648 | tf_op jit(solution)/shard_map/ppermute | solution.py:31
  24.5 2.5 collective-permute-start.2
  38.3 12.7 %collective-permute-done.4 = bf16[1,2,176,768]{3,2,1,0:T(8,128)(2,1)S(1)} collective-permute-done((bf16[1,2,176,768]{3,2,1,0:T(8,128)(2,1)S(1)}, bf16[1,2,176,768]{3,2,1,0:T(8,128)(2,1)S(1)}, u32[]{:S(2)}, u32[]{:S(2)}) %collective-permute-start.4) | collective-permute-done | bytes 540704 | tf_op jit(solution)/shard_map/ppermute | solution.py:36
  51.9 1.8 collective-permute-start.7
  54.2 10.4 %collective-permute-start.11 = (bf16[128,768]{1,0:T(8,128)(2,1)S(1)}, bf16[128,768]{1,0:T(8,128)(2,1)S(1)}, u32[]{:S(2)}, u32[]{:S(2)}) collective-permute-start(bf16[128,768]{1,0:T(8,128)(2,1)S(1)} %collective-permute-done.10.a_ref), channel_id=1, source_target_pairs={{0,16},{8,24},{16,0},{24,8},{1,17},{9,25},{17,1},{25,9},{2,18},{10... | collective-permute-start | bytes 589832 | tf_op jit(solution)/shard_map/ppermute | solution.py:31
  66.2 2.9 shard_map.248
  69.2 4.7 %shard_map.249 = (bf16[512,192]{1,0:T(8,128)(2,1)S(1)}, f32[256,768]{1,0:T(8,128)S(1)}, bf16[256,768]{1,0:T(8,128)(2,1)S(1)}) custom-call(s32[4]{0:T(128)S(1)} %pad_add_fusion.spot_ref, f32[1,1024]{1,0:T(1,128)S(1)} %get-tuple-element.134.marks_ref, bf16[512,192]{1,0:T(8,128)(2,1)S(1)} %get-tuple-element.137.q_ref, ...), custom_call_target="tpu_custom_call" | custom-call | flops 553648128 | bytes 2658304 | tf_op jit(solution)/shard_map/pallas_call | solution.py:101
  76.1 1.8 collective-permute-start.13
  79.5 8.1 %collective-permute-done.13.other_ref = bf16[256,768]{1,0:T(8,128)(2,1)S(1)} collective-permute-done((bf16[256,768]{1,0:T(8,128)(2,1)S(1)}, bf16[256,768]{1,0:T(8,128)(2,1)S(1)}, u32[]{:S(2)}, u32[]{:S(2)}) %collective-permute-start.13) | collective-permute-done | bytes 393248 | tf_op jit(solution)/shard_map/ppermute | solution.py:31
  88.1 1.7 collective-permute-done.18.b_ref.refs_1_
  89.8 3.4 %shard_map.252 = (bf16[512,192]{1,0:T(8,128)(2,1)S(1)}, bf16[512,192]{1,0:T(8,128)(2,1)S(1)}, f32[256,768]{1,0:T(8,128)S(1)}, bf16[256,768]{1,0:T(8,128)(2,1)S(1)}) custom-call(s32[4]{0:T(128)S(1)} %pad_add_fusion.spot_ref, f32[1,1024]{1,0:T(1,128)S(1)} %get-tuple-element.134.marks_ref, f32[1,256]{1,0:T(1,128)S(1)} %get-tuple-element.153.emarks_ref, ...), custom_call_target="tpu_custom_call" | custom-call | flops 301989888 | bytes 3163136 | tf_op jit(solution)/shard_map/pallas_call | solution.py:101
  95.1 1.8 collective-permute-start.20
  96.9 9.4 %collective-permute-done.20.other_ref = bf16[256,768]{1,0:T(8,128)(2,1)S(1)} collective-permute-done((bf16[256,768]{1,0:T(8,128)(2,1)S(1)}, bf16[256,768]{1,0:T(8,128)(2,1)S(1)}, u32[]{:S(2)}, u32[]{:S(2)}) %collective-permute-start.20) | collective-permute-done | bytes 393248 | tf_op jit(solution)/shard_map/ppermute | solution.py:31
  106.8 1.7 collective-permute-done.21.b_ref.x1_ref
  108.5 1.8 shard_map.254
  112.2 1.8 collective-permute-start.23
  114.0 9.4 %collective-permute-done.23.other_ref = bf16[256,768]{1,0:T(8,128)(2,1)S(1)} collective-permute-done((bf16[256,768]{1,0:T(8,128)(2,1)S(1)}, bf16[256,768]{1,0:T(8,128)(2,1)S(1)}, u32[]{:S(2)}, u32[]{:S(2)}) %collective-permute-start.23) | collective-permute-done | bytes 393248 | tf_op jit(solution)/shard_map/ppermute | solution.py:31
  124.2 1.7 collective-permute-done.25.b_ref.g1_ref
  125.9 2.0 shard_map.256
  129.8 1.8 collective-permute-start.27
  132.3 2.3 shard_map.257
  134.6 9.2 %collective-permute-done.27.other_ref = bf16[256,768]{1,0:T(8,128)(2,1)S(1)} collective-permute-done((bf16[256,768]{1,0:T(8,128)(2,1)S(1)}, bf16[256,768]{1,0:T(8,128)(2,1)S(1)}, u32[]{:S(2)}, u32[]{:S(2)}) %collective-permute-start.27) | collective-permute-done | bytes 393248 | tf_op jit(solution)/shard_map/ppermute | solution.py:31
  144.4 1.7 collective-permute-done.28.b_ref.refs_7_
  146.1 4.0 %shard_map.259 = (bf16[512,192]{1,0:T(8,128)(2,1)S(1)}, bf16[256,384]{1,0:T(8,128)(2,1)S(1)}, f32[256,768]{1,0:T(8,128)S(1)}, bf16[256,768]{1,0:T(8,128)(2,1)S(1)}, f32[2,192]{1,0:T(2,128)S(1)}) custom-call(s32[4]{0:T(128)S(1)} %pad_add_fusion.spot_ref, f32[1,1024]{1,0:T(1,128)S(1)} %get-tuple-element.134.marks_ref, ...), custom_call_target="tpu_custom_call" | custom-call | flops 301989888 | bytes 3348992 | tf_op jit(solution)/shard_map/pallas_call | solution.py:101
  152.0 3.7 %collective-permute-start.30 = (bf16[256,768]{1,0:T(8,128)(2,1)S(1)}, bf16[256,768]{1,0:T(8,128)(2,1)S(1)}, u32[]{:S(2)}, u32[]{:S(2)}) collective-permute-start(bf16[256,768]{1,0:T(8,128)(2,1)S(1)} %get-tuple-element.233), channel_id=1, source_target_pairs={{0,16},{8,24},{16,0},{24,8},{1,17},{9,25},{17,1},{25,9},{2,18},{10... | collective-permute-start | bytes 1179656 | tf_op jit(solution)/shard_map/ppermute | solution.py:31
  157.2 1.8 shard_map.260
  159.0 6.1 %collective-permute-done.30.other_ref = bf16[256,768]{1,0:T(8,128)(2,1)S(1)} collective-permute-done((bf16[256,768]{1,0:T(8,128)(2,1)S(1)}, bf16[256,768]{1,0:T(8,128)(2,1)S(1)}, u32[]{:S(2)}, u32[]{:S(2)}) %collective-permute-start.30) | collective-permute-done | bytes 393248 | tf_op jit(solution)/shard_map/ppermute | solution.py:31
  180.1 9.8 %shard_map.262 = (bf16[512,192]{1,0:T(8,128)(2,1)S(1)}, bf16[1024,384]{1,0:T(8,128)(2,1)S(1)}, f32[2,192]{1,0:T(2,128)S(1)}) custom-call(s32[4]{0:T(128)S(1)} %pad_add_fusion.spot_ref, f32[1,1024]{1,0:T(1,128)S(1)} %get-tuple-element.134.marks_ref, bf16[256,768]{1,0:T(8,128)(2,1)} %get-tuple-element.191.a_ref.refs_5_, ...), custom_call_target="tpu_custom_call" | custom-call | flops 1006632960 | bytes 3053056 | tf_op jit(solution)/shard_map/pallas_call | solution.py:101
  190.0 3.6 %shard_map.263 = (f32[2,4,48,768]{3,2,1,0:T(8,128)S(1)}, bf16[2,4,48,768]{3,2,1,0:T(8,128)(2,1)S(1)}) custom-call(s32[4]{0:T(128)S(1)} %pad_add_fusion.spot_ref, bf16[1024,768]{1,0:T(8,128)(2,1)S(1)} %get-tuple-element.133.r_ref.refs_0_.refs_2_, bf16[512,192]{1,0:T(8,128)(2,1)S(1)} %get-tuple-element.192.refs_1_.q_ref, ...), custom_call_target="tpu_custom_call" | custom-call | flops 905969664 | bytes 6881280 | tf_op jit(solution)/shard_map/pallas_call | solution.py:101
  198.0 1.7 collective-permute-start.47
  201.2 8.2 %collective-permute-done.32 = bf16[2,4,48,768]{3,2,1,0:T(8,128)(2,1)S(1)} collective-permute-done((bf16[2,4,48,768]{3,2,1,0:T(8,128)(2,1)S(1)}, bf16[2,4,48,768]{3,2,1,0:T(8,128)(2,1)S(1)}, u32[]{:S(2)}, u32[]{:S(2)}) %collective-permute-start.32) | collective-permute-done | bytes 589856 | tf_op jit(solution)/shard_map/ppermute | solution.py:36
  209.6 14.9 %collective-permute-done.52 = bf16[2,4,48,768]{3,2,1,0:T(8,128)(2,1)S(1)} collective-permute-done((bf16[2,4,48,768]{3,2,1,0:T(8,128)(2,1)S(1)}, bf16[2,4,48,768]{3,2,1,0:T(8,128)(2,1)S(1)}, u32[]{:S(2)}, u32[]{:S(2)}) %collective-permute-start.52) | collective-permute-done | bytes 589856 | tf_op jit(solution)/shard_map/ppermute | solution.py:36
  226.6 2.0 collective-permute-start.58
  230.1 7.1 %collective-permute-done.36 = bf16[1,128,384]{2,1,0:T(8,128)(2,1)S(1)} collective-permute-done((bf16[1,128,384]{2,1,0:T(8,128)(2,1)S(1)}, bf16[1,128,384]{2,1,0:T(8,128)(2,1)S(1)}, u32[]{:S(2)}, u32[]{:S(2)}) %collective-permute-start.36) | collective-permute-done | bytes 98336 | tf_op jit(solution)/shard_map/ppermute | solution.py:36
  240.2 3.0 collective-permute-done.38
  243.2 8.7 %collective-permute-done.53 = bf16[4,48,768]{2,1,0:T(8,128)(2,1)S(1)} collective-permute-done((bf16[4,48,768]{2,1,0:T(8,128)(2,1)S(1)}, bf16[4,48,768]{2,1,0:T(8,128)(2,1)S(1)}, u32[]{:S(2)}, u32[]{:S(2)}) %collective-permute-start.53) | collective-permute-done | bytes 294944 | tf_op jit(solution)/shard_map/ppermute | solution.py:36
  258.1 2.3 collective-permute-done.54
  260.4 6.2 %collective-permute-done.41 = bf16[4,48,768]{2,1,0:T(8,128)(2,1)S(1)} collective-permute-done((bf16[4,48,768]{2,1,0:T(8,128)(2,1)S(1)}, bf16[4,48,768]{2,1,0:T(8,128)(2,1)S(1)}, u32[]{:S(2)}, u32[]{:S(2)}) %collective-permute-start.41) | collective-permute-done | bytes 294944 | tf_op jit(solution)/shard_map/ppermute | solution.py:36
  269.0 4.1 %collective-permute-done.42 = bf16[2,48,768]{2,1,0:T(8,128)(2,1)S(1)} collective-permute-done((bf16[2,48,768]{2,1,0:T(8,128)(2,1)S(1)}, bf16[2,48,768]{2,1,0:T(8,128)(2,1)S(1)}, u32[]{:S(2)}, u32[]{:S(2)}) %collective-permute-start.42) | collective-permute-done | bytes 147488 | tf_op jit(solution)/shard_map/ppermute | solution.py:31
  276.6 5.1 %collective-permute-done.56.b_ref = bf16[4,48,768]{2,1,0:T(8,128)(2,1)S(1)} collective-permute-done((bf16[4,48,768]{2,1,0:T(8,128)(2,1)S(1)}, bf16[4,48,768]{2,1,0:T(8,128)(2,1)S(1)}, u32[]{:S(2)}, u32[]{:S(2)}) %collective-permute-start.56) | collective-permute-done | bytes 294944 | tf_op jit(solution)/shard_map/ppermute | solution.py:36
  286.0 6.1 %collective-permute-done.67 = f32[17,192]{1,0:T(8,128)S(1)} collective-permute-done((f32[17,192]{1,0:T(8,128)S(1)}, f32[17,192]{1,0:T(8,128)S(1)}, u32[]{:S(2)}, u32[]{:S(2)}) %collective-permute-start.67) | collective-permute-done | bytes 13088 | tf_op jit(solution)/shard_map/ppermute | solution.py:36
  292.9 9.5 %collective-permute-done.68 = f32[17,192]{1,0:T(8,128)S(1)} collective-permute-done((f32[17,192]{1,0:T(8,128)S(1)}, f32[17,192]{1,0:T(8,128)S(1)}, u32[]{:S(2)}, u32[]{:S(2)}) %collective-permute-start.68) | collective-permute-done | bytes 13088 | tf_op jit(solution)/shard_map/ppermute | solution.py:36
  302.4 3.5 %collective-permute-start.39 = (bf16[160,768]{1,0:T(8,128)(2,1)}, bf16[160,768]{1,0:T(8,128)(2,1)}, u32[]{:S(2)}, u32[]{:S(2)}) collective-permute-start(bf16[160,768]{1,0:T(8,128)(2,1)} %pad_maximum_fusion.7), channel_id=1, source_target_pairs={{0,0},{1,1},{2,8},{3,9},{4,16},{5,17},{6,24},{7,25},{8,2},{9,3},{1... | collective-permute-start | bytes 737288 | tf_op jit(solution)/shard_map/ppermute | solution.py:48
  310.0 2.6 stack.119
  313.9 3.0 shard_map.267
  319.3 3.3 %shard_map.266 = (f32[192,768]{1,0:T(8,128)}, f32[192,1536]{1,0:T(8,128)}, f32[192,768]{1,0:T(8,128)}) custom-call(s32[4]{0:T(128)S(1)} %pad_add_fusion.spot_ref, bf16[4,48,768]{2,1,0:T(8,128)(2,1)S(1)} %fusion.27.a_ref, bf16[4,48,768]{2,1,0:T(8,128)(2,1)S(1)} %collective-permute-done.56.b_ref, bf16[2,4,48,768]{3,2,1,0:T(8,128)(2,1)} %collective-permute-done.57.c_ref), custom_call_target="tpu_custom_call" | custom-call | bytes 3538944 | tf_op jit(solution)/shard_map/pallas_call | solution.py:101
  323.1 3.3 %shard_map.265 = (f32[192,2304]{1,0:T(8,128)}, f32[192,768]{1,0:T(8,128)}) custom-call(s32[4]{0:T(128)S(1)} %pad_add_fusion.spot_ref, bf16[4,48,768]{2,1,0:T(8,128)(2,1)S(1)} %fusion.23.a_ref, bf16[4,48,768]{2,1,0:T(8,128)(2,1)S(1)} %collective-permute-done.44.b_ref, bf16[2,4,48,768]{3,2,1,0:T(8,128)(2,1)} %collective-permute-done.45.c_ref), custom_call_target="tpu_custom_call" | custom-call | bytes 3538944 | tf_op jit(solution)/shard_map/pallas_call | solution.py:101
  (275 shorter events, 90.5 us)
Async XLA Ops:
  3.1 21.4 %collective-permute-start = (bf16[176,768]{1,0:T(8,128)(2,1)S(1)}, bf16[176,768]{1,0:T(8,128)(2,1)}, u32[]{:S(2)}, u32[]{:S(2)}) collective-permute-start(bf16[176,768]{1,0:T(8,128)(2,1)S(1)} %fusion.33), channel_id=1, source_target_pairs={{0,0},{1,1},{2,8},{3,9},{4,16},{5,17},{6,24},{7,25},{8,2},{9,3},{1... | collective-permute-start | bytes 811016 | tf_op jit(solution)/shard_map/ppermute | solution.py:48
  7.8 16.7 %collective-permute-start.1 = (bf16[208,576]{1,0:T(8,128)(2,1)S(1)}, bf16[208,576]{1,0:T(8,128)(2,1)S(1)}, u32[]{:S(2)}, u32[]{:S(2)}) collective-permute-start(bf16[208,576]{1,0:T(8,128)(2,1)S(1)} %get-tuple-element.124), channel_id=1, source_target_pairs={{0,16},{8,24},{16,0},{24,8},{1,17},{9,25},{17,1},{25,9},{2,18},{10... | collective-permute-start | bytes 718856 | tf_op jit(solution)/shard_map/ppermute | solution.py:31
  24.5 11.5 %collective-permute-start.2 = (bf16[176,768]{1,0:T(8,128)(2,1)}, bf16[176,768]{1,0:T(8,128)(2,1)S(1)}, u32[]{:S(2)}, u32[]{:S(2)}) collective-permute-start(bf16[176,768]{1,0:T(8,128)(2,1)} %collective-permute-done), channel_id=1, source_target_pairs={{0,16},{8,24},{16,0},{24,8},{1,17},{9,25},{17,1},{25,9},{2,18},{10... | collective-permute-start | bytes 811016 | tf_op jit(solution)/shard_map/ppermute | solution.py:31
  27.0 10.2 %collective-permute-start.3 = (bf16[208,576]{1,0:T(8,128)(2,1)S(1)}, bf16[208,576]{1,0:T(8,128)(2,1)S(1)}, u32[]{:S(2)}, u32[]{:S(2)}) collective-permute-start(bf16[208,576]{1,0:T(8,128)(2,1)S(1)} %collective-permute-done.1.refs_2_), channel_id=1, source_target_pairs={{0,1},{1,0},{2,3},{3,2},{4,5},{5,4},{6,7},{7,6},{8,9},{9,8},{10,11... | collective-permute-start | bytes 718856 | tf_op jit(solution)/shard_map/ppermute | solution.py:36
  37.2 13.8 %collective-permute-start.4 = (bf16[1,2,176,768]{3,2,1,0:T(8,128)(2,1)S(1)}, bf16[1,2,176,768]{3,2,1,0:T(8,128)(2,1)S(1)}, u32[]{:S(2)}, u32[]{:S(2)}) collective-permute-start(bf16[1,2,176,768]{3,2,1,0:T(8,128)(2,1)S(1)} %maximum_bitcast_fusion), channel_id=1, source_target_pairs={{0,1},{1,0},{2,3},{3,2},{4,5},{5,4},{6,7},{7,6},{8,9},{9,8},{10,11... | collective-permute-start | bytes 1622024 | tf_op jit(solution)/shard_map/ppermute | solution.py:36
  37.8 13.5 %collective-permute-start.5 = (bf16[192,1344]{1,0:T(8,128)(2,1)S(1)}, bf16[192,1344]{1,0:T(8,128)(2,1)S(1)}, u32[]{:S(2)}, u32[]{:S(2)}) collective-permute-start(bf16[192,1344]{1,0:T(8,128)(2,1)S(1)} %get-tuple-element.129), channel_id=1, source_target_pairs={{0,16},{8,24},{16,0},{24,8},{1,17},{9,25},{17,1},{25,9},{2,18},{10... | collective-permute-start | bytes 1548296 | tf_op jit(solution)/shard_map/ppermute | solution.py:31
  51.2 15.0 %collective-permute-start.6 = (bf16[2,2,176,768]{3,2,1,0:T(8,128)(2,1)S(1)}, bf16[2,2,176,768]{3,2,1,0:T(8,128)(2,1)S(1)}, u32[]{:S(2)}, u32[]{:S(2)}) collective-permute-start(bf16[2,2,176,768]{3,2,1,0:T(8,128)(2,1)S(1)} %pad_maximum_fusion.a_ref), channel_id=1, source_target_pairs={{0,8},{8,0},{16,24},{24,16},{1,9},{9,1},{17,25},{25,17},{2,10},{10... | collective-permute-start | bytes 3244040 | tf_op jit(solution)/shard_map/ppermute | solution.py:31
  51.9 12.8 %collective-permute-start.7 = (bf16[208,576]{1,0:T(8,128)(2,1)S(1)}, bf16[208,576]{1,0:T(8,128)(2,1)S(1)}, u32[]{:S(2)}, u32[]{:S(2)}) collective-permute-start(bf16[208,576]{1,0:T(8,128)(2,1)S(1)} %get-tuple-element.132), channel_id=1, source_target_pairs={{0,8},{8,0},{16,24},{24,16},{1,9},{9,1},{17,25},{25,17},{2,10},{10... | collective-permute-start | bytes 718856 | tf_op jit(solution)/shard_map/ppermute | solution.py:31
  53.7 12.5 %collective-permute-start.8 = (bf16[208,576]{1,0:T(8,128)(2,1)S(1)}, bf16[208,576]{1,0:T(8,128)(2,1)S(1)}, u32[]{:S(2)}, u32[]{:S(2)}) collective-permute-start(bf16[208,576]{1,0:T(8,128)(2,1)S(1)} %collective-permute-done.1.refs_2_), channel_id=1, source_target_pairs={{0,8},{8,0},{16,24},{24,16},{1,9},{9,1},{17,25},{25,17},{2,10},{10... | collective-permute-start | bytes 718856 | tf_op jit(solution)/shard_map/ppermute | solution.py:31
  53.8 12.4 %collective-permute-start.9 = (bf16[208,576]{1,0:T(8,128)(2,1)S(1)}, bf16[208,576]{1,0:T(8,128)(2,1)S(1)}, u32[]{:S(2)}, u32[]{:S(2)}) collective-permute-start(bf16[208,576]{1,0:T(8,128)(2,1)S(1)} %collective-permute-done.3.refs_3_), channel_id=1, source_target_pairs={{0,8},{8,0},{16,24},{24,16},{1,9},{9,1},{17,25},{25,17},{2,10},{10... | collective-permute-start | bytes 718856 | tf_op jit(solution)/shard_map/ppermute | solution.py:31
  54.2 19.6 %collective-permute-start.11 = (bf16[128,768]{1,0:T(8,128)(2,1)S(1)}, bf16[128,768]{1,0:T(8,128)(2,1)S(1)}, u32[]{:S(2)}, u32[]{:S(2)}) collective-permute-start(bf16[128,768]{1,0:T(8,128)(2,1)S(1)} %collective-permute-done.10.a_ref), channel_id=1, source_target_pairs={{0,16},{8,24},{16,0},{24,8},{1,17},{9,25},{17,1},{25,9},{2,18},{10... | collective-permute-start | bytes 589832 | tf_op jit(solution)/shard_map/ppermute | solution.py:31
  64.7 11.2 %collective-permute-start.15 = (bf16[192,1344]{1,0:T(8,128)(2,1)S(1)}, bf16[192,1344]{1,0:T(8,128)(2,1)S(1)}, u32[]{:S(2)}, u32[]{:S(2)}) collective-permute-start(bf16[192,1344]{1,0:T(8,128)(2,1)S(1)} %collective-permute-done.5.refs_2_), channel_id=1, source_target_pairs={{0,1},{1,0},{2,3},{3,2},{4,5},{5,4},{6,7},{7,6},{8,9},{9,8},{10,11... | collective-permute-start | bytes 1548296 | tf_op jit(solution)/shard_map/ppermute | solution.py:36
  76.1 11.6 %collective-permute-start.13 = (bf16[256,768]{1,0:T(8,128)(2,1)S(1)}, bf16[256,768]{1,0:T(8,128)(2,1)S(1)}, u32[]{:S(2)}, u32[]{:S(2)}) collective-permute-start(bf16[256,768]{1,0:T(8,128)(2,1)S(1)} %get-tuple-element.243), channel_id=1, source_target_pairs={{0,16},{8,24},{16,0},{24,8},{1,17},{9,25},{17,1},{25,9},{2,18},{10... | collective-permute-start | bytes 1179656 | tf_op jit(solution)/shard_map/ppermute | solution.py:31
  95.1 11.2 %collective-permute-start.20 = (bf16[256,768]{1,0:T(8,128)(2,1)S(1)}, bf16[256,768]{1,0:T(8,128)(2,1)S(1)}, u32[]{:S(2)}, u32[]{:S(2)}) collective-permute-start(bf16[256,768]{1,0:T(8,128)(2,1)S(1)} %get-tuple-element.239), channel_id=1, source_target_pairs={{0,16},{8,24},{16,0},{24,8},{1,17},{9,25},{17,1},{25,9},{2,18},{10... | collective-permute-start | bytes 1179656 | tf_op jit(solution)/shard_map/ppermute | solution.py:31
  112.2 11.2 %collective-permute-start.23 = (bf16[256,768]{1,0:T(8,128)(2,1)S(1)}, bf16[256,768]{1,0:T(8,128)(2,1)S(1)}, u32[]{:S(2)}, u32[]{:S(2)}) collective-permute-start(bf16[256,768]{1,0:T(8,128)(2,1)S(1)} %get-tuple-element.237), channel_id=1, source_target_pairs={{0,16},{8,24},{16,0},{24,8},{1,17},{9,25},{17,1},{25,9},{2,18},{10... | collective-permute-start | bytes 1179656 | tf_op jit(solution)/shard_map/ppermute | solution.py:31
  129.8 14.0 %collective-permute-start.27 = (bf16[256,768]{1,0:T(8,128)(2,1)S(1)}, bf16[256,768]{1,0:T(8,128)(2,1)S(1)}, u32[]{:S(2)}, u32[]{:S(2)}) collective-permute-start(bf16[256,768]{1,0:T(8,128)(2,1)S(1)} %get-tuple-element.235), channel_id=1, source_target_pairs={{0,16},{8,24},{16,0},{24,8},{1,17},{9,25},{17,1},{25,9},{2,18},{10... | collective-permute-start | bytes 1179656 | tf_op jit(solution)/shard_map/ppermute | solution.py:31
  150.3 16.1 %collective-permute-start.50 = (bf16[2,4,48,768]{3,2,1,0:T(8,128)(2,1)S(1)}, bf16[2,4,48,768]{3,2,1,0:T(8,128)(2,1)S(1)}, u32[]{:S(2)}, u32[]{:S(2)}) collective-permute-start(bf16[2,4,48,768]{3,2,1,0:T(8,128)(2,1)S(1)} %get-tuple-element.213), channel_id=1, source_target_pairs={{0,2},{1,3},{2,0},{3,1},{4,6},{5,7},{6,4},{7,5},{8,10},{9,11},{10,... | collective-permute-start | bytes 1769480 | tf_op jit(solution)/shard_map/ppermute | solution.py:36
  152.0 13.1 %collective-permute-start.30 = (bf16[256,768]{1,0:T(8,128)(2,1)S(1)}, bf16[256,768]{1,0:T(8,128)(2,1)S(1)}, u32[]{:S(2)}, u32[]{:S(2)}) collective-permute-start(bf16[256,768]{1,0:T(8,128)(2,1)S(1)} %get-tuple-element.233), channel_id=1, source_target_pairs={{0,16},{8,24},{16,0},{24,8},{1,17},{9,25},{17,1},{25,9},{2,18},{10... | collective-permute-start | bytes 1179656 | tf_op jit(solution)/shard_map/ppermute | solution.py:31
  155.7 15.1 %collective-permute-start.48 = (bf16[2,4,48,768]{3,2,1,0:T(8,128)(2,1)S(1)}, bf16[2,4,48,768]{3,2,1,0:T(8,128)(2,1)S(1)}, u32[]{:S(2)}, u32[]{:S(2)}) collective-permute-start(bf16[2,4,48,768]{3,2,1,0:T(8,128)(2,1)S(1)} %get-tuple-element.210), channel_id=1, source_target_pairs={{0,1},{1,0},{2,3},{3,2},{4,5},{5,4},{6,7},{7,6},{8,9},{9,8},{10,11... | collective-permute-start | bytes 1769480 | tf_op jit(solution)/shard_map/ppermute | solution.py:36
  166.4 9.7 %collective-permute-start.31 = (bf16[256,768]{1,0:T(8,128)(2,1)}, bf16[256,768]{1,0:T(8,128)(2,1)}, u32[]{:S(2)}, u32[]{:S(2)}) collective-permute-start(bf16[256,768]{1,0:T(8,128)(2,1)} %get-tuple-element.191.a_ref.refs_5_), channel_id=1, source_target_pairs={{0,8},{8,0},{16,24},{24,16},{1,9},{9,1},{17,25},{25,17},{2,10},{10... | collective-permute-start | bytes 1179656 | tf_op jit(solution)/shard_map/ppermute | solution.py:31
  168.0 26.2 %collective-permute-start.51 = (bf16[4,48,768]{2,1,0:T(8,128)(2,1)}, bf16[4,48,768]{2,1,0:T(8,128)(2,1)}, u32[]{:S(2)}, u32[]{:S(2)}) collective-permute-start(bf16[4,48,768]{2,1,0:T(8,128)(2,1)} %fusion.32), channel_id=1, source_target_pairs={{0,1},{1,0},{2,3},{3,2},{4,5},{5,4},{6,7},{7,6},{8,9},{9,8},{10,11... | collective-permute-start | bytes 884744 | tf_op jit(solution)/shard_map/ppermute | solution.py:36
  172.0 22.2 %collective-permute-start.49 = (bf16[4,48,768]{2,1,0:T(8,128)(2,1)}, bf16[4,48,768]{2,1,0:T(8,128)(2,1)}, u32[]{:S(2)}, u32[]{:S(2)}) collective-permute-start(bf16[4,48,768]{2,1,0:T(8,128)(2,1)} %fusion.30), channel_id=1, source_target_pairs={{0,2},{1,3},{2,0},{3,1},{4,6},{5,7},{6,4},{7,5},{8,10},{9,11},{10,... | collective-permute-start | bytes 884744 | tf_op jit(solution)/shard_map/ppermute | solution.py:36
  173.8 23.0 %collective-permute-start.46 = (bf16[2,4,48,768]{3,2,1,0:T(8,128)(2,1)}, bf16[2,4,48,768]{3,2,1,0:T(8,128)(2,1)S(1)}, u32[]{:S(2)}, u32[]{:S(2)}) collective-permute-start(bf16[2,4,48,768]{3,2,1,0:T(8,128)(2,1)} %copy-done.16), channel_id=1, source_target_pairs={{0,1},{1,0},{2,3},{3,2},{4,5},{5,4},{6,7},{7,6},{8,9},{9,8},{10,11... | collective-permute-start | bytes 1769480 | tf_op jit(solution)/shard_map/ppermute | solution.py:36
  193.6 15.7 %collective-permute-start.32 = (bf16[2,4,48,768]{3,2,1,0:T(8,128)(2,1)S(1)}, bf16[2,4,48,768]{3,2,1,0:T(8,128)(2,1)S(1)}, u32[]{:S(2)}, u32[]{:S(2)}) collective-permute-start(bf16[2,4,48,768]{3,2,1,0:T(8,128)(2,1)S(1)} %get-tuple-element.196), channel_id=1, source_target_pairs={{0,1},{1,0},{2,3},{3,2},{4,5},{5,4},{6,7},{7,6},{8,9},{9,8},{10,11... | collective-permute-start | bytes 1769480 | tf_op jit(solution)/shard_map/ppermute | solution.py:36
  195.5 29.0 %collective-permute-start.52 = (bf16[2,4,48,768]{3,2,1,0:T(8,128)(2,1)S(1)}, bf16[2,4,48,768]{3,2,1,0:T(8,128)(2,1)S(1)}, u32[]{:S(2)}, u32[]{:S(2)}) collective-permute-start(bf16[2,4,48,768]{3,2,1,0:T(8,128)(2,1)S(1)} %pad_maximum_fusion.2), channel_id=1, source_target_pairs={{0,4},{1,5},{2,6},{3,7},{4,0},{5,1},{6,2},{7,3},{8,12},{9,13},{10,... | collective-permute-start | bytes 1769480 | tf_op jit(solution)/shard_map/ppermute | solution.py:36
  198.0 30.7 %collective-permute-start.47 = (bf16[4,48,768]{2,1,0:T(8,128)(2,1)S(1)}, bf16[4,48,768]{2,1,0:T(8,128)(2,1)S(1)}, u32[]{:S(2)}, u32[]{:S(2)}) collective-permute-start(bf16[4,48,768]{2,1,0:T(8,128)(2,1)S(1)} %fusion.28), channel_id=1, source_target_pairs={{0,2},{1,3},{2,0},{3,1},{4,6},{5,7},{6,4},{7,5},{8,10},{9,11},{10,... | collective-permute-start | bytes 884744 | tf_op jit(solution)/shard_map/ppermute | solution.py:36
  224.7 31.6 %collective-permute-start.33 = (bf16[1,512,384]{2,1,0:T(8,128)(2,1)S(1)}, bf16[1,512,384]{2,1,0:T(8,128)(2,1)S(1)}, u32[]{:S(2)}, u32[]{:S(2)}) collective-permute-start(bf16[1,512,384]{2,1,0:T(8,128)(2,1)S(1)} %slice_bitcast_fusion.4), channel_id=1, source_target_pairs={{0,1},{1,0},{2,3},{3,2},{4,5},{5,4},{6,7},{7,6},{8,9},{9,8},{10,11... | collective-permute-start | bytes 1179656 | tf_op jit(solution)/shard_map/ppermute | solution.py:36
  226.3 25.7 %collective-permute-start.40 = (bf16[4,48,768]{2,1,0:T(8,128)(2,1)S(1)}, bf16[4,48,768]{2,1,0:T(8,128)(2,1)S(1)}, u32[]{:S(2)}, u32[]{:S(2)}) collective-permute-start(bf16[4,48,768]{2,1,0:T(8,128)(2,1)S(1)} %fusion.19), channel_id=1, source_target_pairs={{0,2},{1,3},{2,0},{3,1},{4,6},{5,7},{6,4},{7,5},{8,10},{9,11},{10,... | collective-permute-start | bytes 884744 | tf_op jit(solution)/shard_map/ppermute | solution.py:36
  226.3 11.3 %collective-permute-start.60 = (bf16[2,48,768]{2,1,0:T(8,128)(2,1)S(1)}, bf16[2,48,768]{2,1,0:T(8,128)(2,1)S(1)}, u32[]{:S(2)}, u32[]{:S(2)}) collective-permute-start(bf16[2,48,768]{2,1,0:T(8,128)(2,1)S(1)} %slice_bitcast_fusion.5), channel_id=1, source_target_pairs={{0,16},{8,24},{16,0},{24,8},{1,17},{9,25},{17,1},{25,9},{2,18},{10... | collective-permute-start | bytes 442376 | tf_op jit(solution)/shard_map/ppermute | solution.py:31
  226.6 27.2 %collective-permute-start.58 = (bf16[4,48,768]{2,1,0:T(8,128)(2,1)S(1)}, bf16[4,48,768]{2,1,0:T(8,128)(2,1)S(1)}, u32[]{:S(2)}, u32[]{:S(2)}) collective-permute-start(bf16[4,48,768]{2,1,0:T(8,128)(2,1)S(1)} %get-tuple-element.248.oa_ref), channel_id=1, source_target_pairs={{0,2},{1,3},{2,0},{3,1},{4,6},{5,7},{6,4},{7,5},{8,10},{9,11},{10,... | collective-permute-start | bytes 884744 | tf_op jit(solution)/shard_map/ppermute | solution.py:36
  228.7 8.5 %collective-permute-start.36 = (bf16[1,128,384]{2,1,0:T(8,128)(2,1)S(1)}, bf16[1,128,384]{2,1,0:T(8,128)(2,1)S(1)}, u32[]{:S(2)}, u32[]{:S(2)}) collective-permute-start(bf16[1,128,384]{2,1,0:T(8,128)(2,1)S(1)} %slice_bitcast_fusion.6), channel_id=1, source_target_pairs={{0,1},{1,0},{2,3},{3,2},{4,5},{5,4},{6,7},{7,6},{8,9},{9,8},{10,11... | collective-permute-start | bytes 294920 | tf_op jit(solution)/shard_map/ppermute | solution.py:36
  237.3 14.6 %collective-permute-start.53 = (bf16[4,48,768]{2,1,0:T(8,128)(2,1)S(1)}, bf16[4,48,768]{2,1,0:T(8,128)(2,1)S(1)}, u32[]{:S(2)}, u32[]{:S(2)}) collective-permute-start(bf16[4,48,768]{2,1,0:T(8,128)(2,1)S(1)} %fusion.5), channel_id=1, source_target_pairs={{0,4},{1,5},{2,6},{3,7},{4,0},{5,1},{6,2},{7,3},{8,12},{9,13},{10,... | collective-permute-start | bytes 884744 | tf_op jit(solution)/shard_map/ppermute | solution.py:36
  243.2 9.0 %collective-permute-start.61 = (bf16[2,48,768]{2,1,0:T(8,128)(2,1)S(1)}, bf16[2,48,768]{2,1,0:T(8,128)(2,1)S(1)}, u32[]{:S(2)}, u32[]{:S(2)}) collective-permute-start(bf16[2,48,768]{2,1,0:T(8,128)(2,1)S(1)} %pad_maximum_fusion.10), channel_id=1, source_target_pairs={{0,8},{8,0},{16,24},{24,16},{1,9},{9,1},{17,25},{25,17},{2,10},{10... | collective-permute-start | bytes 442376 | tf_op jit(solution)/shard_map/ppermute | solution.py:31
  252.1 14.5 %collective-permute-start.41 = (bf16[4,48,768]{2,1,0:T(8,128)(2,1)S(1)}, bf16[4,48,768]{2,1,0:T(8,128)(2,1)S(1)}, u32[]{:S(2)}, u32[]{:S(2)}) collective-permute-start(bf16[4,48,768]{2,1,0:T(8,128)(2,1)S(1)} %fusion.15), channel_id=1, source_target_pairs={{0,4},{1,5},{2,6},{3,7},{4,0},{5,1},{6,2},{7,3},{8,12},{9,13},{10,... | collective-permute-start | bytes 884744 | tf_op jit(solution)/shard_map/ppermute | solution.py:36
  252.3 14.4 %collective-permute-start.62 = (bf16[4,48,768]{2,1,0:T(8,128)(2,1)S(1)}, bf16[4,48,768]{2,1,0:T(8,128)(2,1)S(1)}, u32[]{:S(2)}, u32[]{:S(2)}) collective-permute-start(bf16[4,48,768]{2,1,0:T(8,128)(2,1)S(1)} %get-tuple-element.250.ia_ref), channel_id=1, source_target_pairs={{0,1},{1,0},{2,3},{3,2},{4,5},{5,4},{6,7},{7,6},{8,9},{9,8},{10,11... | collective-permute-start | bytes 884744 | tf_op jit(solution)/shard_map/ppermute | solution.py:36
  254.7 59.2 %collective-permute-start.59 = (bf16[2,4,48,768]{3,2,1,0:T(8,128)(2,1)}, bf16[2,4,48,768]{3,2,1,0:T(8,128)(2,1)S(1)}, u32[]{:S(2)}, u32[]{:S(2)}) collective-permute-start(bf16[2,4,48,768]{3,2,1,0:T(8,128)(2,1)} %pad_maximum_fusion.4), channel_id=1, source_target_pairs={{0,1},{1,0},{2,3},{3,2},{4,5},{5,4},{6,7},{7,6},{8,9},{9,8},{10,11... | collective-permute-start | bytes 1769480 | tf_op jit(solution)/shard_map/ppermute | solution.py:36
  256.5 27.3 %collective-permute-start.66 = (f32[17,192]{1,0:T(8,128)S(1)}, f32[17,192]{1,0:T(8,128)S(1)}, u32[]{:S(2)}, u32[]{:S(2)}) collective-permute-start(f32[17,192]{1,0:T(8,128)S(1)} %pad_maximum_fusion.12), channel_id=1, source_target_pairs={{0,1},{1,0},{2,3},{3,2},{4,5},{5,4},{6,7},{7,6},{8,9},{9,8},{10,11... | collective-permute-start | bytes 39176 | tf_op jit(solution)/shard_map/ppermute | solution.py:36
  260.4 14.3 %collective-permute-start.34 = (bf16[256,768]{1,0:T(8,128)(2,1)S(1)}, bf16[256,768]{1,0:T(8,128)(2,1)S(1)}, u32[]{:S(2)}, u32[]{:S(2)}) collective-permute-start(bf16[256,768]{1,0:T(8,128)(2,1)S(1)} %get-tuple-element.201), channel_id=1, source_target_pairs={{0,8},{8,0},{16,24},{24,16},{1,9},{9,1},{17,25},{25,17},{2,10},{10... | collective-permute-start | bytes 1179656 | tf_op jit(solution)/shard_map/ppermute | solution.py:31
  266.7 6.3 %collective-permute-start.42 = (bf16[2,48,768]{2,1,0:T(8,128)(2,1)S(1)}, bf16[2,48,768]{2,1,0:T(8,128)(2,1)S(1)}, u32[]{:S(2)}, u32[]{:S(2)}) collective-permute-start(bf16[2,48,768]{2,1,0:T(8,128)(2,1)S(1)} %slice.269), channel_id=1, source_target_pairs={{0,16},{8,24},{16,0},{24,8},{1,17},{9,25},{17,1},{25,9},{2,18},{10... | collective-permute-start | bytes 442376 | tf_op jit(solution)/shard_map/ppermute | solution.py:31
  268.9 45.0 %collective-permute-start.63 = (bf16[2,4,48,768]{3,2,1,0:T(8,128)(2,1)}, bf16[2,4,48,768]{3,2,1,0:T(8,128)(2,1)S(1)}, u32[]{:S(2)}, u32[]{:S(2)}) collective-permute-start(bf16[2,4,48,768]{3,2,1,0:T(8,128)(2,1)} %pad_maximum_fusion.5), channel_id=1, source_target_pairs={{0,2},{1,3},{2,0},{3,1},{4,6},{5,7},{6,4},{7,5},{8,10},{9,11},{10,... | collective-permute-start | bytes 1769480 | tf_op jit(solution)/shard_map/ppermute | solution.py:36
  273.0 8.6 %collective-permute-start.56 = (bf16[4,48,768]{2,1,0:T(8,128)(2,1)S(1)}, bf16[4,48,768]{2,1,0:T(8,128)(2,1)S(1)}, u32[]{:S(2)}, u32[]{:S(2)}) collective-permute-start(bf16[4,48,768]{2,1,0:T(8,128)(2,1)S(1)} %fusion.27.a_ref), channel_id=1, source_target_pairs={{0,1},{1,0},{2,3},{3,2},{4,5},{5,4},{6,7},{7,6},{8,9},{9,8},{10,11... | collective-permute-start | bytes 884744 | tf_op jit(solution)/shard_map/ppermute | solution.py:36
  276.2 7.5 %collective-permute-start.35 = (bf16[128,768]{1,0:T(8,128)(2,1)S(1)}, bf16[128,768]{1,0:T(8,128)(2,1)S(1)}, u32[]{:S(2)}, u32[]{:S(2)}) collective-permute-start(bf16[128,768]{1,0:T(8,128)(2,1)S(1)} %slice.365), channel_id=1, source_target_pairs={{0,16},{8,24},{16,0},{24,8},{1,17},{9,25},{17,1},{25,9},{2,18},{10... | collective-permute-start | bytes 589832 | tf_op jit(solution)/shard_map/ppermute | solution.py:31
  281.7 24.3 %collective-permute-start.44 = (bf16[4,48,768]{2,1,0:T(8,128)(2,1)S(1)}, bf16[4,48,768]{2,1,0:T(8,128)(2,1)S(1)}, u32[]{:S(2)}, u32[]{:S(2)}) collective-permute-start(bf16[4,48,768]{2,1,0:T(8,128)(2,1)S(1)} %fusion.23.a_ref), channel_id=1, source_target_pairs={{0,2},{1,3},{2,0},{3,1},{4,6},{5,7},{6,4},{7,5},{8,10},{9,11},{10,... | collective-permute-start | bytes 884744 | tf_op jit(solution)/shard_map/ppermute | solution.py:36
  283.8 8.4 %collective-permute-start.67 = (f32[17,192]{1,0:T(8,128)S(1)}, f32[17,192]{1,0:T(8,128)S(1)}, u32[]{:S(2)}, u32[]{:S(2)}) collective-permute-start(f32[17,192]{1,0:T(8,128)S(1)} %add.128), channel_id=1, source_target_pairs={{0,2},{1,3},{2,0},{3,1},{4,6},{5,7},{6,4},{7,5},{8,10},{9,11},{10,... | collective-permute-start | bytes 39176 | tf_op jit(solution)/shard_map/ppermute | solution.py:36
  284.8 34.5 %collective-permute-start.57 = (bf16[2,4,48,768]{3,2,1,0:T(8,128)(2,1)}, bf16[2,4,48,768]{3,2,1,0:T(8,128)(2,1)}, u32[]{:S(2)}, u32[]{:S(2)}) collective-permute-start(bf16[2,4,48,768]{3,2,1,0:T(8,128)(2,1)} %pad_maximum_fusion.3), channel_id=1, source_target_pairs={{0,2},{1,3},{2,0},{3,1},{4,6},{5,7},{6,4},{7,5},{8,10},{9,11},{10,... | collective-permute-start | bytes 1769480 | tf_op jit(solution)/shard_map/ppermute | solution.py:36
  292.2 10.3 %collective-permute-start.68 = (f32[17,192]{1,0:T(8,128)S(1)}, f32[17,192]{1,0:T(8,128)S(1)}, u32[]{:S(2)}, u32[]{:S(2)}) collective-permute-start(f32[17,192]{1,0:T(8,128)S(1)} %add.129), channel_id=1, source_target_pairs={{0,4},{1,5},{2,6},{3,7},{4,0},{5,1},{6,2},{7,3},{8,12},{9,13},{10,... | collective-permute-start | bytes 39176 | tf_op jit(solution)/shard_map/ppermute | solution.py:36
  302.4 14.5 %collective-permute-start.39 = (bf16[160,768]{1,0:T(8,128)(2,1)}, bf16[160,768]{1,0:T(8,128)(2,1)}, u32[]{:S(2)}, u32[]{:S(2)}) collective-permute-start(bf16[160,768]{1,0:T(8,128)(2,1)} %pad_maximum_fusion.7), channel_id=1, source_target_pairs={{0,0},{1,1},{2,8},{3,9},{4,16},{5,17},{6,24},{7,25},{8,2},{9,3},{1... | collective-permute-start | bytes 737288 | tf_op jit(solution)/shard_map/ppermute | solution.py:48
  306.9 16.2 %collective-permute-start.45 = (bf16[2,4,48,768]{3,2,1,0:T(8,128)(2,1)}, bf16[2,4,48,768]{3,2,1,0:T(8,128)(2,1)}, u32[]{:S(2)}, u32[]{:S(2)}) collective-permute-start(bf16[2,4,48,768]{3,2,1,0:T(8,128)(2,1)} %pad_maximum_fusion.1), channel_id=1, source_target_pairs={{0,1},{1,0},{2,3},{3,2},{4,5},{5,4},{6,7},{7,6},{8,9},{9,8},{10,11... | collective-permute-start | bytes 1769480 | tf_op jit(solution)/shard_map/ppermute | solution.py:36
  (57 other events, 286.0 us)
